TPU v7x, 256 devices: a whole 4x4x8 slice. The times are simulated.
256 devices in a mesh: mass: 32 (over x, z), sub: 8 (over y, core).
Axes of the slice: x: 4, y: 4, z: 8, core: 2. Of those that a mesh axis runs over, the one named last changes fastest.
Arguments:
- spectra: bfloat16 [32768, 4096], P(('mass', 'sub')), may hold values from -6 to 6
- w_in: bfloat16 [4096, 2048], P(None, 'sub'), may hold values from -0.09375 to 0.09375
- w_out: bfloat16 [2048, 512], P('sub'), may hold values from -0.125 to 0.125
- partner_rows: int32 [32, 8, 32, 8], P('mass', 'sub'), may hold values from 0 to 127
- pair_counts: int32 [32, 8, 32], P('mass', 'sub'), may hold values from 0 to 8, as said below
- pair_labels: int32 [32, 8, 32, 8], P('mass', 'sub'), may hold values from 0 to 1, as said below
Outputs:
- grad_in: float32 [4096, 2048], P('mass', 'sub')
- grad_out_t: float32 [512, 2048], P('mass', 'sub')
Inputs may be any that keep to these rules, and one draw needn't show every extreme that they name: pair_counts[m, s, q] equals pair_counts[q, s, m], is 0 for q = m, and at most 8; some count equals 8. pair_labels[m, s, q, c] equals pair_labels[q, s, m, c] for q != m.
All inputs are finite; a program needn't handle non-finite values.
Results may differ from a plain program's by a relative error of at most 0.0053.
Values may be sent and summed in bfloat16 or wider, within the bound.
A program may use at most 64 MiB of HBM per device.

v0:
```python
import jax
import jax.numpy as jnp
from jax import lax
from jax.sharding import PartitionSpec as P


def per_device(spectra, w_in, w_out, partner_rows, pair_counts, pair_labels):
    own_rows = spectra.shape[0]
    peers = partner_rows.shape[2]
    slots = partner_rows.shape[3]
    shard_rows = lax.all_gather(spectra, "sub", axis=0, tiled=True)
    pre = jnp.dot(shard_rows, w_in, preferred_element_type=jnp.float32)
    hidden = jax.nn.silu(pre).astype(jnp.bfloat16)
    embed = lax.psum_scatter(
        jnp.dot(hidden, w_out, preferred_element_type=jnp.float32),
        "sub",
        scatter_dimension=0,
        tiled=True,
    )
    norm = jnp.sqrt(jnp.sum(embed * embed, axis=-1, keepdims=True) + 1e-06)
    unit = embed / norm
    unit_b = unit.astype(jnp.bfloat16)
    flat_rows = partner_rows.reshape(peers * slots)
    selector = flat_rows[:, None] == jnp.arange(own_rows, dtype=jnp.int32)[None, :]
    mine = jnp.dot(
        selector.astype(jnp.bfloat16), unit_b, preferred_element_type=jnp.float32
    ).astype(jnp.bfloat16)
    outgoing = mine.reshape(peers, slots, mine.shape[1])
    incoming = lax.all_to_all(outgoing, "mass", split_axis=0, concat_axis=0, tiled=True)
    theirs = incoming.astype(jnp.float32)
    sim = jnp.sum(outgoing.astype(jnp.float32) * theirs, axis=-1)
    valid = jnp.arange(slots, dtype=jnp.int32)[None, :] < pair_counts.reshape(peers)[:, None]
    labels = pair_labels.reshape(peers, slots).astype(jnp.float32)
    coef = jnp.where(valid, 2.0 * (sim - labels), jnp.float32(0.0))
    weighted = (coef[..., None] * theirs).reshape(peers * slots, theirs.shape[2])
    grad_unit = lax.dot_general(
        selector.astype(jnp.float32),
        weighted,
        (((0,), (0,)), ((), ())),
        precision=lax.Precision.HIGHEST,
    )
    along = jnp.sum(unit * grad_unit, axis=-1, keepdims=True)
    grad_embed = ((grad_unit - unit * along) / norm).astype(jnp.bfloat16)
    grad_rows = lax.all_gather(grad_embed, "sub", axis=0, tiled=True)
    back = lax.dot_general(
        grad_rows, w_out, (((1,), (1,)), ((), ())), preferred_element_type=jnp.float32
    )
    gate = jax.nn.sigmoid(pre)
    grad_pre = (back * gate * (1.0 + pre * (1.0 - gate))).astype(jnp.bfloat16)
    out_part = lax.dot_general(
        grad_rows, hidden, (((0,), (0,)), ((), ())), preferred_element_type=jnp.float32
    )
    in_part = lax.dot_general(
        shard_rows, grad_pre, (((0,), (0,)), ((), ())), preferred_element_type=jnp.float32
    )
    grad_in, grad_out_t = (
        lax.psum_scatter(in_part, "mass", scatter_dimension=0, tiled=True),
        lax.psum_scatter(out_part, "mass", scatter_dimension=0, tiled=True),
    )
    return (grad_in, grad_out_t)


def solution(mesh):
    placed = (
        P(("mass", "sub"), None),
        P(None, "sub"),
        P("sub", None),
        P("mass", "sub", None, None),
        P("mass", "sub", None),
        P("mass", "sub", None, None),
    )
    return jax.shard_map(
        per_device,
        mesh=mesh,
        in_specs=placed,
        out_specs=(P("mass", "sub"), P("mass", "sub")),
        check_vma=False,
    )
```

profile of v0, /device:TPU:1, one launch (start us, length us, event | category | flops | bytes accessed | tf_op | source)
XLA Modules:
  0.0 607.8 jit_solution(683276801553638963)
XLA Ops:
  7.2 0.0 all-gather.3.cloned.1.call-start
  7.2 0.7 all-gather.3.cloned.1.call-update
  7.9 0.0 reduce-scatter.4.cloned.1.call-start
  8.0 58.5 %all-gather.3.cloned.1.call-done = bf16[1024,4096]{1,0:T(8,128)(2,1)} async-done(((bf16[128,4096]{1,0:T(8,128)(2,1)}), bf16[1024,4096]{1,0:T(8,128)(2,1)}) %all-gather.3.cloned.1.call-update) | async-done | bytes 8388624 | tf_op jit(solution)/shard_map/all_gather | solution.py:11
  66.4 5.7 fusion.20
  72.2 1.8 fusion.19
  74.0 0.0 reduce-scatter.4.cloned.1.call-update
  74.1 0.1 copy.13
  74.1 0.1 eq.15
  74.2 33.3 %reduce-scatter.4.cloned.1.call-done = f32[128,512]{1,0:T(8,128)} async-done(((f32[1024,512]{1,0:T(8,128)}), f32[128,512]{1,0:T(8,128)}) %reduce-scatter.4.cloned.1.call-update) | async-done | bytes 262160 | tf_op jit(solution)/shard_map/reduce_scatter | solution.py:14
  107.6 1.1 multiply_reduce_fusion.1
  108.6 2.0 fusion.2
  110.6 9.3 %all-to-all-start = ((bf16[32,8,512]{2,1,0:T(8,128)(2,1)}), bf16[32,8,512]{2,1,0:T(8,128)(2,1)S(1)}, u32[]{:S(2)}, u32[]{:S(2)}) async-start(bf16[32,8,512]{2,1,0:T(8,128)(2,1)} %fusion.2), calls=%async_computation.1 | async-start | bytes 524288 | tf_op jit(solution)/shard_map/all_to_all | solution.py:29
  119.9 0.0 all-gather.5.cloned.1.call-start
  120.0 0.1 copy.14
  120.0 9.5 %all-to-all-done = bf16[32,8,512]{2,1,0:T(8,128)(2,1)S(1)} async-done(((bf16[32,8,512]{2,1,0:T(8,128)(2,1)}), bf16[32,8,512]{2,1,0:T(8,128)(2,1)S(1)}, u32[]{:S(2)}, u32[]{:S(2)}) %all-to-all-start) | async-done | bytes 262176 | tf_op jit(solution)/shard_map/all_to_all | solution.py:29
  129.6 1.1 fusion.6
  130.7 0.1 fusion.16
  130.8 1.5 multiply_reduce_fusion
  132.3 1.7 divide_convert_fusion
  134.0 0.0 all-gather.5.cloned.1.call-update
  134.0 0.0 reduce-scatter.6.cloned.1.call-start
  134.1 25.9 %all-gather.5.cloned.1.call-done = bf16[1024,512]{1,0:T(8,128)(2,1)} async-done(((bf16[128,512]{1,0:T(8,128)(2,1)}), bf16[1024,512]{1,0:T(8,128)(2,1)}) %all-gather.5.cloned.1.call-update) | async-done | bytes 1048592 | tf_op jit(solution)/shard_map/all_gather | solution.py:44
  159.9 9.0 %convolution_bitcast_fusion = f32[4096,256]{0,1:T(8,128)} fusion(bf16[1024,4096]{1,0:T(8,128)(2,1)} %all-gather.3.cloned.1.call-done, bf16[1024,512]{1,0:T(8,128)(2,1)} %all-gather.5.cloned.1.call-done, bf16[256,512]{1,0:T(8,128)(2,1)} %param.8, f32[1024,256]{1,0:T(8,128)S(1)} %fusion.20), kind=kOutput, calls=%fused_computation | convolution fusion | flops 2418278400 | bytes 14942208 | tf_op jit(solution)/shard_map/dot_general | solution.py:53
  168.9 0.0 reduce-scatter.6.cloned.1.call-update
  168.9 0.0 reduce-scatter.8.cloned.1.call-start
  169.0 1.1 copy-done.1
  170.1 2.6 fusion.18
  172.7 0.0 reduce-scatter.8.cloned.1.call-update
  172.7 212.9 %reduce-scatter.6.cloned.1.call-done = f32[128,256]{0,1:T(8,128)} async-done(((f32[4096,256]{0,1:T(8,128)}), f32[128,256]{0,1:T(8,128)}) %reduce-scatter.6.cloned.1.call-update) | async-done | bytes 131088 | tf_op jit(solution)/shard_map/reduce_scatter | solution.py:57
  385.7 1.7 copy.15
  387.3 214.0 %reduce-scatter.8.cloned.1.call-done = f32[16,256]{1,0:T(8,128)} async-done(((f32[512,256]{1,0:T(8,128)}), f32[16,256]{1,0:T(8,128)}) %reduce-scatter.8.cloned.1.call-update) | async-done | bytes 16400 | tf_op jit(solution)/shard_map/reduce_scatter | solution.py:58
  (14 shorter events, 0.0 us)
Async XLA Ops:
  7.2 59.3 %copy-start = (bf16[4096,256]{1,0:T(8,128)(2,1)S(1)}, bf16[4096,256]{1,0:T(8,128)(2,1)}, u32[]{:S(2)}) copy-start(bf16[4096,256]{1,0:T(8,128)(2,1)} %param.7) | copy-start | bytes 6291460
  7.2 59.3 %all-gather.3.cloned.1.call-start = ((), (), s32[]{:S(2)}) async-start(), calls=%async_computation.4 | async-start | bytes 9437184 | tf_op jit(solution)/shard_map/all_gather | solution.py:11
  7.9 64.2 %copy-start.3 = (bf16[256,512]{1,0:T(8,128)(2,1)S(1)}, bf16[256,512]{1,0:T(8,128)(2,1)}, u32[]{:S(2)}) copy-start(bf16[256,512]{1,0:T(8,128)(2,1)} %param.8) | copy-start | bytes 786436
  7.9 99.6 %reduce-scatter.4.cloned.1.call-start = ((), (), s32[]{:S(2)}) async-start(), calls=%async_computation.5 | async-start | bytes 2359296 | tf_op jit(solution)/shard_map/reduce_scatter | solution.py:14
  72.2 87.8 %copy-start.2 = (f32[1024,256]{1,0:T(8,128)}, f32[1024,256]{1,0:T(8,128)S(1)}, u32[]{:S(2)}) copy-start(f32[1024,256]{1,0:T(8,128)S(1)} %fusion.20) | copy-start | bytes 3145732
  72.2 1.9 copy-start.4
  72.2 47.8 %copy-start.5 = (s32[1,1,32,8]{2,3,1,0:T(8,128)S(1)}, s32[1,1,32,8]{2,3,1,0:T(8,128)}, u32[]{:S(2)}) copy-start(s32[1,1,32,8]{2,3,1,0:T(8,128)} %param.11) | copy-start | bytes 3076
  72.2 58.5 %copy-start.6 = (s32[1,1,32]{2,1,0:T(1,128)S(1)}, s32[1,1,32]{2,1,0:T(1,128)}, u32[]{:S(2)}) copy-start(s32[1,1,32]{2,1,0:T(1,128)} %param.10) | copy-start | bytes 388
  110.6 19.0 %all-to-all-start = ((bf16[32,8,512]{2,1,0:T(8,128)(2,1)}), bf16[32,8,512]{2,1,0:T(8,128)(2,1)S(1)}, u32[]{:S(2)}, u32[]{:S(2)}) async-start(bf16[32,8,512]{2,1,0:T(8,128)(2,1)} %fusion.2), calls=%async_computation.1 | async-start | bytes 524288 | tf_op jit(solution)/shard_map/all_to_all | solution.py:29
  119.9 40.0 %all-gather.5.cloned.1.call-start = ((), (), s32[]{:S(2)}) async-start(), calls=%async_computation.6 | async-start | bytes 1179648 | tf_op jit(solution)/shard_map/all_gather | solution.py:44
  134.0 251.7 %reduce-scatter.6.cloned.1.call-start = ((), (), s32[]{:S(2)}) async-start(), calls=%async_computation.7 | async-start | bytes 4325376 | tf_op jit(solution)/shard_map/reduce_scatter | solution.py:57
  168.9 1.2 copy-start.1
  168.9 432.4 %reduce-scatter.8.cloned.1.call-start = ((), (), s32[]{:S(2)}) async-start(), calls=%async_computation.8 | async-start | bytes 540672 | tf_op jit(solution)/shard_map/reduce_scatter | solution.py:58
Sparse Core Ops, SparseCore 0:
  9.9 56.5 all-gather.2
  74.2 33.3 reduce-scatter.3
  134.1 25.7 all-gather.4
  169.1 216.5 reduce-scatter.5
  390.4 210.8 reduce-scatter.7
where the time goes:
time: 613 us; the launch traced here: 608 us
  waiting for transfers between devices  555 us (91%)
  matrix products  22.5 us (4%)
  between operations  13.9 us (2%)
  starting transfers between devices  9.51 us (2%)
    reduce_scatter x1, waiting for transfers between devices, per_device(): lax.psum_scatter(out_part, 'mass', scatter_dimension=0, tiled=True)  214 us
    reduce_scatter x1, waiting for transfers between devices, per_device(): lax.psum_scatter(in_part, 'mass', scatter_dimension=0, tiled=True)  213 us
    all_gather x1, waiting for transfers between devices, per_device(): shard_rows = lax.all_gather(spectra, 'sub', axis=0, tiled=True)  58.5 us
    reduce_scatter x1, waiting for transfers between devices, per_device(): lax.psum_scatter(jnp.dot(hidden, w_out, preferred_element_type=jnp.float3...  33.3 us
    all_gather x1, waiting for transfers between devices, per_device(): grad_rows = lax.all_gather(grad_embed, 'sub', axis=0, tiled=True)  25.9 us
  transfers between devices with their start and end apart: 6, of which 6 were waited for; matrix products, arithmetic and copies ran while one was open for 1% of the time, Pallas kernels for 0%

commit v1 on v0

--- a/solution.py
+++ b/solution.py
@@ -53,10 +53,23 @@
     in_part = lax.dot_general(
         shard_rows, grad_pre, (((0,), (0,)), ((), ())), preferred_element_type=jnp.float32
     )
-    grad_in, grad_out_t = (
-        lax.psum_scatter(in_part, "mass", scatter_dimension=0, tiled=True),
-        lax.psum_scatter(out_part, "mass", scatter_dimension=0, tiled=True),
+    n_mass = peers
+    in_rows = in_part.shape[0] // n_mass
+    out_rows = out_part.shape[0] // n_mass
+    partial = jnp.concatenate(
+        [
+            in_part.reshape(n_mass, in_rows, in_part.shape[1]),
+            out_part.reshape(n_mass, out_rows, out_part.shape[1]),
+        ],
+        axis=1,
+    ).astype(jnp.bfloat16)
+    summed = jnp.sum(
+        lax.all_to_all(partial, "mass", split_axis=0, concat_axis=0, tiled=True).astype(
+            jnp.float32
+        ),
+        axis=0,
     )
+    grad_in, grad_out_t = summed[:in_rows], summed[in_rows:]
     return (grad_in, grad_out_t)
 
 

time: 613 us -> 249 us (0.41)
  waiting for transfers between devices: 555 us -> 128 us
  blocking collectives: 0 us -> 64.8 us
    reduce_scatter x2 -> x0, waiting for transfers between devices: 427 us -> none  [the longest x1 214 us: per_device(): lax.psum_scatter(out_part, 'mass', scatter_dimension=0, tiled=True)]
    all_to_all x0 -> x1, blocking collectives: none -> 64.8 us  [per_device(): lax.all_to_all(partial, 'mass', split_axis=0, concat_axis=0, tiled=True)]
  transfers between devices with their start and end apart: 6 -> 4, of which waited for: 6 -> 4; matrix products, arithmetic and copies ran while one was open for 1% -> 0% of each run, Pallas kernels for 0% -> 0%
where the time goes in v1:
time: 249 us; the launch traced here: 248 us
  waiting for transfers between devices  128 us (51%)
  blocking collectives  64.8 us (26%)
  matrix products  21.5 us (9%)
  between operations  13.9 us (6%)
  starting transfers between devices  9.43 us (4%)
  local copies, waits for them, and re-layouts  6.69 us (3%)
  other arithmetic  3.58 us (1%)
    all_to_all x1, blocking collectives, per_device(): lax.all_to_all(partial, 'mass', split_axis=0, concat_axis=0, tiled=True)  64.8 us
    all_gather x1, waiting for transfers between devices, per_device(): shard_rows = lax.all_gather(spectra, 'sub', axis=0, tiled=True)  58.5 us
    reduce_scatter x1, waiting for transfers between devices, per_device(): lax.psum_scatter(jnp.dot(hidden, w_out, preferred_element_type=jnp.float3...  33.3 us
    all_gather x1, waiting for transfers between devices, per_device(): grad_rows = lax.all_gather(grad_embed, 'sub', axis=0, tiled=True)  25.9 us
    all_to_all x1, waiting for transfers between devices, per_device(): lax.all_to_all(outgoing, 'mass', split_axis=0, concat_axis=0, tiled=True)  9.55 us
    all_to_all x1, starting transfers between devices, per_device(): lax.all_to_all(outgoing, 'mass', split_axis=0, concat_axis=0, tiled=True)  9.31 us
    dot_general x1, matrix products, per_device(): lax.dot_general(shard_rows, grad_pre, (((0,), (0,)), ((), ())), preferred...  8.59 us
    dot_general x1, matrix products, per_device(): pre = jnp.dot(shard_rows, w_in, preferred_element_type=jnp.float32)  5.71 us
  transfers between devices with their start and end apart: 4, of which 4 were waited for; matrix products, arithmetic and copies ran while one was open for 0% of the time, Pallas kernels for 0%

profile of v1, /device:TPU:1, one launch (start us, length us, event | category | flops | bytes accessed | tf_op | source)
XLA Modules:
  0.0 247.9 jit_solution(8469015729756273993)
XLA Ops:
  7.2 0.0 copy-start
  7.2 0.0 all-gather.3.cloned.1.call-start
  7.2 0.7 all-gather.3.cloned.1.call-update
  7.9 0.0 reduce-scatter.2.cloned.1.call-start
  8.0 58.5 %all-gather.3.cloned.1.call-done = bf16[1024,4096]{1,0:T(8,128)(2,1)} async-done(((bf16[128,4096]{1,0:T(8,128)(2,1)}), bf16[1024,4096]{1,0:T(8,128)(2,1)}) %all-gather.3.cloned.1.call-update) | async-done | bytes 8388624 | tf_op jit(solution)/shard_map/all_gather | solution.py:11
  66.4 5.7 %fusion.20 = f32[1024,256]{1,0:T(8,128)S(1)} fusion(bf16[1024,4096]{1,0:T(8,128)(2,1)} %all-gather.3.cloned.1.call-done, bf16[4096,256]{1,0:T(8,128)(2,1)S(1)} %copy-done), kind=kOutput, calls=%fused_computation.37 | convolution fusion | flops 2147483648 | bytes 11534336 | tf_op jit(solution)/shard_map/dot_general | solution.py:12
  72.2 1.0 copy-done.8
  73.1 1.8 fusion.19
  75.0 0.0 reduce-scatter.2.cloned.1.call-update
  75.0 0.1 copy.13
  75.1 0.1 eq.15
  75.2 33.3 %reduce-scatter.2.cloned.1.call-done = f32[128,512]{1,0:T(8,128)} async-done(((f32[1024,512]{1,0:T(8,128)}), f32[128,512]{1,0:T(8,128)}) %reduce-scatter.2.cloned.1.call-update) | async-done | bytes 262160 | tf_op jit(solution)/shard_map/reduce_scatter | solution.py:14
  108.5 1.1 multiply_reduce_fusion.1
  109.6 2.0 fusion.3
  111.6 9.3 %all-to-all-start = ((bf16[32,8,512]{2,1,0:T(8,128)(2,1)}), bf16[32,8,512]{2,1,0:T(8,128)(2,1)S(1)}, u32[]{:S(2)}, u32[]{:S(2)}) async-start(bf16[32,8,512]{2,1,0:T(8,128)(2,1)} %fusion.3), calls=%async_computation.1 | async-start | bytes 524288 | tf_op jit(solution)/shard_map/all_to_all | solution.py:29
  120.9 0.0 all-gather.5.cloned.1.call-start
  121.0 0.1 copy.14
  121.1 9.5 %all-to-all-done = bf16[32,8,512]{2,1,0:T(8,128)(2,1)S(1)} async-done(((bf16[32,8,512]{2,1,0:T(8,128)(2,1)}), bf16[32,8,512]{2,1,0:T(8,128)(2,1)S(1)}, u32[]{:S(2)}, u32[]{:S(2)}) %all-to-all-start) | async-done | bytes 262176 | tf_op jit(solution)/shard_map/all_to_all | solution.py:29
  130.6 1.1 fusion.7
  131.7 0.1 fusion.17
  131.8 1.5 multiply_reduce_fusion
  133.3 0.8 divide_convert_fusion
  134.1 0.0 all-gather.5.cloned.1.call-update
  134.1 25.9 %all-gather.5.cloned.1.call-done = bf16[1024,512]{1,0:T(8,128)(2,1)} async-done(((bf16[128,512]{1,0:T(8,128)(2,1)}), bf16[1024,512]{1,0:T(8,128)(2,1)}) %all-gather.5.cloned.1.call-update) | async-done | bytes 1048592 | tf_op jit(solution)/shard_map/all_gather | solution.py:44
  160.0 8.6 %fusion = bf16[4096,256]{0,1:T(8,128)(2,1)} fusion(bf16[1024,4096]{1,0:T(8,128)(2,1)} %all-gather.3.cloned.1.call-done, bf16[1024,512]{1,0:T(8,128)(2,1)} %all-gather.5.cloned.1.call-done, bf16[256,512]{1,0:T(8,128)(2,1)S(1)} %copy-done.7, f32[1024,256]{1,0:T(8,128)} %copy-done.8), kind=kOutput, calls=%fused_computation.1 | convolution fusion | flops 2419326976 | bytes 12845056 | tf_op jit(solution)/shard_map/dot_general | solution.py:53
  168.6 4.2 %copy.19 = bf16[4096,256]{1,0:T(8,128)(2,1)} copy(bf16[4096,256]{0,1:T(8,128)(2,1)} %fusion) | data formatting | bytes 4194304 | tf_op jit(solution)/shard_map/reshape | solution.py:61
  172.8 1.9 convolution_convert_fusion.1
  174.8 0.2 pad_maximum_fusion
  174.9 64.8 %all_to_all.10 = bf16[32,144,256]{2,1,0:T(8,128)(2,1)S(1)} all-to-all(bf16[32,144,256]{2,1,0:T(8,128)(2,1)S(1)} %pad_maximum_fusion), channel_id=1, replica_groups=mesh['mass'=32,'sub'=8] {'mass'}, dimensions={0} | all-to-all | bytes 4718592 | tf_op jit(solution)/shard_map/all_to_all | solution.py:67
  239.7 0.3 convert_reduce_fusion
  240.1 0.6 slice.9
  240.7 0.7 slice.8
  (17 shorter events, 0.0 us)
Async XLA Ops:
  7.2 59.3 %copy-start = (bf16[4096,256]{1,0:T(8,128)(2,1)S(1)}, bf16[4096,256]{1,0:T(8,128)(2,1)}, u32[]{:S(2)}) copy-start(bf16[4096,256]{1,0:T(8,128)(2,1)} %param.7) | copy-start | bytes 6291460
  7.2 59.3 %all-gather.3.cloned.1.call-start = ((), (), s32[]{:S(2)}) async-start(), calls=%async_computation.3 | async-start | bytes 9437184 | tf_op jit(solution)/shard_map/all_gather | solution.py:11
  7.9 65.2 %copy-start.7 = (bf16[256,512]{1,0:T(8,128)(2,1)S(1)}, bf16[256,512]{1,0:T(8,128)(2,1)}, u32[]{:S(2)}) copy-start(bf16[256,512]{1,0:T(8,128)(2,1)} %param.8) | copy-start | bytes 786436
  7.9 100.6 %reduce-scatter.2.cloned.1.call-start = ((), (), s32[]{:S(2)}) async-start(), calls=%async_computation.4 | async-start | bytes 2359296 | tf_op jit(solution)/shard_map/reduce_scatter | solution.py:14
  72.1 1.0 copy-start.8
  73.1 1.9 copy-start.3
  74.9 46.0 %copy-start.4 = (s32[1,1,32,8]{2,3,1,0:T(8,128)S(1)}, s32[1,1,32,8]{2,3,1,0:T(8,128)}, u32[]{:S(2)}) copy-start(s32[1,1,32,8]{2,3,1,0:T(8,128)} %param.11) | copy-start | bytes 3076
  75.0 56.8 %copy-start.5 = (s32[1,1,32]{2,1,0:T(1,128)S(1)}, s32[1,1,32]{2,1,0:T(1,128)}, u32[]{:S(2)}) copy-start(s32[1,1,32]{2,1,0:T(1,128)} %param.10) | copy-start | bytes 388
  108.5 24.8 %copy-start.2 = (f32[128,512]{1,0:T(8,128)S(1)}, f32[128,512]{1,0:T(8,128)}, u32[]{:S(2)}) copy-start(f32[128,512]{1,0:T(8,128)} %reduce-scatter.2.cloned.1.call-done) | copy-start | bytes 786436
  111.6 19.0 %all-to-all-start = ((bf16[32,8,512]{2,1,0:T(8,128)(2,1)}), bf16[32,8,512]{2,1,0:T(8,128)(2,1)S(1)}, u32[]{:S(2)}, u32[]{:S(2)}) async-start(bf16[32,8,512]{2,1,0:T(8,128)(2,1)} %fusion.3), calls=%async_computation.1 | async-start | bytes 524288 | tf_op jit(solution)/shard_map/all_to_all | solution.py:29
  120.9 39.1 %all-gather.5.cloned.1.call-start = ((), (), s32[]{:S(2)}) async-start(), calls=%async_computation.5 | async-start | bytes 1179648 | tf_op jit(solution)/shard_map/all_gather | solution.py:44
  168.6 4.2 %copy-start.6 = (bf16[1024,512]{1,0:T(8,128)(2,1)S(1)}, bf16[1024,512]{1,0:T(8,128)(2,1)}, u32[]{:S(2)}) copy-start(bf16[1024,512]{1,0:T(8,128)(2,1)} %all-gather.5.cloned.1.call-done) | copy-start | bytes 3145732
  172.8 2.0 copy-start.1
Sparse Core Ops, SparseCore 0:
  9.9 56.5 all-gather.2
  75.1 33.3 reduce-scatter.1
  134.2 25.7 all-gather.4

commit v2 on v1

--- a/solution.py
+++ b/solution.py
@@ -1,7 +1,65 @@
+import functools
+
 import jax
 import jax.numpy as jnp
 from jax import lax
+from jax.experimental import pallas as pl
+from jax.experimental.pallas import tpu as pltpu
 from jax.sharding import PartitionSpec as P
+
+MESH = pl.DeviceIdType.MESH
+
+
+def _exchange_kernel(n, x_ref, o_ref, got, send_sems, recv_sems):
+    me = lax.axis_index("mass")
+    barrier = pltpu.get_barrier_semaphore()
+    for k in range(1, n):
+        pl.semaphore_signal(
+            barrier, inc=1, device_id={"mass": lax.rem(me + k, n)}, device_id_type=MESH
+        )
+    pl.semaphore_wait(barrier, n - 1)
+    sends = []
+    for k in range(1, n):
+        peer = lax.rem(me + k, n)
+        copy = pltpu.make_async_remote_copy(
+            src_ref=x_ref.at[peer],
+            dst_ref=got.at[me],
+            send_sem=send_sems.at[k],
+            recv_sem=recv_sems.at[k],
+            device_id={"mass": peer},
+            device_id_type=MESH,
+        )
+        copy.start()
+        sends.append(copy)
+    o_ref[me] = x_ref[me]
+    for k in range(1, n):
+        sends[k - 1].wait_send()
+        source = lax.rem(me + n - k, n)
+        pltpu.make_async_remote_copy(
+            src_ref=x_ref.at[source],
+            dst_ref=got.at[source],
+            send_sem=send_sems.at[k],
+            recv_sem=recv_sems.at[k],
+            device_id={"mass": source},
+            device_id_type=MESH,
+        ).wait_recv()
+        o_ref[source] = got[source]
+
+
+def mass_exchange(x, collective_id):
+    n = x.shape[0]
+    return pl.pallas_call(
+        functools.partial(_exchange_kernel, n),
+        out_shape=jax.ShapeDtypeStruct(x.shape, x.dtype),
+        in_specs=[pl.BlockSpec(memory_space=pltpu.VMEM)],
+        out_specs=pl.BlockSpec(memory_space=pltpu.VMEM),
+        scratch_shapes=[
+            pltpu.VMEM(x.shape, x.dtype),
+            pltpu.SemaphoreType.DMA((n,)),
+            pltpu.SemaphoreType.DMA((n,)),
+        ],
+        compiler_params=pltpu.CompilerParams(collective_id=collective_id, has_side_effects=True),
+    )(x)
 
 
 def per_device(spectra, w_in, w_out, partner_rows, pair_counts, pair_labels):
@@ -26,7 +84,7 @@
         selector.astype(jnp.bfloat16), unit_b, preferred_element_type=jnp.float32
     ).astype(jnp.bfloat16)
     outgoing = mine.reshape(peers, slots, mine.shape[1])
-    incoming = lax.all_to_all(outgoing, "mass", split_axis=0, concat_axis=0, tiled=True)
+    incoming = mass_exchange(outgoing, 0)
     theirs = incoming.astype(jnp.float32)
     sim = jnp.sum(outgoing.astype(jnp.float32) * theirs, axis=-1)
     valid = jnp.arange(slots, dtype=jnp.int32)[None, :] < pair_counts.reshape(peers)[:, None]
@@ -64,7 +122,7 @@
         axis=1,
     ).astype(jnp.bfloat16)
     summed = jnp.sum(
-        lax.all_to_all(partial, "mass", split_axis=0, concat_axis=0, tiled=True).astype(
+        mass_exchange(partial, 1).astype(
             jnp.float32
         ),
         axis=0,

time: 249 us -> 251 us (level)
  Pallas kernels: 0 us -> 79.6 us
  blocking collectives: 64.8 us -> 0 us
  starting transfers between devices: 9.43 us -> 0.12 us
  waiting for transfers between devices: 128 us -> 122 us
  other arithmetic: 3.58 us -> 6.76 us
    pallas_call x0 -> x2, Pallas kernels: none -> 79.6 us  [mass_exchange(): pl.pallas_call(functools.partial(_exchange_kernel, n), out_shape=jax.Shap...]
    all_to_all x1 -> x0, blocking collectives: 64.8 us -> none  [per_device(): lax.all_to_all(partial, 'mass', split_axis=0, concat_axis=0, tiled=True)]
    all_to_all x1 -> x0, waiting for transfers between devices: 9.55 us -> none  [per_device(): lax.all_to_all(outgoing, 'mass', split_axis=0, concat_axis=0, tiled=True)]
    all_to_all x1 -> x0, starting transfers between devices: 9.31 us -> none  [per_device(): lax.all_to_all(outgoing, 'mass', split_axis=0, concat_axis=0, tiled=True)]
    reshape x1 -> x0, local copies, waits for them, and re-layouts: 4.17 us -> none  [per_device(): in_part.reshape(n_mass, in_rows, in_part.shape[1])]
    dot_general x0 -> x1, local copies, waits for them, and re-layouts: none -> 4.14 us  [per_device(): lax.dot_general(shard_rows, grad_pre, (((0,), (0,)), ((), ())), preferred...]
    all_gather x1, waiting for transfers between devices: 25.9 us -> 29.2 us  [per_device(): grad_rows = lax.all_gather(grad_embed, 'sub', axis=0, tiled=True)]
  transfers between devices with their start and end apart: 4 -> 3, of which waited for: 4 -> 3; matrix products, arithmetic and copies ran while one was open for 0% -> 0% of each run, Pallas kernels for 0% -> 0%
where the time goes in v2:
time: 251 us; the launch traced here: 250 us
  waiting for transfers between devices  122 us (49%)
  Pallas kernels  79.6 us (32%)
  matrix products  21.6 us (9%)
  between operations  13.9 us (6%)
  other arithmetic  6.76 us (3%)
  local copies, waits for them, and re-layouts  6.66 us (3%)
    pallas_call x2, Pallas kernels, mass_exchange(): pl.pallas_call(functools.partial(_exchange_kernel, n), out_shape=jax.Shap...  79.6 us
    all_gather x1, waiting for transfers between devices, per_device(): shard_rows = lax.all_gather(spectra, 'sub', axis=0, tiled=True)  58.5 us
    reduce_scatter x1, waiting for transfers between devices, per_device(): lax.psum_scatter(jnp.dot(hidden, w_out, preferred_element_type=jnp.float3...  33.2 us
    all_gather x1, waiting for transfers between devices, per_device(): grad_rows = lax.all_gather(grad_embed, 'sub', axis=0, tiled=True)  29.2 us
    dot_general x1, matrix products, per_device(): lax.dot_general(shard_rows, grad_pre, (((0,), (0,)), ((), ())), preferred...  8.58 us
    dot_general x1, matrix products, per_device(): pre = jnp.dot(shard_rows, w_in, preferred_element_type=jnp.float32)  5.71 us
  transfers between devices with their start and end apart: 3, of which 3 were waited for; matrix products, arithmetic and copies ran while one was open for 0% of the time, Pallas kernels for 0%

profile of v2, /device:TPU:1, one launch (start us, length us, event | category | flops | bytes accessed | tf_op | source)
XLA Modules:
  0.0 250.2 jit_solution(4674469365164945367)
XLA Ops:
  7.2 0.0 copy-start
  7.2 0.0 all-gather.3.cloned.1.call-start
  7.2 0.7 all-gather.3.cloned.1.call-update
  7.9 0.0 copy-start.7
  7.9 0.0 reduce-scatter.2.cloned.1.call-start
  8.0 58.5 %all-gather.3.cloned.1.call-done = bf16[1024,4096]{1,0:T(8,128)(2,1)} async-done(((bf16[128,4096]{1,0:T(8,128)(2,1)}), bf16[1024,4096]{1,0:T(8,128)(2,1)}) %all-gather.3.cloned.1.call-update) | async-done | bytes 8388624 | tf_op jit(solution)/shard_map/all_gather | solution.py:69
  66.4 5.7 %fusion.20 = f32[1024,256]{1,0:T(8,128)S(1)} fusion(bf16[1024,4096]{1,0:T(8,128)(2,1)} %all-gather.3.cloned.1.call-done, bf16[4096,256]{1,0:T(8,128)(2,1)S(1)} %copy-done), kind=kOutput, calls=%fused_computation.37 | convolution fusion | flops 2147483648 | bytes 11534336 | tf_op jit(solution)/shard_map/dot_general | solution.py:70
  72.2 1.0 copy-done.8
  73.1 1.8 fusion.19
  75.0 0.0 reduce-scatter.2.cloned.1.call-update
  75.0 0.0 all-gather.5.cloned.1.call-start
  75.0 0.1 copy.13
  75.1 0.1 eq.15
  75.2 0.1 copy.14
  75.3 33.2 %reduce-scatter.2.cloned.1.call-done = f32[128,512]{1,0:T(8,128)} async-done(((f32[1024,512]{1,0:T(8,128)}), f32[128,512]{1,0:T(8,128)}) %reduce-scatter.2.cloned.1.call-update) | async-done | bytes 262160 | tf_op jit(solution)/shard_map/reduce_scatter | solution.py:72
  108.5 1.1 multiply_reduce_fusion.1
  109.6 2.0 fusion.3.x_ref
  111.6 14.3 %shard_map.77 = bf16[32,8,512]{2,1,0:T(8,128)(2,1)} custom-call(bf16[32,8,512]{2,1,0:T(8,128)(2,1)} %fusion.3.x_ref), custom_call_target="tpu_custom_call" | custom-call | tf_op jit(solution)/shard_map/pallas_call | solution.py:51
  125.9 1.2 fusion.7
  127.1 0.1 fusion.17
  127.2 1.6 multiply_reduce_fusion
  128.8 0.8 divide_convert_fusion
  129.5 0.0 all-gather.5.cloned.1.call-update
  129.6 29.2 %all-gather.5.cloned.1.call-done = bf16[1024,512]{1,0:T(8,128)(2,1)} async-done(((bf16[128,512]{1,0:T(8,128)(2,1)}), bf16[1024,512]{1,0:T(8,128)(2,1)}) %all-gather.5.cloned.1.call-update) | async-done | bytes 1048592 | tf_op jit(solution)/shard_map/all_gather | solution.py:102
  158.8 8.6 %fusion = bf16[4096,256]{0,1:T(8,128)(2,1)} fusion(bf16[1024,4096]{1,0:T(8,128)(2,1)} %all-gather.3.cloned.1.call-done, bf16[1024,512]{1,0:T(8,128)(2,1)} %all-gather.5.cloned.1.call-done, bf16[256,512]{1,0:T(8,128)(2,1)S(1)} %copy-done.7, f32[1024,256]{1,0:T(8,128)} %copy-done.8), kind=kOutput, calls=%fused_computation.1 | convolution fusion | flops 2419326976 | bytes 12845056 | tf_op jit(solution)/shard_map/dot_general | solution.py:111
  167.4 4.1 %copy.15 = bf16[4096,256]{1,0:T(8,128)(2,1)} copy(bf16[4096,256]{0,1:T(8,128)(2,1)} %fusion) | data formatting | bytes 4194304 | tf_op jit(solution)/shard_map/dot_general | solution.py:111
  171.5 1.9 convolution_convert_fusion.1
  173.5 1.6 pad_maximum_fusion.x_ref
  175.1 65.3 %shard_map.78 = bf16[32,144,256]{2,1,0:T(8,128)(2,1)} custom-call(bf16[32,144,256]{2,1,0:T(8,128)(2,1)} %pad_maximum_fusion.x_ref), custom_call_target="tpu_custom_call" | custom-call | tf_op jit(solution)/shard_map/pallas_call | solution.py:51
  240.3 2.0 convert_reduce_fusion
  242.4 0.6 slice.9
  243.0 0.7 slice.8
  (16 shorter events, 0.0 us)
Async XLA Ops:
  7.2 59.3 %copy-start = (bf16[4096,256]{1,0:T(8,128)(2,1)S(1)}, bf16[4096,256]{1,0:T(8,128)(2,1)}, u32[]{:S(2)}) copy-start(bf16[4096,256]{1,0:T(8,128)(2,1)} %param.7) | copy-start | bytes 6291460
  7.2 59.3 %all-gather.3.cloned.1.call-start = ((), (), s32[]{:S(2)}) async-start(), calls=%async_computation.1 | async-start | bytes 9437184 | tf_op jit(solution)/shard_map/all_gather | solution.py:69
  7.9 65.2 %copy-start.7 = (bf16[256,512]{1,0:T(8,128)(2,1)S(1)}, bf16[256,512]{1,0:T(8,128)(2,1)}, u32[]{:S(2)}) copy-start(bf16[256,512]{1,0:T(8,128)(2,1)} %param.8) | copy-start | bytes 786436
  7.9 100.6 %reduce-scatter.2.cloned.1.call-start = ((), (), s32[]{:S(2)}) async-start(), calls=%async_computation.2 | async-start | bytes 2359296 | tf_op jit(solution)/shard_map/reduce_scatter | solution.py:72
  72.1 1.0 copy-start.8
  73.1 1.9 copy-start.3
  73.1 2.1 copy-start.4
  74.9 52.2 %copy-start.5 = (s32[1,1,32]{2,1,0:T(1,128)S(1)}, s32[1,1,32]{2,1,0:T(1,128)}, u32[]{:S(2)}) copy-start(s32[1,1,32]{2,1,0:T(1,128)} %param.10) | copy-start | bytes 388
  75.0 83.8 %all-gather.5.cloned.1.call-start = ((), (), s32[]{:S(2)}) async-start(), calls=%async_computation.3 | async-start | bytes 1179648 | tf_op jit(solution)/shard_map/all_gather | solution.py:102
  108.5 20.3 %copy-start.2 = (f32[128,512]{1,0:T(8,128)S(1)}, f32[128,512]{1,0:T(8,128)}, u32[]{:S(2)}) copy-start(f32[128,512]{1,0:T(8,128)} %reduce-scatter.2.cloned.1.call-done) | copy-start | bytes 786436
  167.4 4.1 %copy-start.6 = (bf16[1024,512]{1,0:T(8,128)(2,1)S(1)}, bf16[1024,512]{1,0:T(8,128)(2,1)}, u32[]{:S(2)}) copy-start(bf16[1024,512]{1,0:T(8,128)(2,1)} %all-gather.5.cloned.1.call-done) | copy-start | bytes 3145732
  171.5 2.0 copy-start.1
Sparse Core Ops, SparseCore 0:
  9.9 56.5 all-gather.2
  75.1 33.3 reduce-scatter.1
  129.7 29.0 all-gather.4

commit v3 on v2

--- a/solution.py
+++ b/solution.py
@@ -10,51 +10,51 @@
 MESH = pl.DeviceIdType.MESH
 
 
-def _exchange_kernel(n, x_ref, o_ref, got, send_sems, recv_sems):
-    me = lax.axis_index("mass")
+def _exchange_kernel(n, axis, gather, x_ref, o_ref, got, send_sems, recv_sems):
+    me = lax.axis_index(axis)
     barrier = pltpu.get_barrier_semaphore()
     for k in range(1, n):
         pl.semaphore_signal(
-            barrier, inc=1, device_id={"mass": lax.rem(me + k, n)}, device_id_type=MESH
+            barrier, inc=1, device_id={axis: lax.rem(me + k, n)}, device_id_type=MESH
         )
     pl.semaphore_wait(barrier, n - 1)
     sends = []
     for k in range(1, n):
         peer = lax.rem(me + k, n)
         copy = pltpu.make_async_remote_copy(
-            src_ref=x_ref.at[peer],
+            src_ref=x_ref if gather else x_ref.at[peer],
             dst_ref=got.at[me],
             send_sem=send_sems.at[k],
             recv_sem=recv_sems.at[k],
-            device_id={"mass": peer},
+            device_id={axis: peer},
             device_id_type=MESH,
         )
         copy.start()
         sends.append(copy)
-    o_ref[me] = x_ref[me]
+    o_ref[me] = x_ref[...] if gather else x_ref[me]
     for k in range(1, n):
         sends[k - 1].wait_send()
         source = lax.rem(me + n - k, n)
         pltpu.make_async_remote_copy(
-            src_ref=x_ref.at[source],
+            src_ref=x_ref if gather else x_ref.at[source],
             dst_ref=got.at[source],
             send_sem=send_sems.at[k],
             recv_sem=recv_sems.at[k],
-            device_id={"mass": source},
+            device_id={axis: source},
             device_id_type=MESH,
         ).wait_recv()
         o_ref[source] = got[source]
 
 
-def mass_exchange(x, collective_id):
-    n = x.shape[0]
+def exchange(x, axis, n, collective_id, gather=False):
+    shape = (n,) + x.shape if gather else x.shape
     return pl.pallas_call(
-        functools.partial(_exchange_kernel, n),
-        out_shape=jax.ShapeDtypeStruct(x.shape, x.dtype),
+        functools.partial(_exchange_kernel, n, axis, gather),
+        out_shape=jax.ShapeDtypeStruct(shape, x.dtype),
         in_specs=[pl.BlockSpec(memory_space=pltpu.VMEM)],
         out_specs=pl.BlockSpec(memory_space=pltpu.VMEM),
         scratch_shapes=[
-            pltpu.VMEM(x.shape, x.dtype),
+            pltpu.VMEM(shape, x.dtype),
             pltpu.SemaphoreType.DMA((n,)),
             pltpu.SemaphoreType.DMA((n,)),
         ],
@@ -69,11 +69,11 @@
     shard_rows = lax.all_gather(spectra, "sub", axis=0, tiled=True)
     pre = jnp.dot(shard_rows, w_in, preferred_element_type=jnp.float32)
     hidden = jax.nn.silu(pre).astype(jnp.bfloat16)
-    embed = lax.psum_scatter(
-        jnp.dot(hidden, w_out, preferred_element_type=jnp.float32),
-        "sub",
-        scatter_dimension=0,
-        tiled=True,
+    n_sub = shard_rows.shape[0] // own_rows
+    embed_part = jnp.dot(hidden, w_out, preferred_element_type=jnp.float32)
+    embed = jnp.sum(
+        exchange(embed_part.reshape(n_sub, own_rows, embed_part.shape[1]), "sub", n_sub, 2),
+        axis=0,
     )
     norm = jnp.sqrt(jnp.sum(embed * embed, axis=-1, keepdims=True) + 1e-06)
     unit = embed / norm
@@ -84,7 +84,7 @@
         selector.astype(jnp.bfloat16), unit_b, preferred_element_type=jnp.float32
     ).astype(jnp.bfloat16)
     outgoing = mine.reshape(peers, slots, mine.shape[1])
-    incoming = mass_exchange(outgoing, 0)
+    incoming = exchange(outgoing, "mass", peers, 0)
     theirs = incoming.astype(jnp.float32)
     sim = jnp.sum(outgoing.astype(jnp.float32) * theirs, axis=-1)
     valid = jnp.arange(slots, dtype=jnp.int32)[None, :] < pair_counts.reshape(peers)[:, None]
@@ -99,7 +99,9 @@
     )
     along = jnp.sum(unit * grad_unit, axis=-1, keepdims=True)
     grad_embed = ((grad_unit - unit * along) / norm).astype(jnp.bfloat16)
-    grad_rows = lax.all_gather(grad_embed, "sub", axis=0, tiled=True)
+    grad_rows = exchange(grad_embed, "sub", n_sub, 3, gather=True).reshape(
+        n_sub * own_rows, grad_embed.shape[1]
+    )
     back = lax.dot_general(
         grad_rows, w_out, (((1,), (1,)), ((), ())), preferred_element_type=jnp.float32
     )
@@ -122,7 +124,7 @@
         axis=1,
     ).astype(jnp.bfloat16)
     summed = jnp.sum(
-        mass_exchange(partial, 1).astype(
+        exchange(partial, "mass", peers, 1).astype(
             jnp.float32
         ),
         axis=0,

time: 251 us -> 235 us (0.936)
  waiting for transfers between devices: 122 us -> 57.6 us
  Pallas kernels: 79.6 us -> 124 us
    pallas_call x2 -> x4, Pallas kernels: 79.6 us -> 124 us  [exchange(): pl.pallas_call(functools.partial(_exchange_kernel, n, axis, gather), out_...]
    reduce_scatter x1 -> x0, waiting for transfers between devices: 33.2 us -> none  [per_device(): lax.psum_scatter(jnp.dot(hidden, w_out, preferred_element_type=jnp.float3...]
    all_gather x1 -> x0, waiting for transfers between devices: 29.2 us -> none  [per_device(): grad_rows = lax.all_gather(grad_embed, 'sub', axis=0, tiled=True)]
  transfers between devices with their start and end apart: 3 -> 1, of which waited for: 3 -> 1; matrix products, arithmetic and copies ran while one was open for 0% -> 1% of each run, Pallas kernels for 0% -> 0%
where the time goes in v3:
time: 235 us; the launch traced here: 233 us
  Pallas kernels  124 us (53%)
  waiting for transfers between devices  57.6 us (25%)
  matrix products  20.9 us (9%)
  between operations  14.1 us (6%)
  local copies, waits for them, and re-layouts  8.43 us (4%)
  other arithmetic  7.56 us (3%)
    pallas_call x4, Pallas kernels, exchange(): pl.pallas_call(functools.partial(_exchange_kernel, n, axis, gather), out_...  124 us
    all_gather x1, waiting for transfers between devices, per_device(): shard_rows = lax.all_gather(spectra, 'sub', axis=0, tiled=True)  56.9 us
    dot_general x1, matrix products, per_device(): lax.dot_general(shard_rows, grad_pre, (((0,), (0,)), ((), ())), preferred...  8.62 us
    dot_general x1, matrix products, per_device(): pre = jnp.dot(shard_rows, w_in, preferred_element_type=jnp.float32)  5.71 us
  transfers between devices with their start and end apart: 1, of which 1 were waited for; matrix products, arithmetic and copies ran while one was open for 1% of the time, Pallas kernels for 0%

profile of v3, /device:TPU:1, one launch (start us, length us, event | category | flops | bytes accessed | tf_op | source)
XLA Modules:
  0.0 232.9 jit_solution(11741888890608572175)
XLA Ops:
  7.2 0.0 copy-start
  7.2 0.0 all-gather.2.cloned.1.call-start
  7.2 0.7 all-gather.2.cloned.1.call-update
  7.9 0.8 copy.15
  8.7 0.1 eq.15
  8.8 0.8 copy.16
  9.5 56.9 %all-gather.2.cloned.1.call-done = bf16[1024,4096]{1,0:T(8,128)(2,1)} async-done(((bf16[128,4096]{1,0:T(8,128)(2,1)}), bf16[1024,4096]{1,0:T(8,128)(2,1)}) %all-gather.2.cloned.1.call-update) | async-done | bytes 8388624 | tf_op jit(solution)/shard_map/all_gather | solution.py:69
  66.4 0.0 copy-done
  66.4 5.7 %fusion.21 = f32[1024,256]{1,0:T(8,128)S(1)} fusion(bf16[1024,4096]{1,0:T(8,128)(2,1)} %all-gather.2.cloned.1.call-done, bf16[4096,256]{1,0:T(8,128)(2,1)S(1)} %copy-done), kind=kOutput, calls=%fused_computation.38 | convolution fusion | flops 2147483648 | bytes 11534336 | tf_op jit(solution)/shard_map/dot_general | solution.py:70
  72.1 0.0 copy-done.4
  72.2 0.0 copy-start.5
  72.2 1.9 fusion.20
  74.0 29.6 %shard_map.77 = f32[8,128,512]{2,1,0:T(8,128)} custom-call(f32[8,128,512]{2,1,0:T(8,128)} %bitcast.37), custom_call_target="tpu_custom_call" | custom-call | tf_op jit(solution)/shard_map/pallas_call | solution.py:51
  103.7 0.0 copy-start.3
  103.7 1.8 reduce_sum.45
  105.5 0.1 multiply_reduce_fusion.1
  105.6 1.0 fusion.3.x_ref
  106.7 16.1 %shard_map.78 = bf16[32,8,512]{2,1,0:T(8,128)(2,1)} custom-call(bf16[32,8,512]{2,1,0:T(8,128)(2,1)} %fusion.3.x_ref), custom_call_target="tpu_custom_call" | custom-call | tf_op jit(solution)/shard_map/pallas_call | solution.py:51
  122.8 1.2 fusion.7
  124.0 0.1 fusion.18
  124.0 1.5 multiply_reduce_fusion
  125.5 0.8 divide_convert_fusion.x_ref
  126.3 17.2 %shard_map.79 = bf16[8,128,512]{2,1,0:T(8,128)(2,1)} custom-call(bf16[128,512]{1,0:T(8,128)(2,1)} %divide_convert_fusion.x_ref), custom_call_target="tpu_custom_call" | custom-call | tf_op jit(solution)/shard_map/pallas_call | solution.py:51
  143.6 8.6 %fusion = bf16[4096,256]{0,1:T(8,128)(2,1)} fusion(bf16[1024,4096]{1,0:T(8,128)(2,1)} %all-gather.2.cloned.1.call-done, bf16[1024,512]{1,0:T(8,128)(2,1)} %bitcast.35, bf16[256,512]{1,0:T(8,128)(2,1)S(1)} %copy-done.4, f32[1024,256]{1,0:T(8,128)} %copy-done.5), kind=kOutput, calls=%fused_computation.1 | convolution fusion | flops 2419326976 | bytes 12845056 | tf_op jit(solution)/shard_map/dot_general | solution.py:113
  152.2 4.2 %copy.17 = bf16[4096,256]{1,0:T(8,128)(2,1)} copy(bf16[4096,256]{0,1:T(8,128)(2,1)} %fusion) | data formatting | bytes 4194304 | tf_op jit(solution)/shard_map/dot_general | solution.py:113
  156.4 1.3 copy.18
  157.7 2.2 convolution_convert_fusion.1
  160.0 1.6 pad_maximum_fusion.x_ref
  161.5 61.2 %shard_map.80 = bf16[32,144,256]{2,1,0:T(8,128)(2,1)} custom-call(bf16[32,144,256]{2,1,0:T(8,128)(2,1)} %pad_maximum_fusion.x_ref), custom_call_target="tpu_custom_call" | custom-call | tf_op jit(solution)/shard_map/pallas_call | solution.py:51
  222.8 2.0 convert_reduce_fusion
  224.8 0.7 slice.8
  225.5 0.6 slice.9
  (8 shorter events, 0.0 us)
Async XLA Ops:
  7.2 59.3 %copy-start = (bf16[4096,256]{1,0:T(8,128)(2,1)S(1)}, bf16[4096,256]{1,0:T(8,128)(2,1)}, u32[]{:S(2)}) copy-start(bf16[4096,256]{1,0:T(8,128)(2,1)} %param.7) | copy-start | bytes 6291460
  7.2 59.3 %all-gather.2.cloned.1.call-start = ((), (), s32[]{:S(2)}) async-start(), calls=%async_computation | async-start | bytes 9437184 | tf_op jit(solution)/shard_map/all_gather | solution.py:69
  9.5 62.6 %copy-start.4 = (bf16[256,512]{1,0:T(8,128)(2,1)S(1)}, bf16[256,512]{1,0:T(8,128)(2,1)}, u32[]{:S(2)}) copy-start(bf16[256,512]{1,0:T(8,128)(2,1)} %param.8) | copy-start | bytes 786436
  72.2 1.9 copy-start.5
  103.7 20.3 %copy-start.3 = (s32[1,1,32]{2,1,0:T(1,128)S(1)}, s32[1,1,32]{2,1,0:T(1,128)}, u32[]{:S(2)}) copy-start(s32[1,1,32]{2,1,0:T(1,128)} %param.10) | copy-start | bytes 388
  152.2 4.2 %copy-start.2 = (bf16[8,128,512]{2,1,0:T(8,128)(2,1)S(1)}, bf16[8,128,512]{2,1,0:T(8,128)(2,1)}, u32[]{:S(2)}) copy-start(bf16[8,128,512]{2,1,0:T(8,128)(2,1)} %shard_map.79) | copy-start | bytes 3145732
  157.7 2.3 copy-start.1
Sparse Core Ops, SparseCore 0:
  9.9 56.5 all-gather.1

commit v4 on v3

--- a/solution.py
+++ b/solution.py
@@ -10,46 +10,52 @@
 MESH = pl.DeviceIdType.MESH
 
 
-def _exchange_kernel(n, axis, gather, x_ref, o_ref, got, send_sems, recv_sems):
+def _exchange_kernel(n, stride, axis, gather, x_ref, o_ref, got, send_sems, recv_sems):
     me = lax.axis_index(axis)
+    mine = lax.rem(lax.div(me, stride), n)
+    base = me - mine * stride
+
+    def member(j):
+        return base + j * stride
+
     barrier = pltpu.get_barrier_semaphore()
     for k in range(1, n):
         pl.semaphore_signal(
-            barrier, inc=1, device_id={axis: lax.rem(me + k, n)}, device_id_type=MESH
+            barrier, inc=1, device_id={axis: member(lax.rem(mine + k, n))}, device_id_type=MESH
         )
     pl.semaphore_wait(barrier, n - 1)
     sends = []
     for k in range(1, n):
-        peer = lax.rem(me + k, n)
+        peer = lax.rem(mine + k, n)
         copy = pltpu.make_async_remote_copy(
             src_ref=x_ref if gather else x_ref.at[peer],
-            dst_ref=got.at[me],
+            dst_ref=got.at[mine],
             send_sem=send_sems.at[k],
             recv_sem=recv_sems.at[k],
-            device_id={axis: peer},
+            device_id={axis: member(peer)},
             device_id_type=MESH,
         )
         copy.start()
         sends.append(copy)
-    o_ref[me] = x_ref[...] if gather else x_ref[me]
+    o_ref[mine] = x_ref[...] if gather else x_ref[mine]
     for k in range(1, n):
         sends[k - 1].wait_send()
-        source = lax.rem(me + n - k, n)
+        source = lax.rem(mine + n - k, n)
         pltpu.make_async_remote_copy(
             src_ref=x_ref if gather else x_ref.at[source],
             dst_ref=got.at[source],
             send_sem=send_sems.at[k],
             recv_sem=recv_sems.at[k],
-            device_id={axis: source},
+            device_id={axis: member(source)},
             device_id_type=MESH,
         ).wait_recv()
         o_ref[source] = got[source]
 
 
-def exchange(x, axis, n, collective_id, gather=False):
+def exchange(x, axis, n, collective_id, gather=False, stride=1):
     shape = (n,) + x.shape if gather else x.shape
     return pl.pallas_call(
-        functools.partial(_exchange_kernel, n, axis, gather),
+        functools.partial(_exchange_kernel, n, stride, axis, gather),
         out_shape=jax.ShapeDtypeStruct(shape, x.dtype),
         in_specs=[pl.BlockSpec(memory_space=pltpu.VMEM)],
         out_specs=pl.BlockSpec(memory_space=pltpu.VMEM),
@@ -62,7 +68,37 @@
     )(x)
 
 
-def per_device(spectra, w_in, w_out, partner_rows, pair_counts, pair_labels):
+def reduce_scatter(x, axis, inner, first_inner, first_id):
+    outer = x.shape[0] // inner
+    blocks = x.reshape((outer, inner) + x.shape[1:])
+    phases = [(outer, inner), (inner, 1)]
+    if first_inner:
+        blocks = jnp.swapaxes(blocks, 0, 1)
+        phases.reverse()
+    for number, (size, stride) in enumerate(phases):
+        if size == 1:
+            blocks = blocks[0].astype(jnp.float32)
+            continue
+        got = exchange(blocks.astype(x.dtype), axis, size, first_id + number, stride=stride)
+        blocks = jnp.sum(got.astype(jnp.float32), axis=0)
+    return blocks
+
+
+def inner_size(devices):
+    coords = [tuple(getattr(d, "coords", ())) for d in devices]
+    if len(coords) < 2 or not coords[0]:
+        return len(coords)
+    varying = [c for c in range(len(coords[0])) if len({p[c] for p in coords}) > 1]
+    slow = [c for c in varying if coords[1][c] == coords[0][c]]
+    if not slow:
+        return 1
+    run = 0
+    while run < len(coords) and coords[run][slow[0]] == coords[0][slow[0]]:
+        run += 1
+    return run
+
+
+def per_device(mass_inner, sub_inner, spectra, w_in, w_out, partner_rows, pair_counts, pair_labels):
     own_rows = spectra.shape[0]
     peers = partner_rows.shape[2]
     slots = partner_rows.shape[3]
@@ -71,9 +107,8 @@
     hidden = jax.nn.silu(pre).astype(jnp.bfloat16)
     n_sub = shard_rows.shape[0] // own_rows
     embed_part = jnp.dot(hidden, w_out, preferred_element_type=jnp.float32)
-    embed = jnp.sum(
-        exchange(embed_part.reshape(n_sub, own_rows, embed_part.shape[1]), "sub", n_sub, 2),
-        axis=0,
+    embed = reduce_scatter(
+        embed_part.reshape(n_sub, own_rows, embed_part.shape[1]), "sub", sub_inner, True, 2
     )
     norm = jnp.sqrt(jnp.sum(embed * embed, axis=-1, keepdims=True) + 1e-06)
     unit = embed / norm
@@ -84,7 +119,7 @@
         selector.astype(jnp.bfloat16), unit_b, preferred_element_type=jnp.float32
     ).astype(jnp.bfloat16)
     outgoing = mine.reshape(peers, slots, mine.shape[1])
-    incoming = exchange(outgoing, "mass", peers, 0)
+    incoming = exchange(outgoing, "mass", peers, 1)
     theirs = incoming.astype(jnp.float32)
     sim = jnp.sum(outgoing.astype(jnp.float32) * theirs, axis=-1)
     valid = jnp.arange(slots, dtype=jnp.int32)[None, :] < pair_counts.reshape(peers)[:, None]
@@ -99,7 +134,7 @@
     )
     along = jnp.sum(unit * grad_unit, axis=-1, keepdims=True)
     grad_embed = ((grad_unit - unit * along) / norm).astype(jnp.bfloat16)
-    grad_rows = exchange(grad_embed, "sub", n_sub, 3, gather=True).reshape(
+    grad_rows = exchange(grad_embed, "sub", n_sub, 4, gather=True).reshape(
         n_sub * own_rows, grad_embed.shape[1]
     )
     back = lax.dot_general(
@@ -123,12 +158,7 @@
         ],
         axis=1,
     ).astype(jnp.bfloat16)
-    summed = jnp.sum(
-        exchange(partial, "mass", peers, 1).astype(
-            jnp.float32
-        ),
-        axis=0,
-    )
+    summed = reduce_scatter(partial, "mass", mass_inner, False, 5)
     grad_in, grad_out_t = summed[:in_rows], summed[in_rows:]
     return (grad_in, grad_out_t)
 
@@ -142,8 +172,10 @@
         P("mass", "sub", None),
         P("mass", "sub", None, None),
     )
+    mass_inner = inner_size(list(mesh.devices[:, 0]))
+    sub_inner = inner_size(list(mesh.devices[0, :]))
     return jax.shard_map(
-        per_device,
+        functools.partial(per_device, mass_inner, sub_inner),
         mesh=mesh,
         in_specs=placed,
         out_specs=(P("mass", "sub"), P("mass", "sub")),

time: 235 us -> 225 us (0.957)
  Pallas kernels: 124 us -> 111 us
  other arithmetic: 7.56 us -> 12.1 us
    pallas_call x4 -> x6, Pallas kernels: 124 us -> 111 us  [exchange(): pl.pallas_call(functools.partial(_exchange_kernel, n, stride, axis, gathe...]
    reduce_sum x2 -> x4, other arithmetic: 3.83 us -> 8.36 us  [reduce_scatter(): blocks = jnp.sum(got.astype(jnp.float32), axis=0)]
where the time goes in v4:
time: 225 us
  Pallas kernels  111 us (49%)
  waiting for transfers between devices  57.6 us (26%)
  matrix products  19.5 us (9%)
  between operations  14.2 us (6%)
  other arithmetic  12.1 us (5%)
  local copies, waits for them, and re-layouts  10.5 us (5%)
    pallas_call x6, Pallas kernels, exchange(): pl.pallas_call(functools.partial(_exchange_kernel, n, stride, axis, gathe...  111 us
    all_gather x1, waiting for transfers between devices, per_device(): shard_rows = lax.all_gather(spectra, 'sub', axis=0, tiled=True)  56.9 us
    dot_general x1, matrix products, per_device(): lax.dot_general(shard_rows, grad_pre, (((0,), (0,)), ((), ())), preferred...  8.62 us
    reduce_sum x4, other arithmetic, reduce_scatter(): blocks = jnp.sum(got.astype(jnp.float32), axis=0)  8.36 us
    dot_general x1, matrix products, per_device(): pre = jnp.dot(shard_rows, w_in, preferred_element_type=jnp.float32)  5.71 us
  transfers between devices with their start and end apart: 1, of which 1 were waited for; matrix products, arithmetic and copies ran while one was open for 1% of the time, Pallas kernels for 0%

profile of v4, /device:TPU:1, one launch (start us, length us, event | category | flops | bytes accessed | tf_op | source)
XLA Modules:
  0.0 224.6 jit_solution(3467095790222830318)
XLA Ops:
  7.2 0.7 all-gather.2.cloned.1.call-update
  7.9 0.8 copy.16
  8.7 0.1 eq.15
  8.8 0.8 copy.18
  9.5 56.9 %all-gather.2.cloned.1.call-done = bf16[1024,4096]{1,0:T(8,128)(2,1)} async-done(((bf16[128,4096]{1,0:T(8,128)(2,1)}), bf16[1024,4096]{1,0:T(8,128)(2,1)}) %all-gather.2.cloned.1.call-update) | async-done | bytes 8388624 | tf_op jit(solution)/shard_map/all_gather | solution.py:105
  66.4 5.7 %fusion.21 = f32[1024,256]{1,0:T(8,128)S(1)} fusion(bf16[1024,4096]{1,0:T(8,128)(2,1)} %all-gather.2.cloned.1.call-done, bf16[4096,256]{1,0:T(8,128)(2,1)S(1)} %copy-done), kind=kOutput, calls=%fused_computation.39 | convolution fusion | flops 2147483648 | bytes 11534336 | tf_op jit(solution)/shard_map/dot_general | solution.py:106
  72.2 0.5 fusion.20
  72.6 0.6 copy-done.5
  73.2 1.5 copy.23
  74.7 5.7 %shard_map.77 = f32[2,4,128,512]{3,2,1,0:T(8,128)} custom-call(f32[2,4,128,512]{3,2,1,0:T(8,128)} %bitcast.40), custom_call_target="tpu_custom_call" | custom-call | tf_op jit(solution)/shard_map/pallas_call | solution.py:57
  80.5 2.9 %reduce_sum.66.x_ref = f32[4,128,512]{2,1,0:T(8,128)} reduce(f32[2,4,128,512]{3,2,1,0:T(8,128)} %shard_map.77, f32[]{:T(128)} %constant.3.clone.1), dimensions={0}, to_apply=%region_0.1 | reduce | flops 262144 | bytes 3145732 | tf_op jit(solution)/shard_map/reduce_sum | solution.py:83
  83.4 17.1 %shard_map.78 = f32[4,128,512]{2,1,0:T(8,128)} custom-call(f32[4,128,512]{2,1,0:T(8,128)} %reduce_sum.66.x_ref), custom_call_target="tpu_custom_call" | custom-call | tf_op jit(solution)/shard_map/pallas_call | solution.py:57
  100.5 1.3 reduce_sum.67
  101.8 0.1 multiply_reduce_fusion.1
  101.9 1.0 fusion.3.x_ref
  103.0 16.0 %shard_map.79 = bf16[32,8,512]{2,1,0:T(8,128)(2,1)} custom-call(bf16[32,8,512]{2,1,0:T(8,128)(2,1)} %fusion.3.x_ref), custom_call_target="tpu_custom_call" | custom-call | tf_op jit(solution)/shard_map/pallas_call | solution.py:57
  118.9 1.2 fusion.7
  120.1 0.1 fusion.18
  120.2 1.5 multiply_reduce_fusion
  121.7 0.8 divide_convert_fusion.x_ref
  122.4 18.9 %shard_map.80 = bf16[8,128,512]{2,1,0:T(8,128)(2,1)} custom-call(bf16[128,512]{1,0:T(8,128)(2,1)} %divide_convert_fusion.x_ref), custom_call_target="tpu_custom_call" | custom-call | tf_op jit(solution)/shard_map/pallas_call | solution.py:57
  141.4 8.6 %fusion = bf16[4096,256]{0,1:T(8,128)(2,1)} fusion(bf16[1024,4096]{1,0:T(8,128)(2,1)} %all-gather.2.cloned.1.call-done, bf16[1024,512]{1,0:T(8,128)(2,1)} %bitcast.41, bf16[256,512]{1,0:T(8,128)(2,1)S(1)} %copy-done.4, f32[1024,256]{1,0:T(8,128)} %copy-done.5), kind=kOutput, calls=%fused_computation.1 | convolution fusion | flops 2419326976 | bytes 12845056 | tf_op jit(solution)/shard_map/dot_general | solution.py:148
  150.0 4.2 %copy.19 = bf16[4096,256]{1,0:T(8,128)(2,1)} copy(bf16[4096,256]{0,1:T(8,128)(2,1)} %fusion) | data formatting | bytes 4194304 | tf_op jit(solution)/shard_map/dot_general | solution.py:148
  154.2 1.3 copy.20
  155.5 2.2 convolution_convert_fusion.1
  157.8 1.6 pad_maximum_fusion.x_ref
  159.3 31.5 %shard_map.81 = bf16[4,8,144,256]{3,2,1,0:T(8,128)(2,1)} custom-call(bf16[4,8,144,256]{3,2,1,0:T(8,128)(2,1)} %pad_maximum_fusion.x_ref), custom_call_target="tpu_custom_call" | custom-call | tf_op jit(solution)/shard_map/pallas_call | solution.py:57
  190.9 3.0 %reduce_sum.71.x_ref = bf16[8,144,256]{2,1,0:T(8,128)(2,1)} reduce(bf16[4,8,144,256]{3,2,1,0:T(8,128)(2,1)} %shard_map.81, bf16[]{:T(256)} %constant.11.clone.1), dimensions={0}, to_apply=%region_5.6 | reduce | flops 884736 | bytes 2949122 | tf_op jit(solution)/shard_map/reduce_sum | solution.py:83
  193.9 21.4 %shard_map.82 = bf16[8,144,256]{2,1,0:T(8,128)(2,1)} custom-call(bf16[8,144,256]{2,1,0:T(8,128)(2,1)} %reduce_sum.71.x_ref), custom_call_target="tpu_custom_call" | custom-call | tf_op jit(solution)/shard_map/pallas_call | solution.py:57
  215.3 1.2 convert_reduce_fusion
  216.5 0.7 slice.8
  217.2 0.6 slice.9
  (13 shorter events, 0.1 us)
Async XLA Ops:
  7.2 59.3 %copy-start = (bf16[4096,256]{1,0:T(8,128)(2,1)S(1)}, bf16[4096,256]{1,0:T(8,128)(2,1)}, u32[]{:S(2)}) copy-start(bf16[4096,256]{1,0:T(8,128)(2,1)} %param.7) | copy-start | bytes 6291460
  7.2 59.3 %all-gather.2.cloned.1.call-start = ((), (), s32[]{:S(2)}) async-start(), calls=%async_computation | async-start | bytes 9437184 | tf_op jit(solution)/shard_map/all_gather | solution.py:105
  9.5 62.6 %copy-start.4 = (bf16[256,512]{1,0:T(8,128)(2,1)S(1)}, bf16[256,512]{1,0:T(8,128)(2,1)}, u32[]{:S(2)}) copy-start(bf16[256,512]{1,0:T(8,128)(2,1)} %param.8) | copy-start | bytes 786436
  72.2 1.1 copy-start.5
  83.4 36.7 %copy-start.3 = (s32[1,1,32]{2,1,0:T(1,128)S(1)}, s32[1,1,32]{2,1,0:T(1,128)}, u32[]{:S(2)}) copy-start(s32[1,1,32]{2,1,0:T(1,128)} %param.10) | copy-start | bytes 388
  150.0 4.2 %copy-start.2 = (bf16[8,128,512]{2,1,0:T(8,128)(2,1)S(1)}, bf16[8,128,512]{2,1,0:T(8,128)(2,1)}, u32[]{:S(2)}) copy-start(bf16[8,128,512]{2,1,0:T(8,128)(2,1)} %shard_map.80) | copy-start | bytes 3145732
  155.5 2.2 %copy-start.1 = (bf16[4096,256]{1,0:T(8,128)(2,1)S(1)}, bf16[4096,256]{1,0:T(8,128)(2,1)}, u32[]{:S(2)}) copy-start(bf16[4096,256]{1,0:T(8,128)(2,1)} %copy.19) | copy-start | bytes 6291460
Sparse Core Ops, SparseCore 0:
  9.9 56.5 all-gather.1

commit v5 on v4

--- a/solution.py
+++ b/solution.py
@@ -1,4 +1,5 @@
 import functools
+import math
 
 import jax
 import jax.numpy as jnp
@@ -64,17 +65,22 @@
             pltpu.SemaphoreType.DMA((n,)),
             pltpu.SemaphoreType.DMA((n,)),
         ],
-        compiler_params=pltpu.CompilerParams(collective_id=collective_id, has_side_effects=True),
+        compiler_params=pltpu.CompilerParams(
+            collective_id=collective_id,
+            has_side_effects=True,
+            vmem_limit_bytes=min(3 * x.dtype.itemsize * math.prod(shape) + (8 << 20), 60 << 20),
+        ),
     )(x)
 
 
 def reduce_scatter(x, axis, inner, first_inner, first_id):
     outer = x.shape[0] // inner
-    blocks = x.reshape((outer, inner) + x.shape[1:])
-    phases = [(outer, inner), (inner, 1)]
     if first_inner:
-        blocks = jnp.swapaxes(blocks, 0, 1)
-        phases.reverse()
+        blocks = x.reshape((inner, outer) + x.shape[1:])
+        phases = [(inner, 1), (outer, inner)]
+    else:
+        blocks = x.reshape((outer, inner) + x.shape[1:])
+        phases = [(outer, inner), (inner, 1)]
     for number, (size, stride) in enumerate(phases):
         if size == 1:
             blocks = blocks[0].astype(jnp.float32)
@@ -82,6 +88,17 @@
         got = exchange(blocks.astype(x.dtype), axis, size, first_id + number, stride=stride)
         blocks = jnp.sum(got.astype(jnp.float32), axis=0)
     return blocks
+
+
+def all_gather(x, axis, n, inner, first_id):
+    outer = n // inner
+    got = x[None]
+    if outer > 1:
+        got = exchange(x, axis, outer, first_id, gather=True, stride=inner)
+    got = got[None]
+    if inner > 1:
+        got = exchange(got[0], axis, inner, first_id + 1, gather=True)
+    return got.reshape((n * x.shape[0],) + x.shape[1:])
 
 
 def inner_size(devices):
@@ -98,17 +115,16 @@
     return run
 
 
-def per_device(mass_inner, sub_inner, spectra, w_in, w_out, partner_rows, pair_counts, pair_labels):
+def per_device(n_sub, mass_inner, sub_inner, spectra, w_in, w_out, partner_rows, pair_counts, pair_labels):
     own_rows = spectra.shape[0]
     peers = partner_rows.shape[2]
     slots = partner_rows.shape[3]
-    shard_rows = lax.all_gather(spectra, "sub", axis=0, tiled=True)
+    shard_rows = all_gather(spectra, "sub", n_sub, sub_inner, 2)
     pre = jnp.dot(shard_rows, w_in, preferred_element_type=jnp.float32)
     hidden = jax.nn.silu(pre).astype(jnp.bfloat16)
-    n_sub = shard_rows.shape[0] // own_rows
     embed_part = jnp.dot(hidden, w_out, preferred_element_type=jnp.float32)
     embed = reduce_scatter(
-        embed_part.reshape(n_sub, own_rows, embed_part.shape[1]), "sub", sub_inner, True, 2
+        embed_part.reshape(n_sub, own_rows, embed_part.shape[1]), "sub", sub_inner, True, 4
     )
     norm = jnp.sqrt(jnp.sum(embed * embed, axis=-1, keepdims=True) + 1e-06)
     unit = embed / norm
@@ -134,9 +150,7 @@
     )
     along = jnp.sum(unit * grad_unit, axis=-1, keepdims=True)
     grad_embed = ((grad_unit - unit * along) / norm).astype(jnp.bfloat16)
-    grad_rows = exchange(grad_embed, "sub", n_sub, 4, gather=True).reshape(
-        n_sub * own_rows, grad_embed.shape[1]
-    )
+    grad_rows = all_gather(grad_embed, "sub", n_sub, sub_inner, 6)
     back = lax.dot_general(
         grad_rows, w_out, (((1,), (1,)), ((), ())), preferred_element_type=jnp.float32
     )
@@ -158,7 +172,7 @@
         ],
         axis=1,
     ).astype(jnp.bfloat16)
-    summed = reduce_scatter(partial, "mass", mass_inner, False, 5)
+    summed = reduce_scatter(partial, "mass", mass_inner, False, 8)
     grad_in, grad_out_t = summed[:in_rows], summed[in_rows:]
     return (grad_in, grad_out_t)
 
@@ -175,7 +189,7 @@
     mass_inner = inner_size(list(mesh.devices[:, 0]))
     sub_inner = inner_size(list(mesh.devices[0, :]))
     return jax.shard_map(
-        functools.partial(per_device, mass_inner, sub_inner),
+        functools.partial(per_device, mesh.shape["sub"], mass_inner, sub_inner),
         mesh=mesh,
         in_specs=placed,
         out_specs=(P("mass", "sub"), P("mass", "sub")),

time: 225 us -> 187 us (0.83)
  waiting for transfers between devices: 57.6 us -> 0 us
  Pallas kernels: 111 us -> 153 us
  between operations: 14.2 us -> 0.88 us
  other arithmetic: 12.1 us -> 5.73 us
  matrix products: 19.5 us -> 14.2 us
  local copies, waits for them, and re-layouts: 10.5 us -> 13.7 us
    all_gather x1 -> x0, waiting for transfers between devices: 56.9 us -> none  [per_device(): shard_rows = lax.all_gather(spectra, 'sub', axis=0, tiled=True)]
    pallas_call x6 -> x9, Pallas kernels: 111 us -> 153 us  [exchange(): pl.pallas_call(functools.partial(_exchange_kernel, n, stride, axis, gathe...]
    unnamed x14 -> x28, local copies, waits for them, and re-layouts: 2.13 us -> 6.93 us
    dot_general x1, matrix products: 5.71 us -> 2.34 us  [per_device(): pre = jnp.dot(shard_rows, w_in, preferred_element_type=jnp.float32)]
    reduce_sum x4, other arithmetic: 8.36 us -> 5.1 us  [reduce_scatter(): blocks = jnp.sum(got.astype(jnp.float32), axis=0)]
  transfers between devices with their start and end apart: 1 -> 0, of which waited for: 1 -> 0; matrix products, arithmetic and copies ran while one was open for 1% -> 0% of each run, Pallas kernels for 0% -> 0%
where the time goes in v5:
time: 187 us
  Pallas kernels  153 us (82%)
  matrix products  14.2 us (8%)
  local copies, waits for them, and re-layouts  13.7 us (7%)
  other arithmetic  5.73 us (3%)
    pallas_call x9, Pallas kernels, exchange(): pl.pallas_call(functools.partial(_exchange_kernel, n, stride, axis, gathe...  153 us
    dot_general x1, matrix products, per_device(): lax.dot_general(shard_rows, grad_pre, (((0,), (0,)), ((), ())), preferred...  8.31 us
    unnamed x28, local copies, waits for them, and re-layouts  6.93 us
    reduce_sum x4, other arithmetic, reduce_scatter(): blocks = jnp.sum(got.astype(jnp.float32), axis=0)  5.1 us
    dot_general x1, local copies, waits for them, and re-layouts, per_device(): lax.dot_general(shard_rows, grad_pre, (((0,), (0,)), ((), ())), preferred...  4.1 us

profile of v5, /device:TPU:1, one launch (start us, length us, event | category | flops | bytes accessed | tf_op | source)
XLA Modules:
  0.0 187.2 jit_solution(4036889766886667898)
XLA Ops:
  0.7 1.4 copy-done.5
  2.0 49.4 %shard_map.77.x_ref = bf16[4,128,4096]{2,1,0:T(8,128)(2,1)S(1)} custom-call(bf16[128,4096]{1,0:T(8,128)(2,1)S(1)} %copy-done.5), custom_call_target="tpu_custom_call" | custom-call | tf_op jit(solution)/shard_map/pallas_call | solution.py:58
  51.4 9.4 %shard_map.78 = bf16[2,4,128,4096]{3,2,1,0:T(8,128)(2,1)S(1)} custom-call(bf16[4,128,4096]{2,1,0:T(8,128)(2,1)S(1)} %shard_map.77.x_ref), custom_call_target="tpu_custom_call" | custom-call | tf_op jit(solution)/shard_map/pallas_call | solution.py:58
  60.8 2.3 %fusion.21 = f32[1024,256]{1,0:T(8,128)S(1)} fusion(bf16[1024,4096]{1,0:T(8,128)(2,1)S(1)} %bitcast.37, bf16[4096,256]{1,0:T(8,128)(2,1)S(1)} %copy-done), kind=kOutput, calls=%fused_computation.38 | convolution fusion | flops 2147483648 | bytes 11534336 | tf_op jit(solution)/shard_map/dot_general | solution.py:123
  63.2 0.8 copy-done.2
  64.0 0.5 fusion.20
  64.5 0.5 copy-done.12
  65.0 2.8 %shard_map.79 = f32[2,4,128,512]{3,2,1,0:T(8,128)S(1)} custom-call(f32[2,4,128,512]{3,2,1,0:T(8,128)S(1)} %bitcast.41), custom_call_target="tpu_custom_call" | custom-call | tf_op jit(solution)/shard_map/pallas_call | solution.py:58
  67.8 1.4 copy-done.3
  69.2 2.9 %reduce_sum.66.x_ref = f32[4,128,512]{2,1,0:T(8,128)} reduce(f32[2,4,128,512]{3,2,1,0:T(8,128)} %copy-done.3, f32[]{:T(128)} %constant.3.clone.1), dimensions={0}, to_apply=%region_0.1 | reduce | flops 262144 | bytes 3145732 | tf_op jit(solution)/shard_map/reduce_sum | solution.py:89
  72.1 1.2 copy-done.4
  73.3 14.7 %shard_map.80 = f32[4,128,512]{2,1,0:T(8,128)S(1)} custom-call(f32[4,128,512]{2,1,0:T(8,128)S(1)} %copy-done.4), custom_call_target="tpu_custom_call" | custom-call | tf_op jit(solution)/shard_map/pallas_call | solution.py:58
  88.1 0.1 multiply_reduce_fusion.1
  88.3 0.1 eq.15
  88.4 0.3 fusion.3.x_ref
  88.7 16.3 %shard_map.81 = bf16[32,8,512]{2,1,0:T(8,128)(2,1)S(1)} custom-call(bf16[32,8,512]{2,1,0:T(8,128)(2,1)S(1)} %fusion.3.x_ref), custom_call_target="tpu_custom_call" | custom-call | tf_op jit(solution)/shard_map/pallas_call | solution.py:58
  105.0 0.1 fusion.7
  105.3 0.5 multiply_reduce_fusion
  105.9 0.1 divide_convert_fusion.x_ref
  106.0 9.2 %shard_map.82.x_ref = bf16[4,128,512]{2,1,0:T(8,128)(2,1)S(1)} custom-call(bf16[128,512]{1,0:T(8,128)(2,1)S(1)} %divide_convert_fusion.x_ref), custom_call_target="tpu_custom_call" | custom-call | tf_op jit(solution)/shard_map/pallas_call | solution.py:58
  115.3 4.4 %shard_map.83 = bf16[2,4,128,512]{3,2,1,0:T(8,128)(2,1)S(1)} custom-call(bf16[4,128,512]{2,1,0:T(8,128)(2,1)S(1)} %shard_map.82.x_ref), custom_call_target="tpu_custom_call" | custom-call | tf_op jit(solution)/shard_map/pallas_call | solution.py:58
  119.7 8.3 %fusion = bf16[4096,256]{0,1:T(8,128)(2,1)} fusion(bf16[1024,4096]{1,0:T(8,128)(2,1)} %bitcast.38, bf16[1024,512]{1,0:T(8,128)(2,1)S(1)} %bitcast.39, bf16[256,512]{1,0:T(8,128)(2,1)S(1)} %copy-done.11, f32[1024,256]{1,0:T(8,128)} %copy-done.12), kind=kOutput, calls=%fused_computation.1 | convolution fusion | flops 2419326976 | bytes 12845056 | tf_op jit(solution)/shard_map/dot_general | solution.py:162
  128.0 4.1 %copy.17 = bf16[4096,256]{1,0:T(8,128)(2,1)} copy(bf16[4096,256]{0,1:T(8,128)(2,1)} %fusion) | data formatting | bytes 4194304 | tf_op jit(solution)/shard_map/dot_general | solution.py:162
  132.1 1.3 copy.18
  133.5 2.2 %convolution_convert_fusion.1 = bf16[4,8,16,256]{3,2,1,0:T(8,128)(2,1)S(1)} fusion(bf16[4,8,16,1024]{3,2,1,0:T(8,128)(2,1)} %bitcast.43, f32[1024,256]{1,0:T(8,128)} %copy-done.12), kind=kOutput, calls=%fused_computation.6 | convolution fusion | flops 269877248 | bytes 2359296 | tf_op jit(solution)/shard_map/dot_general | solution.py:159
  135.7 0.2 pad_maximum_fusion.x_ref
  135.9 29.0 %shard_map.84 = bf16[4,8,144,256]{3,2,1,0:T(8,128)(2,1)S(1)} custom-call(bf16[4,8,144,256]{3,2,1,0:T(8,128)(2,1)S(1)} %pad_maximum_fusion.x_ref), custom_call_target="tpu_custom_call" | custom-call | tf_op jit(solution)/shard_map/pallas_call | solution.py:58
  164.9 1.4 copy-done.1
  166.3 2.1 %reduce_sum.71.x_ref = bf16[8,144,256]{2,1,0:T(8,128)(2,1)S(1)} reduce(bf16[4,8,144,256]{3,2,1,0:T(8,128)(2,1)} %copy-done.1, bf16[]{:T(256)} %constant.11.clone.1), dimensions={0}, to_apply=%region_5.6 | reduce | flops 884736 | bytes 2949122 | tf_op jit(solution)/shard_map/reduce_sum | solution.py:89
  168.4 17.4 %shard_map.85 = bf16[8,144,256]{2,1,0:T(8,128)(2,1)S(1)} custom-call(bf16[8,144,256]{2,1,0:T(8,128)(2,1)S(1)} %reduce_sum.71.x_ref), custom_call_target="tpu_custom_call" | custom-call | tf_op jit(solution)/shard_map/pallas_call | solution.py:58
  185.9 0.7 slice.8
  186.6 0.6 slice.9
  (26 shorter events, 0.4 us)
Async XLA Ops:
  0.6 60.2 %copy-start = (bf16[4096,256]{1,0:T(8,128)(2,1)S(1)}, bf16[4096,256]{1,0:T(8,128)(2,1)}, u32[]{:S(2)}) copy-start(bf16[4096,256]{1,0:T(8,128)(2,1)} %param.7) | copy-start | bytes 6291460
  0.6 1.4 copy-start.5
  60.8 3.2 %copy-start.2 = (bf16[2,4,128,4096]{3,2,1,0:T(8,128)(2,1)}, bf16[2,4,128,4096]{3,2,1,0:T(8,128)(2,1)S(1)}, u32[]{:S(2)}) copy-start(bf16[2,4,128,4096]{3,2,1,0:T(8,128)(2,1)S(1)} %shard_map.78) | copy-start | bytes 25165828
  60.8 3.2 %copy-start.10 = (bf16[256,512]{1,0:T(8,128)(2,1)S(1)}, bf16[256,512]{1,0:T(8,128)(2,1)}, u32[]{:S(2)}) copy-start(bf16[256,512]{1,0:T(8,128)(2,1)} %param.8) | copy-start | bytes 786436
  64.0 1.0 copy-start.12
  67.8 1.4 copy-start.3
  72.0 1.2 copy-start.4
  73.3 15.0 %copy-start.7 = (s32[1,1,32,8]{2,3,1,0:T(8,128)S(1)}, s32[1,1,32,8]{2,3,1,0:T(8,128)}, u32[]{:S(2)}) copy-start(s32[1,1,32,8]{2,3,1,0:T(8,128)} %param.9) | copy-start | bytes 3076
  73.3 31.9 %copy-start.8 = (s32[1,1,32,8]{2,3,1,0:T(8,128)S(1)}, s32[1,1,32,8]{2,3,1,0:T(8,128)}, u32[]{:S(2)}) copy-start(s32[1,1,32,8]{2,3,1,0:T(8,128)} %param.11) | copy-start | bytes 3076
  73.3 32.0 %copy-start.9 = (s32[1,1,32]{2,1,0:T(1,128)S(1)}, s32[1,1,32]{2,1,0:T(1,128)}, u32[]{:S(2)}) copy-start(s32[1,1,32]{2,1,0:T(1,128)} %param.10) | copy-start | bytes 388
  105.0 14.7 %copy-start.11 = (bf16[256,512]{1,0:T(8,128)(2,1)S(1)}, bf16[256,512]{1,0:T(8,128)(2,1)}, u32[]{:S(2)}) copy-start(bf16[256,512]{1,0:T(8,128)(2,1)} %param.8) | copy-start | bytes 786436
  133.4 2.3 %copy-start.6 = (bf16[4096,256]{1,0:T(8,128)(2,1)S(1)}, bf16[4096,256]{1,0:T(8,128)(2,1)}, u32[]{:S(2)}) copy-start(bf16[4096,256]{1,0:T(8,128)(2,1)} %copy.17) | copy-start | bytes 6291460
  164.9 1.4 copy-start.1

commit v6 on v5

--- a/solution.py
+++ b/solution.py
@@ -159,21 +159,24 @@
     out_part = lax.dot_general(
         grad_rows, hidden, (((0,), (0,)), ((), ())), preferred_element_type=jnp.float32
     )
-    in_part = lax.dot_general(
-        shard_rows, grad_pre, (((0,), (0,)), ((), ())), preferred_element_type=jnp.float32
+    in_part_t = lax.dot_general(
+        grad_pre, shard_rows, (((0,), (0,)), ((), ())), preferred_element_type=jnp.float32
     )
     n_mass = peers
-    in_rows = in_part.shape[0] // n_mass
+    hid = in_part_t.shape[0]
+    in_cols = in_part_t.shape[1] // n_mass
     out_rows = out_part.shape[0] // n_mass
+    lanes = in_cols
     partial = jnp.concatenate(
         [
-            in_part.reshape(n_mass, in_rows, in_part.shape[1]),
-            out_part.reshape(n_mass, out_rows, out_part.shape[1]),
+            jnp.swapaxes(in_part_t.astype(jnp.bfloat16).reshape(hid, n_mass, in_cols), 0, 1),
+            out_part.astype(jnp.bfloat16).reshape(n_mass, out_rows * hid // lanes, lanes),
         ],
         axis=1,
-    ).astype(jnp.bfloat16)
+    )
     summed = reduce_scatter(partial, "mass", mass_inner, False, 8)
-    grad_in, grad_out_t = summed[:in_rows], summed[in_rows:]
+    grad_in = summed[:hid].T
+    grad_out_t = summed[hid:].reshape(out_rows, hid)
     return (grad_in, grad_out_t)
 
 

time: 187 us -> 186 us (level)
    dot_general x2 -> x0, local copies, waits for them, and re-layouts: 5.43 us -> none  [the longest x1 4.1 us: per_device(): lax.dot_general(shard_rows, grad_pre, (((0,), (0,)), ((), ())), preferred...]
    reshape x0 -> x2, local copies, waits for them, and re-layouts: none -> 4.23 us  [the longest x1 3.61 us: per_device(): in_part_t.astype(jnp.bfloat16).reshape(hid, n_mass, in_cols)]
    unnamed x28 -> x27, local copies, waits for them, and re-layouts: 6.93 us -> 7.68 us
where the time goes in v6:
time: 186 us
  Pallas kernels  153 us (82%)
  matrix products  12.6 us (7%)
  local copies, waits for them, and re-layouts  12.1 us (7%)
  other arithmetic  7.34 us (4%)
    pallas_call x9, Pallas kernels, exchange(): pl.pallas_call(functools.partial(_exchange_kernel, n, stride, axis, gathe...  153 us
    dot_general x1, matrix products, per_device(): lax.dot_general(grad_pre, shard_rows, (((0,), (0,)), ((), ())), preferred...  8.39 us
    unnamed x27, local copies, waits for them, and re-layouts  7.68 us
    reduce_sum x4, other arithmetic, reduce_scatter(): blocks = jnp.sum(got.astype(jnp.float32), axis=0)  5.11 us

profile of v6, /device:TPU:1, one launch (start us, length us, event | category | flops | bytes accessed | tf_op | source)
XLA Modules:
  0.0 185.6 jit_solution(10468847771399483043)
XLA Ops:
  0.7 1.4 copy-done.5
  2.0 49.4 %shard_map.77.x_ref = bf16[4,128,4096]{2,1,0:T(8,128)(2,1)S(1)} custom-call(bf16[128,4096]{1,0:T(8,128)(2,1)S(1)} %copy-done.5), custom_call_target="tpu_custom_call" | custom-call | tf_op jit(solution)/shard_map/pallas_call | solution.py:58
  51.4 9.4 %shard_map.78 = bf16[2,4,128,4096]{3,2,1,0:T(8,128)(2,1)S(1)} custom-call(bf16[4,128,4096]{2,1,0:T(8,128)(2,1)S(1)} %shard_map.77.x_ref), custom_call_target="tpu_custom_call" | custom-call | tf_op jit(solution)/shard_map/pallas_call | solution.py:58
  60.8 2.3 %fusion.20 = f32[1024,256]{1,0:T(8,128)S(1)} fusion(bf16[1024,4096]{1,0:T(8,128)(2,1)S(1)} %bitcast.36, bf16[4096,256]{1,0:T(8,128)(2,1)S(1)} %copy-done), kind=kOutput, calls=%fused_computation.39 | convolution fusion | flops 2147483648 | bytes 11534336 | tf_op jit(solution)/shard_map/dot_general | solution.py:123
  63.2 0.8 copy-done.2
  64.0 0.5 fusion.19
  64.5 0.5 copy-done.10
  65.0 2.8 %shard_map.79 = f32[2,4,128,512]{3,2,1,0:T(8,128)S(1)} custom-call(f32[2,4,128,512]{3,2,1,0:T(8,128)S(1)} %bitcast.38), custom_call_target="tpu_custom_call" | custom-call | tf_op jit(solution)/shard_map/pallas_call | solution.py:58
  67.8 1.4 copy-done.3
  69.2 2.9 %reduce_sum.66.x_ref = f32[4,128,512]{2,1,0:T(8,128)} reduce(f32[2,4,128,512]{3,2,1,0:T(8,128)} %copy-done.3, f32[]{:T(128)} %constant.3.clone.1), dimensions={0}, to_apply=%region_0.1 | reduce | flops 262144 | bytes 3145732 | tf_op jit(solution)/shard_map/reduce_sum | solution.py:89
  72.1 1.2 copy-done.4
  73.3 14.7 %shard_map.80 = f32[4,128,512]{2,1,0:T(8,128)S(1)} custom-call(f32[4,128,512]{2,1,0:T(8,128)S(1)} %copy-done.4), custom_call_target="tpu_custom_call" | custom-call | tf_op jit(solution)/shard_map/pallas_call | solution.py:58
  88.1 0.1 multiply_reduce_fusion.1
  88.3 0.1 eq.15
  88.4 0.3 fusion.3.x_ref
  88.7 16.3 %shard_map.81 = bf16[32,8,512]{2,1,0:T(8,128)(2,1)S(1)} custom-call(bf16[32,8,512]{2,1,0:T(8,128)(2,1)S(1)} %fusion.3.x_ref), custom_call_target="tpu_custom_call" | custom-call | tf_op jit(solution)/shard_map/pallas_call | solution.py:58
  105.0 0.1 fusion.7
  105.3 0.5 multiply_reduce_fusion
  105.8 0.1 divide_convert_fusion.x_ref
  106.0 9.2 %shard_map.82.x_ref = bf16[4,128,512]{2,1,0:T(8,128)(2,1)S(1)} custom-call(bf16[128,512]{1,0:T(8,128)(2,1)S(1)} %divide_convert_fusion.x_ref), custom_call_target="tpu_custom_call" | custom-call | tf_op jit(solution)/shard_map/pallas_call | solution.py:58
  115.2 4.4 %shard_map.83 = bf16[2,4,128,512]{3,2,1,0:T(8,128)(2,1)S(1)} custom-call(bf16[4,128,512]{2,1,0:T(8,128)(2,1)S(1)} %shard_map.82.x_ref), custom_call_target="tpu_custom_call" | custom-call | tf_op jit(solution)/shard_map/pallas_call | solution.py:58
  119.7 8.4 %fusion = bf16[32,32,8,128]{3,2,1,0:T(8,128)(2,1)} fusion(bf16[1024,4096]{1,0:T(8,128)(2,1)} %bitcast.37, bf16[1024,512]{1,0:T(8,128)(2,1)S(1)} %bitcast.39, bf16[256,512]{1,0:T(8,128)(2,1)} %param.8, f32[1024,256]{1,0:T(8,128)} %copy-done.10), kind=kOutput, calls=%fused_computation.3 | convolution fusion | flops 2419326976 | bytes 12845056 | tf_op jit(solution)/shard_map/dot_general | solution.py:162
  128.1 3.6 %copy.21 = bf16[32,32,8,128]{3,2,0,1:T(8,128)(2,1)} copy(bf16[32,32,8,128]{3,2,1,0:T(8,128)(2,1)} %fusion) | data formatting | bytes 4194304 | tf_op jit(solution)/shard_map/reshape | solution.py:172
  131.7 0.6 convolution_convert_fusion.1
  132.3 0.1 concatenate.9
  132.4 1.8 pad_maximum_fusion.x_ref
  134.2 29.0 %shard_map.84 = bf16[4,8,288,128]{3,2,1,0:T(8,128)(2,1)S(1)} custom-call(bf16[4,8,288,128]{3,2,1,0:T(8,128)(2,1)S(1)} %pad_maximum_fusion.x_ref), custom_call_target="tpu_custom_call" | custom-call | tf_op jit(solution)/shard_map/pallas_call | solution.py:58
  163.2 1.4 copy-done.1
  164.6 2.1 %reduce_sum.71.x_ref = bf16[8,288,128]{2,1,0:T(8,128)(2,1)S(1)} reduce(bf16[4,8,288,128]{3,2,1,0:T(8,128)(2,1)} %copy-done.1, bf16[]{:T(256)} %constant.11.clone.1), dimensions={0}, to_apply=%region_5.6 | reduce | flops 884736 | bytes 2949122 | tf_op jit(solution)/shard_map/reduce_sum | solution.py:89
  166.7 17.4 %shard_map.85 = bf16[8,288,128]{2,1,0:T(8,128)(2,1)S(1)} custom-call(bf16[8,288,128]{2,1,0:T(8,128)(2,1)S(1)} %reduce_sum.71.x_ref), custom_call_target="tpu_custom_call" | custom-call | tf_op jit(solution)/shard_map/pallas_call | solution.py:58
  184.2 0.8 copy.18
  185.0 0.6 reshape.76
  (26 shorter events, 0.5 us)
Async XLA Ops:
  0.6 60.2 %copy-start = (bf16[4096,256]{1,0:T(8,128)(2,1)S(1)}, bf16[4096,256]{1,0:T(8,128)(2,1)}, u32[]{:S(2)}) copy-start(bf16[4096,256]{1,0:T(8,128)(2,1)} %param.7) | copy-start | bytes 6291460
  0.6 1.4 copy-start.5
  60.8 3.2 %copy-start.2 = (bf16[2,4,128,4096]{3,2,1,0:T(8,128)(2,1)}, bf16[2,4,128,4096]{3,2,1,0:T(8,128)(2,1)S(1)}, u32[]{:S(2)}) copy-start(bf16[2,4,128,4096]{3,2,1,0:T(8,128)(2,1)S(1)} %shard_map.78) | copy-start | bytes 25165828
  60.8 3.2 %copy-start.9 = (bf16[256,512]{1,0:T(8,128)(2,1)S(1)}, bf16[256,512]{1,0:T(8,128)(2,1)}, u32[]{:S(2)}) copy-start(bf16[256,512]{1,0:T(8,128)(2,1)} %param.8) | copy-start | bytes 786436
  64.0 1.0 copy-start.10
  67.8 1.4 copy-start.3
  72.0 1.2 copy-start.4
  73.3 15.0 %copy-start.6 = (s32[1,1,32,8]{2,3,1,0:T(8,128)S(1)}, s32[1,1,32,8]{2,3,1,0:T(8,128)}, u32[]{:S(2)}) copy-start(s32[1,1,32,8]{2,3,1,0:T(8,128)} %param.9) | copy-start | bytes 3076
  73.3 31.9 %copy-start.7 = (s32[1,1,32,8]{2,3,1,0:T(8,128)S(1)}, s32[1,1,32,8]{2,3,1,0:T(8,128)}, u32[]{:S(2)}) copy-start(s32[1,1,32,8]{2,3,1,0:T(8,128)} %param.11) | copy-start | bytes 3076
  73.3 32.0 %copy-start.8 = (s32[1,1,32]{2,1,0:T(1,128)S(1)}, s32[1,1,32]{2,1,0:T(1,128)}, u32[]{:S(2)}) copy-start(s32[1,1,32]{2,1,0:T(1,128)} %param.10) | copy-start | bytes 388
  128.1 3.6 %copy-start.11 = (f32[1024,256]{1,0:T(8,128)S(1)}, f32[1024,256]{1,0:T(8,128)}, u32[]{:S(2)}) copy-start(f32[1024,256]{1,0:T(8,128)} %copy-done.10) | copy-start | bytes 3145732
  163.2 1.4 copy-start.1

commit v7 on v6

--- a/solution.py
+++ b/solution.py
@@ -155,7 +155,9 @@
         grad_rows, w_out, (((1,), (1,)), ((), ())), preferred_element_type=jnp.float32
     )
     gate = jax.nn.sigmoid(pre)
-    grad_pre = (back * gate * (1.0 + pre * (1.0 - gate))).astype(jnp.bfloat16)
+    grad_pre = lax.optimization_barrier(
+        (back * gate * (1.0 + pre * (1.0 - gate))).astype(jnp.bfloat16)
+    )
     out_part = lax.dot_general(
         grad_rows, hidden, (((0,), (0,)), ((), ())), preferred_element_type=jnp.float32
     )

time: 186 us -> 182 us (0.978)
  matrix products: 12.6 us -> 10.5 us
    dot_general x1, matrix products: 8.39 us -> 5.77 us  [per_device(): lax.dot_general(grad_pre, shard_rows, (((0,), (0,)), ((), ())), preferred...]
    unnamed x27 -> x29, local copies, waits for them, and re-layouts: 7.68 us -> 7.69 us
where the time goes in v7:
time: 182 us
  Pallas kernels  153 us (84%)
  matrix products  10.5 us (6%)
  local copies, waits for them, and re-layouts  10.4 us (6%)
  other arithmetic  7.34 us (4%)
    pallas_call x9, Pallas kernels, exchange(): pl.pallas_call(functools.partial(_exchange_kernel, n, stride, axis, gathe...  153 us
    unnamed x29, local copies, waits for them, and re-layouts  7.69 us
    dot_general x1, matrix products, per_device(): lax.dot_general(grad_pre, shard_rows, (((0,), (0,)), ((), ())), preferred...  5.77 us
    reduce_sum x4, other arithmetic, reduce_scatter(): blocks = jnp.sum(got.astype(jnp.float32), axis=0)  5.11 us

profile of v7, /device:TPU:1, one launch (start us, length us, event | category | flops | bytes accessed | tf_op | source)
XLA Modules:
  0.0 181.8 jit_solution(16331409233083989086)
XLA Ops:
  0.7 1.4 copy-done.5
  2.0 49.4 %shard_map.77.x_ref = bf16[4,128,4096]{2,1,0:T(8,128)(2,1)S(1)} custom-call(bf16[128,4096]{1,0:T(8,128)(2,1)S(1)} %copy-done.5), custom_call_target="tpu_custom_call" | custom-call | tf_op jit(solution)/shard_map/pallas_call | solution.py:58
  51.4 9.4 %shard_map.78 = bf16[2,4,128,4096]{3,2,1,0:T(8,128)(2,1)S(1)} custom-call(bf16[4,128,4096]{2,1,0:T(8,128)(2,1)S(1)} %shard_map.77.x_ref), custom_call_target="tpu_custom_call" | custom-call | tf_op jit(solution)/shard_map/pallas_call | solution.py:58
  60.8 2.3 %fusion.15 = f32[1024,256]{1,0:T(8,128)S(1)} fusion(bf16[1024,4096]{1,0:T(8,128)(2,1)S(1)} %bitcast.37, bf16[4096,256]{1,0:T(8,128)(2,1)S(1)} %copy-done), kind=kOutput, calls=%fused_computation.34 | convolution fusion | flops 2147483648 | bytes 11534336 | tf_op jit(solution)/shard_map/dot_general | solution.py:123
  63.2 0.8 copy-done.1
  64.0 0.5 fusion.14
  64.5 0.5 copy-done.11
  65.0 2.8 %shard_map.79 = f32[2,4,128,512]{3,2,1,0:T(8,128)S(1)} custom-call(f32[2,4,128,512]{3,2,1,0:T(8,128)S(1)} %bitcast.39), custom_call_target="tpu_custom_call" | custom-call | tf_op jit(solution)/shard_map/pallas_call | solution.py:58
  67.8 1.4 copy-done.3
  69.2 2.9 %reduce_sum.66.x_ref = f32[4,128,512]{2,1,0:T(8,128)} reduce(f32[2,4,128,512]{3,2,1,0:T(8,128)} %copy-done.3, f32[]{:T(128)} %constant.3.clone.1), dimensions={0}, to_apply=%region_0.1 | reduce | flops 262144 | bytes 3145732 | tf_op jit(solution)/shard_map/reduce_sum | solution.py:89
  72.1 1.2 copy-done.4
  73.3 14.7 %shard_map.80 = f32[4,128,512]{2,1,0:T(8,128)S(1)} custom-call(f32[4,128,512]{2,1,0:T(8,128)S(1)} %copy-done.4), custom_call_target="tpu_custom_call" | custom-call | tf_op jit(solution)/shard_map/pallas_call | solution.py:58
  88.1 0.1 multiply_reduce_fusion.1
  88.4 0.3 fusion.3.x_ref
  88.7 16.3 %shard_map.81 = bf16[32,8,512]{2,1,0:T(8,128)(2,1)S(1)} custom-call(bf16[32,8,512]{2,1,0:T(8,128)(2,1)S(1)} %fusion.3.x_ref), custom_call_target="tpu_custom_call" | custom-call | tf_op jit(solution)/shard_map/pallas_call | solution.py:58
  105.0 0.1 fusion.4
  105.3 0.5 multiply_reduce_fusion
  105.9 0.1 divide_convert_fusion.x_ref
  106.0 9.2 %shard_map.82.x_ref = bf16[4,128,512]{2,1,0:T(8,128)(2,1)S(1)} custom-call(bf16[128,512]{1,0:T(8,128)(2,1)S(1)} %divide_convert_fusion.x_ref), custom_call_target="tpu_custom_call" | custom-call | tf_op jit(solution)/shard_map/pallas_call | solution.py:58
  115.2 4.4 %shard_map.83 = bf16[2,4,128,512]{3,2,1,0:T(8,128)(2,1)S(1)} custom-call(bf16[4,128,512]{2,1,0:T(8,128)(2,1)S(1)} %shard_map.82.x_ref), custom_call_target="tpu_custom_call" | custom-call | tf_op jit(solution)/shard_map/pallas_call | solution.py:58
  119.7 0.5 fusion.2
  120.3 5.8 %fusion = bf16[32,32,8,128]{3,2,1,0:T(8,128)(2,1)S(1)} fusion(bf16[1024,256]{1,0:T(8,128)(2,1)S(1)} %fusion.2, bf16[1024,4096]{1,0:T(8,128)(2,1)} %bitcast.38), kind=kOutput, calls=%fused_computation.3 | convolution fusion | flops 2148532224 | bytes 11010048 | tf_op jit(solution)/shard_map/dot_general | solution.py:164
  126.0 1.9 %copy.21 = bf16[32,32,8,128]{3,2,0,1:T(8,128)(2,1)} copy(bf16[32,32,8,128]{3,2,1,0:T(8,128)(2,1)S(1)} %fusion) | data formatting | bytes 4194304 | tf_op jit(solution)/shard_map/reshape | solution.py:174
  128.0 0.6 convolution_convert_fusion.1
  128.6 0.1 concatenate.9
  128.6 1.8 pad_maximum_fusion.x_ref
  130.4 29.0 %shard_map.84 = bf16[4,8,288,128]{3,2,1,0:T(8,128)(2,1)S(1)} custom-call(bf16[4,8,288,128]{3,2,1,0:T(8,128)(2,1)S(1)} %pad_maximum_fusion.x_ref), custom_call_target="tpu_custom_call" | custom-call | tf_op jit(solution)/shard_map/pallas_call | solution.py:58
  159.5 1.4 copy-done.2
  160.9 2.1 %reduce_sum.71.x_ref = bf16[8,288,128]{2,1,0:T(8,128)(2,1)S(1)} reduce(bf16[4,8,288,128]{3,2,1,0:T(8,128)(2,1)} %copy-done.2, bf16[]{:T(256)} %constant.11.clone.1), dimensions={0}, to_apply=%region_5.6 | reduce | flops 884736 | bytes 2949122 | tf_op jit(solution)/shard_map/reduce_sum | solution.py:89
  162.9 17.4 %shard_map.85 = bf16[8,288,128]{2,1,0:T(8,128)(2,1)S(1)} custom-call(bf16[8,288,128]{2,1,0:T(8,128)(2,1)S(1)} %reduce_sum.71.x_ref), custom_call_target="tpu_custom_call" | custom-call | tf_op jit(solution)/shard_map/pallas_call | solution.py:58
  180.5 0.8 copy.18
  181.2 0.6 reshape.76
  (29 shorter events, 0.5 us)
Async XLA Ops:
  0.6 60.2 %copy-start = (bf16[4096,256]{1,0:T(8,128)(2,1)S(1)}, bf16[4096,256]{1,0:T(8,128)(2,1)}, u32[]{:S(2)}) copy-start(bf16[4096,256]{1,0:T(8,128)(2,1)} %param.7) | copy-start | bytes 6291460
  0.6 1.4 copy-start.5
  60.8 3.2 %copy-start.1 = (bf16[2,4,128,4096]{3,2,1,0:T(8,128)(2,1)}, bf16[2,4,128,4096]{3,2,1,0:T(8,128)(2,1)S(1)}, u32[]{:S(2)}) copy-start(bf16[2,4,128,4096]{3,2,1,0:T(8,128)(2,1)S(1)} %shard_map.78) | copy-start | bytes 25165828
  60.8 3.2 %copy-start.9 = (bf16[256,512]{1,0:T(8,128)(2,1)S(1)}, bf16[256,512]{1,0:T(8,128)(2,1)}, u32[]{:S(2)}) copy-start(bf16[256,512]{1,0:T(8,128)(2,1)} %param.8) | copy-start | bytes 786436
  64.0 1.0 copy-start.11
  67.8 1.4 copy-start.3
  72.0 1.2 copy-start.4
  73.3 15.0 %copy-start.6 = (s32[1,1,32,8]{2,3,1,0:T(8,128)S(1)}, s32[1,1,32,8]{2,3,1,0:T(8,128)}, u32[]{:S(2)}) copy-start(s32[1,1,32,8]{2,3,1,0:T(8,128)} %param.9) | copy-start | bytes 3076
  73.3 31.9 %copy-start.7 = (s32[1,1,32,8]{2,3,1,0:T(8,128)S(1)}, s32[1,1,32,8]{2,3,1,0:T(8,128)}, u32[]{:S(2)}) copy-start(s32[1,1,32,8]{2,3,1,0:T(8,128)} %param.11) | copy-start | bytes 3076
  73.3 32.0 %copy-start.8 = (s32[1,1,32]{2,1,0:T(1,128)S(1)}, s32[1,1,32]{2,1,0:T(1,128)}, u32[]{:S(2)}) copy-start(s32[1,1,32]{2,1,0:T(1,128)} %param.10) | copy-start | bytes 388
  105.0 14.7 %copy-start.10 = (bf16[256,512]{1,0:T(8,128)(2,1)S(1)}, bf16[256,512]{1,0:T(8,128)(2,1)}, u32[]{:S(2)}) copy-start(bf16[256,512]{1,0:T(8,128)(2,1)} %param.8) | copy-start | bytes 786436
  105.3 14.5 %copy-start.12 = (f32[1024,256]{1,0:T(8,128)S(1)}, f32[1024,256]{1,0:T(8,128)}, u32[]{:S(2)}) copy-start(f32[1024,256]{1,0:T(8,128)} %copy-done.11) | copy-start | bytes 3145732
  159.4 1.4 copy-start.2

commit v8 on v7

--- a/solution.py
+++ b/solution.py
@@ -90,14 +90,90 @@
     return blocks
 
 
-def all_gather(x, axis, n, inner, first_id):
+def _gather_kernel(n_outer, n_inner, axis, x_ref, o_ref, got, send_sems, recv_sems):
+    me = lax.axis_index(axis)
+    ci = lax.rem(me, n_inner)
+    yo = lax.div(me, n_inner)
+
+    def device(c, y):
+        return {axis: y * n_inner + c}
+
+    def slot(c, y):
+        return c * n_outer + y
+
+    outer_peers = [lax.rem(yo + k, n_outer) for k in range(1, n_outer)]
+    inner_peers = [lax.rem(ci + j, n_inner) for j in range(1, n_inner)]
+    barrier = pltpu.get_barrier_semaphore()
+    for y in outer_peers:
+        pl.semaphore_signal(barrier, inc=1, device_id=device(ci, y), device_id_type=MESH)
+    for c in inner_peers:
+        pl.semaphore_signal(barrier, inc=1, device_id=device(c, yo), device_id_type=MESH)
+    pl.semaphore_wait(barrier, len(outer_peers) + len(inner_peers))
+
+    sends = []
+
+    def send(src, c, y, to):
+        copy = pltpu.make_async_remote_copy(
+            src_ref=src,
+            dst_ref=got.at[c, y],
+            send_sem=send_sems.at[len(sends)],
+            recv_sem=recv_sems.at[slot(c, y)],
+            device_id=to,
+            device_id_type=MESH,
+        )
+        copy.start()
+        sends.append(copy)
+
+    def receive(c, y):
+        pltpu.make_async_remote_copy(
+            src_ref=x_ref,
+            dst_ref=got.at[c, y],
+            send_sem=send_sems.at[0],
+            recv_sem=recv_sems.at[slot(c, y)],
+            device_id=device(c, y),
+            device_id_type=MESH,
+        ).wait_recv()
+
+    for y in outer_peers:
+        send(x_ref, ci, yo, device(ci, y))
+    for c in inner_peers:
+        send(x_ref, ci, yo, device(c, yo))
+    o_ref[ci, yo] = x_ref[...]
+    for k in range(1, n_outer):
+        y = lax.rem(yo + n_outer - k, n_outer)
+        receive(ci, y)
+        for c in inner_peers:
+            send(got.at[ci, y], ci, y, device(c, yo))
+        o_ref[ci, y] = got[ci, y]
+    for j in range(1, n_inner):
+        c = lax.rem(ci + n_inner - j, n_inner)
+        for k in range(n_outer):
+            y = lax.rem(yo + k, n_outer)
+            receive(c, y)
+            o_ref[c, y] = got[c, y]
+    for copy in sends:
+        copy.wait_send()
+
+
+def all_gather(x, axis, n, inner, collective_id):
     outer = n // inner
-    got = x[None]
-    if outer > 1:
-        got = exchange(x, axis, outer, first_id, gather=True, stride=inner)
-    got = got[None]
-    if inner > 1:
-        got = exchange(got[0], axis, inner, first_id + 1, gather=True)
+    shape = (inner, outer) + x.shape
+    got = pl.pallas_call(
+        functools.partial(_gather_kernel, outer, inner, axis),
+        out_shape=jax.ShapeDtypeStruct(shape, x.dtype),
+        in_specs=[pl.BlockSpec(memory_space=pltpu.VMEM)],
+        out_specs=pl.BlockSpec(memory_space=pltpu.VMEM),
+        scratch_shapes=[
+            pltpu.VMEM(shape, x.dtype),
+            pltpu.SemaphoreType.DMA((n,)),
+            pltpu.SemaphoreType.DMA((n,)),
+        ],
+        compiler_params=pltpu.CompilerParams(
+            collective_id=collective_id,
+            has_side_effects=True,
+            vmem_limit_bytes=min(3 * x.dtype.itemsize * math.prod(shape) + (8 << 20), 60 << 20),
+        ),
+    )(x)
     return got.reshape((n * x.shape[0],) + x.shape[1:])
 
 

time: 182 us -> 179 us (0.984)
  Pallas kernels: 153 us -> 150 us
    pallas_call x9 -> x5, Pallas kernels: 153 us -> 81.6 us  [exchange(): pl.pallas_call(functools.partial(_exchange_kernel, n, stride, axis, gathe...]
    pallas_call x0 -> x2, Pallas kernels: none -> 68.1 us  [all_gather(): pl.pallas_call(functools.partial(_gather_kernel, outer, inner, axis), out...]
where the time goes in v8:
time: 179 us
  Pallas kernels  150 us (84%)
  matrix products  10.5 us (6%)
  local copies, waits for them, and re-layouts  10.4 us (6%)
  other arithmetic  7.34 us (4%)
    pallas_call x5, Pallas kernels, exchange(): pl.pallas_call(functools.partial(_exchange_kernel, n, stride, axis, gathe...  81.6 us
    pallas_call x2, Pallas kernels, all_gather(): pl.pallas_call(functools.partial(_gather_kernel, outer, inner, axis), out...  68.1 us
    unnamed x29, local copies, waits for them, and re-layouts  7.69 us
    dot_general x1, matrix products, per_device(): lax.dot_general(grad_pre, shard_rows, (((0,), (0,)), ((), ())), preferred...  5.77 us
    reduce_sum x4, other arithmetic, reduce_scatter(): blocks = jnp.sum(got.astype(jnp.float32), axis=0)  5.11 us

profile of v8, /device:TPU:1, one launch (start us, length us, event | category | flops | bytes accessed | tf_op | source)
XLA Modules:
  0.0 178.9 jit_solution(11449420479167313554)
XLA Ops:
  0.7 1.4 copy-done.5
  2.0 55.3 %shard_map.77 = bf16[2,4,128,4096]{3,2,1,0:T(8,128)(2,1)S(1)} custom-call(bf16[128,4096]{1,0:T(8,128)(2,1)S(1)} %copy-done.5), custom_call_target="tpu_custom_call" | custom-call | tf_op jit(solution)/shard_map/pallas_call | solution.py:161
  57.4 2.3 %fusion.15 = f32[1024,256]{1,0:T(8,128)S(1)} fusion(bf16[1024,4096]{1,0:T(8,128)(2,1)S(1)} %bitcast.37, bf16[4096,256]{1,0:T(8,128)(2,1)S(1)} %copy-done), kind=kOutput, calls=%fused_computation.34 | convolution fusion | flops 2147483648 | bytes 11534336 | tf_op jit(solution)/shard_map/dot_general | solution.py:199
  59.7 0.8 copy-done.1
  60.6 0.5 fusion.14
  61.0 0.5 copy-done.11
  61.6 2.8 %shard_map.78 = f32[2,4,128,512]{3,2,1,0:T(8,128)S(1)} custom-call(f32[2,4,128,512]{3,2,1,0:T(8,128)S(1)} %bitcast.39), custom_call_target="tpu_custom_call" | custom-call | tf_op jit(solution)/shard_map/pallas_call | solution.py:58
  64.3 1.4 copy-done.3
  65.7 2.9 %reduce_sum.66.x_ref = f32[4,128,512]{2,1,0:T(8,128)} reduce(f32[2,4,128,512]{3,2,1,0:T(8,128)} %copy-done.3, f32[]{:T(128)} %constant.3.clone.1), dimensions={0}, to_apply=%region_0.1 | reduce | flops 262144 | bytes 3145732 | tf_op jit(solution)/shard_map/reduce_sum | solution.py:89
  68.6 1.2 copy-done.4
  69.8 15.0 %shard_map.79 = f32[4,128,512]{2,1,0:T(8,128)S(1)} custom-call(f32[4,128,512]{2,1,0:T(8,128)S(1)} %copy-done.4), custom_call_target="tpu_custom_call" | custom-call | tf_op jit(solution)/shard_map/pallas_call | solution.py:58
  84.8 0.1 reduce_sum.67
  84.9 0.1 multiply_reduce_fusion.1
  85.1 0.1 eq.15
  85.2 0.3 fusion.3.x_ref
  85.5 16.6 %shard_map.80 = bf16[32,8,512]{2,1,0:T(8,128)(2,1)S(1)} custom-call(bf16[32,8,512]{2,1,0:T(8,128)(2,1)S(1)} %fusion.3.x_ref), custom_call_target="tpu_custom_call" | custom-call | tf_op jit(solution)/shard_map/pallas_call | solution.py:58
  102.1 0.1 fusion.4
  102.4 0.5 multiply_reduce_fusion
  103.0 0.1 divide_convert_fusion.x_ref
  103.1 12.7 %shard_map.81 = bf16[2,4,128,512]{3,2,1,0:T(8,128)(2,1)S(1)} custom-call(bf16[128,512]{1,0:T(8,128)(2,1)S(1)} %divide_convert_fusion.x_ref), custom_call_target="tpu_custom_call" | custom-call | tf_op jit(solution)/shard_map/pallas_call | solution.py:161
  115.9 0.5 fusion.2
  116.4 5.8 %fusion = bf16[32,32,8,128]{3,2,1,0:T(8,128)(2,1)S(1)} fusion(bf16[1024,256]{1,0:T(8,128)(2,1)S(1)} %fusion.2, bf16[1024,4096]{1,0:T(8,128)(2,1)} %bitcast.38), kind=kOutput, calls=%fused_computation.3 | convolution fusion | flops 2148532224 | bytes 11010048 | tf_op jit(solution)/shard_map/dot_general | solution.py:240
  122.2 1.9 %copy.21 = bf16[32,32,8,128]{3,2,0,1:T(8,128)(2,1)} copy(bf16[32,32,8,128]{3,2,1,0:T(8,128)(2,1)S(1)} %fusion) | data formatting | bytes 4194304 | tf_op jit(solution)/shard_map/reshape | solution.py:250
  124.1 0.6 convolution_convert_fusion.1
  124.7 0.1 concatenate.9
  124.8 1.8 pad_maximum_fusion.x_ref
  126.6 29.4 %shard_map.82 = bf16[4,8,288,128]{3,2,1,0:T(8,128)(2,1)S(1)} custom-call(bf16[4,8,288,128]{3,2,1,0:T(8,128)(2,1)S(1)} %pad_maximum_fusion.x_ref), custom_call_target="tpu_custom_call" | custom-call | tf_op jit(solution)/shard_map/pallas_call | solution.py:58
  156.0 1.4 copy-done.2
  157.4 2.1 %reduce_sum.71.x_ref = bf16[8,288,128]{2,1,0:T(8,128)(2,1)S(1)} reduce(bf16[4,8,288,128]{3,2,1,0:T(8,128)(2,1)} %copy-done.2, bf16[]{:T(256)} %constant.11.clone.1), dimensions={0}, to_apply=%region_5.6 | reduce | flops 884736 | bytes 2949122 | tf_op jit(solution)/shard_map/reduce_sum | solution.py:89
  159.4 17.9 %shard_map.83 = bf16[8,288,128]{2,1,0:T(8,128)(2,1)S(1)} custom-call(bf16[8,288,128]{2,1,0:T(8,128)(2,1)S(1)} %reduce_sum.71.x_ref), custom_call_target="tpu_custom_call" | custom-call | tf_op jit(solution)/shard_map/pallas_call | solution.py:58
  177.5 0.8 copy.18
  178.2 0.6 reshape.76
  (27 shorter events, 0.4 us)
Async XLA Ops:
  0.6 56.7 %copy-start = (bf16[4096,256]{1,0:T(8,128)(2,1)S(1)}, bf16[4096,256]{1,0:T(8,128)(2,1)}, u32[]{:S(2)}) copy-start(bf16[4096,256]{1,0:T(8,128)(2,1)} %param.7) | copy-start | bytes 6291460
  0.6 1.4 copy-start.5
  57.4 3.2 %copy-start.1 = (bf16[2,4,128,4096]{3,2,1,0:T(8,128)(2,1)}, bf16[2,4,128,4096]{3,2,1,0:T(8,128)(2,1)S(1)}, u32[]{:S(2)}) copy-start(bf16[2,4,128,4096]{3,2,1,0:T(8,128)(2,1)S(1)} %shard_map.77) | copy-start | bytes 25165828
  57.4 3.2 %copy-start.9 = (bf16[256,512]{1,0:T(8,128)(2,1)S(1)}, bf16[256,512]{1,0:T(8,128)(2,1)}, u32[]{:S(2)}) copy-start(bf16[256,512]{1,0:T(8,128)(2,1)} %param.8) | copy-start | bytes 786436
  60.6 1.0 copy-start.11
  64.3 1.4 copy-start.3
  68.6 1.2 copy-start.4
  69.8 15.2 %copy-start.6 = (s32[1,1,32,8]{2,3,1,0:T(8,128)S(1)}, s32[1,1,32,8]{2,3,1,0:T(8,128)}, u32[]{:S(2)}) copy-start(s32[1,1,32,8]{2,3,1,0:T(8,128)} %param.9) | copy-start | bytes 3076
  69.8 32.5 %copy-start.7 = (s32[1,1,32,8]{2,3,1,0:T(8,128)S(1)}, s32[1,1,32,8]{2,3,1,0:T(8,128)}, u32[]{:S(2)}) copy-start(s32[1,1,32,8]{2,3,1,0:T(8,128)} %param.11) | copy-start | bytes 3076
  69.8 32.5 %copy-start.8 = (s32[1,1,32]{2,1,0:T(1,128)S(1)}, s32[1,1,32]{2,1,0:T(1,128)}, u32[]{:S(2)}) copy-start(s32[1,1,32]{2,1,0:T(1,128)} %param.10) | copy-start | bytes 388
  85.5 30.3 %copy-start.10 = (bf16[256,512]{1,0:T(8,128)(2,1)S(1)}, bf16[256,512]{1,0:T(8,128)(2,1)}, u32[]{:S(2)}) copy-start(bf16[256,512]{1,0:T(8,128)(2,1)} %param.8) | copy-start | bytes 786436
  102.4 13.5 %copy-start.12 = (f32[1024,256]{1,0:T(8,128)S(1)}, f32[1024,256]{1,0:T(8,128)}, u32[]{:S(2)}) copy-start(f32[1024,256]{1,0:T(8,128)} %copy-done.11) | copy-start | bytes 3145732
  156.0 1.4 copy-start.2

commit v9 on v8

--- a/solution.py
+++ b/solution.py
@@ -175,6 +175,127 @@
         ),
     )(x)
     return got.reshape((n * x.shape[0],) + x.shape[1:])
+
+
+def _reduce_kernel(n_o, n_i, chunks, axis, p_ref, o_ref, g1, b_ref, g2, s1, r1, s2, r2):
+    me = lax.axis_index(axis)
+    zi = lax.rem(me, n_i)
+    xo = lax.div(me, n_i)
+    zc = n_i // chunks
+
+    def device(x, z):
+        return {axis: x * n_i + z}
+
+    barrier = pltpu.get_barrier_semaphore()
+    for k in range(1, n_o):
+        pl.semaphore_signal(
+            barrier, inc=1, device_id=device(lax.rem(xo + k, n_o), zi), device_id_type=MESH
+        )
+    for k in range(1, n_i):
+        pl.semaphore_signal(
+            barrier, inc=1, device_id=device(xo, lax.rem(zi + k, n_i)), device_id_type=MESH
+        )
+    pl.semaphore_wait(barrier, n_o + n_i - 2)
+
+    def along_x(k, c, to, dst_x):
+        blocks = pl.ds(c * zc, zc)
+        return pltpu.make_async_remote_copy(
+            src_ref=p_ref.at[to, blocks],
+            dst_ref=g1.at[dst_x, blocks],
+            send_sem=s1.at[k, c],
+            recv_sem=r1.at[k, c],
+            device_id=device(to, zi),
+            device_id_type=MESH,
+        )
+
+    def along_z(k, z):
+        return pltpu.make_async_remote_copy(
+            src_ref=b_ref.at[z],
+            dst_ref=g2.at[zi],
+            send_sem=s2.at[k],
+            recv_sem=r2.at[k],
+            device_id=device(xo, z),
+            device_id_type=MESH,
+        )
+
+    first = []
+    for c in range(chunks):
+        for k in range(1, n_o):
+            copy = along_x(k, c, lax.rem(xo + k, n_o), xo)
+            copy.start()
+            first.append(copy)
+    sources = [lax.rem(xo + n_o - k, n_o) for k in range(1, n_o)]
+    for c in range(chunks):
+        for k in range(1, n_o):
+            pltpu.make_async_remote_copy(
+                src_ref=p_ref.at[sources[k - 1], pl.ds(c * zc, zc)],
+                dst_ref=g1.at[sources[k - 1], pl.ds(c * zc, zc)],
+                send_sem=s1.at[k, c],
+                recv_sem=r1.at[k, c],
+                device_id=device(sources[k - 1], zi),
+                device_id_type=MESH,
+            ).wait_recv()
+        for z in range(c * zc, (c + 1) * zc):
+            total = p_ref[xo, z].astype(jnp.float32)
+            for src in sources:
+                total = total + g1[src, z].astype(jnp.float32)
+            b_ref[z] = total.astype(b_ref.dtype)
+            offset = lax.rem(z - zi + n_i, n_i)
+
+            @pl.when(offset == 0)
+            def _():
+                o_ref[...] = total
+
+            @pl.when(offset != 0)
+            def _():
+                along_z(offset, z).start()
+
+    for k in range(1, n_i):
+        src = lax.rem(zi + n_i - k, n_i)
+        pltpu.make_async_remote_copy(
+            src_ref=b_ref.at[src],
+            dst_ref=g2.at[src],
+            send_sem=s2.at[k],
+            recv_sem=r2.at[k],
+            device_id=device(xo, src),
+            device_id_type=MESH,
+        ).wait_recv()
+        o_ref[...] = o_ref[...] + g2[src].astype(jnp.float32)
+    for copy in first:
+        copy.wait_send()
+    for z in range(n_i):
+        offset = lax.rem(z - zi + n_i, n_i)
+
+        @pl.when(offset != 0)
+        def _():
+            along_z(offset, z).wait_send()
+
+
+def reduce_scatter_2d(x, axis, inner):
+    n = x.shape[0]
+    outer = n // inner
+    chunks = next(c for c in (4, 2, 1) if inner % c == 0)
+    blocks = x.reshape((outer, inner) + x.shape[1:])
+    return pl.pallas_call(
+        functools.partial(_reduce_kernel, outer, inner, chunks, axis),
+        out_shape=jax.ShapeDtypeStruct(x.shape[1:], jnp.float32),
+        in_specs=[pl.BlockSpec(memory_space=pltpu.VMEM)],
+        out_specs=pl.BlockSpec(memory_space=pltpu.VMEM),
+        scratch_shapes=[
+            pltpu.VMEM(blocks.shape, x.dtype),
+            pltpu.VMEM((inner,) + x.shape[1:], x.dtype),
+            pltpu.VMEM((inner,) + x.shape[1:], x.dtype),
+            pltpu.SemaphoreType.DMA((outer, chunks)),
+            pltpu.SemaphoreType.DMA((outer, chunks)),
+            pltpu.SemaphoreType.DMA((inner,)),
+            pltpu.SemaphoreType.DMA((inner,)),
+        ],
+        compiler_params=pltpu.CompilerParams(
+            collective_id=8,
+            has_side_effects=True,
+            vmem_limit_bytes=min(4 * x.dtype.itemsize * x.size + (8 << 20), 60 << 20),
+        ),
+    )(blocks)
 
 
 def inner_size(devices):
@@ -252,7 +373,7 @@
         ],
         axis=1,
     )
-    summed = reduce_scatter(partial, "mass", mass_inner, False, 8)
+    summed = reduce_scatter_2d(partial, "mass", mass_inner)
     grad_in = summed[:hid].T
     grad_out_t = summed[hid:].reshape(out_rows, hid)
     return (grad_in, grad_out_t)

time: 179 us -> 171 us (0.955)
  Pallas kernels: 150 us -> 145 us
  other arithmetic: 7.34 us -> 5.18 us
    pallas_call x5 -> x3, Pallas kernels: 81.6 us -> 34.3 us  [exchange(): pl.pallas_call(functools.partial(_exchange_kernel, n, stride, axis, gathe...]
    pallas_call x0 -> x1, Pallas kernels: none -> 42.7 us  [reduce_scatter_2d(): pl.pallas_call(functools.partial(_reduce_kernel, outer, inner, chunks, ax...]
    reduce_sum x4 -> x2, other arithmetic: 5.11 us -> 2.96 us  [reduce_scatter(): blocks = jnp.sum(got.astype(jnp.float32), axis=0)]
    unnamed x29 -> x27, local copies, waits for them, and re-layouts: 7.69 us -> 6.29 us
where the time goes in v9:
time: 171 us
  Pallas kernels  145 us (85%)
  matrix products  10.5 us (6%)
  local copies, waits for them, and re-layouts  9.03 us (5%)
  other arithmetic  5.18 us (3%)
    pallas_call x2, Pallas kernels, all_gather(): pl.pallas_call(functools.partial(_gather_kernel, outer, inner, axis), out...  68.1 us
    pallas_call x1, Pallas kernels, reduce_scatter_2d(): pl.pallas_call(functools.partial(_reduce_kernel, outer, inner, chunks, ax...  42.7 us
    pallas_call x3, Pallas kernels, exchange(): pl.pallas_call(functools.partial(_exchange_kernel, n, stride, axis, gathe...  34.3 us
    unnamed x27, local copies, waits for them, and re-layouts  6.29 us
    dot_general x1, matrix products, per_device(): lax.dot_general(grad_pre, shard_rows, (((0,), (0,)), ((), ())), preferred...  5.77 us

profile of v9, /device:TPU:1, one launch (start us, length us, event | category | flops | bytes accessed | tf_op | source)
XLA Modules:
  0.0 170.7 jit_solution(15363585014591431208)
XLA Ops:
  0.7 1.4 copy-done.4
  2.0 55.3 %shard_map.77 = bf16[2,4,128,4096]{3,2,1,0:T(8,128)(2,1)S(1)} custom-call(bf16[128,4096]{1,0:T(8,128)(2,1)S(1)} %copy-done.4), custom_call_target="tpu_custom_call" | custom-call | tf_op jit(solution)/shard_map/pallas_call | solution.py:161
  57.4 2.3 %fusion.15 = f32[1024,256]{1,0:T(8,128)S(1)} fusion(bf16[1024,4096]{1,0:T(8,128)(2,1)S(1)} %bitcast.37, bf16[4096,256]{1,0:T(8,128)(2,1)S(1)} %copy-done), kind=kOutput, calls=%fused_computation.33 | convolution fusion | flops 2147483648 | bytes 11534336 | tf_op jit(solution)/shard_map/dot_general | solution.py:320
  59.7 0.8 copy-done.1
  60.6 0.5 fusion.14
  61.0 0.5 copy-done.10
  61.6 2.8 %shard_map.78 = f32[2,4,128,512]{3,2,1,0:T(8,128)S(1)} custom-call(f32[2,4,128,512]{3,2,1,0:T(8,128)S(1)} %bitcast.39), custom_call_target="tpu_custom_call" | custom-call | tf_op jit(solution)/shard_map/pallas_call | solution.py:58
  64.3 1.4 copy-done.2
  65.7 2.9 %reduce_sum.45.x_ref = f32[4,128,512]{2,1,0:T(8,128)} reduce(f32[2,4,128,512]{3,2,1,0:T(8,128)} %copy-done.2, f32[]{:T(128)} %constant.1.clone.1), dimensions={0}, to_apply=%region_0.1 | reduce | flops 262144 | bytes 3145732 | tf_op jit(solution)/shard_map/reduce_sum | solution.py:89
  68.6 1.2 copy-done.3
  69.8 15.0 %shard_map.79 = f32[4,128,512]{2,1,0:T(8,128)S(1)} custom-call(f32[4,128,512]{2,1,0:T(8,128)S(1)} %copy-done.3), custom_call_target="tpu_custom_call" | custom-call | tf_op jit(solution)/shard_map/pallas_call | solution.py:58
  84.8 0.1 reduce_sum.46
  84.9 0.1 multiply_reduce_fusion.1
  85.1 0.1 copy.15
  85.1 0.1 eq.15
  85.2 0.3 fusion.3.x_ref
  85.5 16.6 %shard_map.80 = bf16[32,8,512]{2,1,0:T(8,128)(2,1)S(1)} custom-call(bf16[32,8,512]{2,1,0:T(8,128)(2,1)S(1)} %fusion.3.x_ref), custom_call_target="tpu_custom_call" | custom-call | tf_op jit(solution)/shard_map/pallas_call | solution.py:58
  102.1 0.1 fusion.4
  102.3 0.1 copy.16
  102.4 0.1 fusion.13
  102.4 0.5 multiply_reduce_fusion
  103.0 0.1 divide_convert_fusion.x_ref
  103.1 12.7 %shard_map.81 = bf16[2,4,128,512]{3,2,1,0:T(8,128)(2,1)S(1)} custom-call(bf16[128,512]{1,0:T(8,128)(2,1)S(1)} %divide_convert_fusion.x_ref), custom_call_target="tpu_custom_call" | custom-call | tf_op jit(solution)/shard_map/pallas_call | solution.py:161
  115.9 0.5 fusion.2
  116.4 5.8 %fusion = bf16[32,32,8,128]{3,2,1,0:T(8,128)(2,1)S(1)} fusion(bf16[1024,256]{1,0:T(8,128)(2,1)S(1)} %fusion.2, bf16[1024,4096]{1,0:T(8,128)(2,1)} %bitcast.38), kind=kOutput, calls=%fused_computation.3 | convolution fusion | flops 2148532224 | bytes 11010048 | tf_op jit(solution)/shard_map/dot_general | solution.py:361
  122.2 1.9 %copy.21 = bf16[32,32,8,128]{3,2,0,1:T(8,128)(2,1)} copy(bf16[32,32,8,128]{3,2,1,0:T(8,128)(2,1)S(1)} %fusion) | data formatting | bytes 4194304 | tf_op jit(solution)/shard_map/reshape | solution.py:371
  124.1 0.6 convolution_convert_fusion.1
  124.7 0.1 concatenate.9
  124.8 1.8 %pad_maximum_fusion.p_ref = bf16[4,8,288,128]{3,2,1,0:T(8,128)(2,1)S(1)} fusion(bf16[4,8,32,128]{3,2,1,0:T(8,128)(2,1)S(1)} %concatenate.9, bf16[4,8,256,128]{3,2,1,0:T(8,128)(2,1)} %bitcast.42), kind=kLoop, calls=%fused_computation.1 | loop fusion | flops 4718592 | bytes 4718592 | tf_op jit(solution)/shard_map/concatenate | solution.py:369
  126.6 42.7 %shard_map.82 = f32[288,128]{1,0:T(8,128)S(1)} custom-call(bf16[4,8,288,128]{3,2,1,0:T(8,128)(2,1)S(1)} %pad_maximum_fusion.p_ref), custom_call_target="tpu_custom_call" | custom-call | tf_op jit(solution)/shard_map/pallas_call | solution.py:279
  169.3 0.8 copy.18
  170.1 0.6 reshape.76
  (22 shorter events, 0.1 us)
Async XLA Ops:
  0.6 56.7 %copy-start = (bf16[4096,256]{1,0:T(8,128)(2,1)S(1)}, bf16[4096,256]{1,0:T(8,128)(2,1)}, u32[]{:S(2)}) copy-start(bf16[4096,256]{1,0:T(8,128)(2,1)} %param.7) | copy-start | bytes 6291460
  0.6 1.4 copy-start.4
  57.4 3.2 %copy-start.1 = (bf16[2,4,128,4096]{3,2,1,0:T(8,128)(2,1)}, bf16[2,4,128,4096]{3,2,1,0:T(8,128)(2,1)S(1)}, u32[]{:S(2)}) copy-start(bf16[2,4,128,4096]{3,2,1,0:T(8,128)(2,1)S(1)} %shard_map.77) | copy-start | bytes 25165828
  57.4 3.2 %copy-start.8 = (bf16[256,512]{1,0:T(8,128)(2,1)S(1)}, bf16[256,512]{1,0:T(8,128)(2,1)}, u32[]{:S(2)}) copy-start(bf16[256,512]{1,0:T(8,128)(2,1)} %param.8) | copy-start | bytes 786436
  60.6 1.0 copy-start.10
  64.3 1.4 copy-start.2
  68.6 1.2 copy-start.3
  69.8 15.2 %copy-start.5 = (s32[1,1,32,8]{2,3,1,0:T(8,128)S(1)}, s32[1,1,32,8]{2,3,1,0:T(8,128)}, u32[]{:S(2)}) copy-start(s32[1,1,32,8]{2,3,1,0:T(8,128)} %param.9) | copy-start | bytes 3076
  69.8 32.5 %copy-start.6 = (s32[1,1,32,8]{2,3,1,0:T(8,128)S(1)}, s32[1,1,32,8]{2,3,1,0:T(8,128)}, u32[]{:S(2)}) copy-start(s32[1,1,32,8]{2,3,1,0:T(8,128)} %param.11) | copy-start | bytes 3076
  69.8 32.5 %copy-start.7 = (s32[1,1,32]{2,1,0:T(1,128)S(1)}, s32[1,1,32]{2,1,0:T(1,128)}, u32[]{:S(2)}) copy-start(s32[1,1,32]{2,1,0:T(1,128)} %param.10) | copy-start | bytes 388
  85.5 30.3 %copy-start.9 = (bf16[256,512]{1,0:T(8,128)(2,1)S(1)}, bf16[256,512]{1,0:T(8,128)(2,1)}, u32[]{:S(2)}) copy-start(bf16[256,512]{1,0:T(8,128)(2,1)} %param.8) | copy-start | bytes 786436
  102.4 13.5 %copy-start.11 = (f32[1024,256]{1,0:T(8,128)S(1)}, f32[1024,256]{1,0:T(8,128)}, u32[]{:S(2)}) copy-start(f32[1024,256]{1,0:T(8,128)} %copy-done.10) | copy-start | bytes 3145732

commit v10 on v9

--- a/solution.py
+++ b/solution.py
@@ -73,7 +73,7 @@
     )(x)
 
 
-def reduce_scatter(x, axis, inner, first_inner, first_id):
+def reduce_scatter(x, axis, inner, first_inner, first_id, wire=(None, None)):
     outer = x.shape[0] // inner
     if first_inner:
         blocks = x.reshape((inner, outer) + x.shape[1:])
@@ -85,7 +85,7 @@
         if size == 1:
             blocks = blocks[0].astype(jnp.float32)
             continue
-        got = exchange(blocks.astype(x.dtype), axis, size, first_id + number, stride=stride)
+        got = exchange(blocks.astype(wire[number] or x.dtype), axis, size, first_id + number, stride=stride)
         blocks = jnp.sum(got.astype(jnp.float32), axis=0)
     return blocks
 
@@ -321,7 +321,8 @@
     hidden = jax.nn.silu(pre).astype(jnp.bfloat16)
     embed_part = jnp.dot(hidden, w_out, preferred_element_type=jnp.float32)
     embed = reduce_scatter(
-        embed_part.reshape(n_sub, own_rows, embed_part.shape[1]), "sub", sub_inner, True, 4
+        embed_part.reshape(n_sub, own_rows, embed_part.shape[1]), "sub", sub_inner, True, 4,
+        wire=(jnp.float32, jnp.bfloat16),
     )
     norm = jnp.sqrt(jnp.sum(embed * embed, axis=-1, keepdims=True) + 1e-06)
     unit = embed / norm

time: 171 us -> 163 us (0.953)
  Pallas kernels: 145 us -> 140 us
    pallas_call x3, Pallas kernels: 34.3 us -> 28.9 us  [exchange(): pl.pallas_call(functools.partial(_exchange_kernel, n, stride, axis, gathe...]
    unnamed x27 -> x23, local copies, waits for them, and re-layouts: 6.29 us -> 5.05 us
where the time goes in v10:
time: 163 us
  Pallas kernels  140 us (86%)
  matrix products  10.5 us (6%)
  local copies, waits for them, and re-layouts  7.8 us (5%)
  other arithmetic  4.17 us (3%)
    pallas_call x2, Pallas kernels, all_gather(): pl.pallas_call(functools.partial(_gather_kernel, outer, inner, axis), out...  68.1 us
    pallas_call x1, Pallas kernels, reduce_scatter_2d(): pl.pallas_call(functools.partial(_reduce_kernel, outer, inner, chunks, ax...  42.7 us
    pallas_call x3, Pallas kernels, exchange(): pl.pallas_call(functools.partial(_exchange_kernel, n, stride, axis, gathe...  28.9 us
    dot_general x1, matrix products, per_device(): lax.dot_general(grad_pre, shard_rows, (((0,), (0,)), ((), ())), preferred...  5.77 us
    unnamed x23, local copies, waits for them, and re-layouts  5.05 us

profile of v10, /device:TPU:1, one launch (start us, length us, event | category | flops | bytes accessed | tf_op | source)
XLA Modules:
  0.0 163.0 jit_solution(8177905154462377266)
XLA Ops:
  0.6 0.0 copy-start
  0.7 1.4 copy-done.3
  2.0 55.3 %shard_map.77 = bf16[2,4,128,4096]{3,2,1,0:T(8,128)(2,1)S(1)} custom-call(bf16[128,4096]{1,0:T(8,128)(2,1)S(1)} %copy-done.3), custom_call_target="tpu_custom_call" | custom-call | tf_op jit(solution)/shard_map/pallas_call | solution.py:161
  57.4 2.3 %fusion.15 = f32[1024,256]{1,0:T(8,128)S(1)} fusion(bf16[1024,4096]{1,0:T(8,128)(2,1)S(1)} %bitcast.37, bf16[4096,256]{1,0:T(8,128)(2,1)S(1)} %copy-done), kind=kOutput, calls=%fused_computation.34 | convolution fusion | flops 2147483648 | bytes 11534336 | tf_op jit(solution)/shard_map/dot_general | solution.py:320
  59.7 0.8 copy-done.1
  60.6 0.5 fusion.14
  61.0 0.5 copy-done.8
  61.6 2.8 %shard_map.78 = f32[2,4,128,512]{3,2,1,0:T(8,128)S(1)} custom-call(f32[2,4,128,512]{3,2,1,0:T(8,128)S(1)} %bitcast.39), custom_call_target="tpu_custom_call" | custom-call | tf_op jit(solution)/shard_map/pallas_call | solution.py:58
  64.3 1.4 copy-done.2
  65.7 1.9 %reduce_sum.45.x_ref = bf16[4,128,512]{2,1,0:T(8,128)(2,1)S(1)} reduce(f32[2,4,128,512]{3,2,1,0:T(8,128)} %copy-done.2, f32[]{:T(128)} %constant.1.clone.1), dimensions={0}, to_apply=%region_0.1 | reduce | flops 262144 | bytes 2621444 | tf_op jit(solution)/shard_map/reduce_sum | solution.py:89
  67.6 9.5 %shard_map.79 = bf16[4,128,512]{2,1,0:T(8,128)(2,1)S(1)} custom-call(bf16[4,128,512]{2,1,0:T(8,128)(2,1)S(1)} %reduce_sum.45.x_ref), custom_call_target="tpu_custom_call" | custom-call | tf_op jit(solution)/shard_map/pallas_call | solution.py:58
  77.2 0.1 convert_reduce_fusion
  77.2 0.1 multiply_reduce_fusion.1
  77.4 0.1 copy.15
  77.5 0.1 eq.15
  77.5 0.3 fusion.3.x_ref
  77.8 16.6 %shard_map.80 = bf16[32,8,512]{2,1,0:T(8,128)(2,1)S(1)} custom-call(bf16[32,8,512]{2,1,0:T(8,128)(2,1)S(1)} %fusion.3.x_ref), custom_call_target="tpu_custom_call" | custom-call | tf_op jit(solution)/shard_map/pallas_call | solution.py:58
  94.4 0.1 fusion.4
  94.6 0.1 copy.16
  94.7 0.1 fusion.13
  94.8 0.5 multiply_reduce_fusion
  95.3 0.1 divide_convert_fusion.x_ref
  95.4 12.7 %shard_map.81 = bf16[2,4,128,512]{3,2,1,0:T(8,128)(2,1)S(1)} custom-call(bf16[128,512]{1,0:T(8,128)(2,1)S(1)} %divide_convert_fusion.x_ref), custom_call_target="tpu_custom_call" | custom-call | tf_op jit(solution)/shard_map/pallas_call | solution.py:161
  108.2 0.5 fusion.2
  108.7 5.8 %fusion = bf16[32,32,8,128]{3,2,1,0:T(8,128)(2,1)S(1)} fusion(bf16[1024,256]{1,0:T(8,128)(2,1)S(1)} %fusion.2, bf16[1024,4096]{1,0:T(8,128)(2,1)} %bitcast.38), kind=kOutput, calls=%fused_computation.3 | convolution fusion | flops 2148532224 | bytes 11010048 | tf_op jit(solution)/shard_map/dot_general | solution.py:362
  114.5 1.9 %copy.21 = bf16[32,32,8,128]{3,2,0,1:T(8,128)(2,1)} copy(bf16[32,32,8,128]{3,2,1,0:T(8,128)(2,1)S(1)} %fusion) | data formatting | bytes 4194304 | tf_op jit(solution)/shard_map/reshape | solution.py:372
  116.4 0.6 convolution_convert_fusion.1
  117.0 0.1 concatenate.9
  117.1 1.8 %pad_maximum_fusion.p_ref = bf16[4,8,288,128]{3,2,1,0:T(8,128)(2,1)S(1)} fusion(bf16[4,8,32,128]{3,2,1,0:T(8,128)(2,1)S(1)} %concatenate.9, bf16[4,8,256,128]{3,2,1,0:T(8,128)(2,1)} %bitcast.42), kind=kLoop, calls=%fused_computation.1 | loop fusion | flops 4718592 | bytes 4718592 | tf_op jit(solution)/shard_map/concatenate | solution.py:370
  118.9 42.7 %shard_map.82 = f32[288,128]{1,0:T(8,128)S(1)} custom-call(bf16[4,8,288,128]{3,2,1,0:T(8,128)(2,1)S(1)} %pad_maximum_fusion.p_ref), custom_call_target="tpu_custom_call" | custom-call | tf_op jit(solution)/shard_map/pallas_call | solution.py:279
  161.6 0.8 copy.18
  162.4 0.6 reshape.76
  (18 shorter events, 0.1 us)
Async XLA Ops:
  0.6 56.7 %copy-start = (bf16[4096,256]{1,0:T(8,128)(2,1)S(1)}, bf16[4096,256]{1,0:T(8,128)(2,1)}, u32[]{:S(2)}) copy-start(bf16[4096,256]{1,0:T(8,128)(2,1)} %param.7) | copy-start | bytes 6291460
  0.6 1.4 copy-start.3
  57.4 3.2 %copy-start.1 = (bf16[2,4,128,4096]{3,2,1,0:T(8,128)(2,1)}, bf16[2,4,128,4096]{3,2,1,0:T(8,128)(2,1)S(1)}, u32[]{:S(2)}) copy-start(bf16[2,4,128,4096]{3,2,1,0:T(8,128)(2,1)S(1)} %shard_map.77) | copy-start | bytes 25165828
  57.4 3.2 %copy-start.7 = (bf16[256,512]{1,0:T(8,128)(2,1)S(1)}, bf16[256,512]{1,0:T(8,128)(2,1)}, u32[]{:S(2)}) copy-start(bf16[256,512]{1,0:T(8,128)(2,1)} %param.8) | copy-start | bytes 786436
  60.6 1.0 copy-start.8
  64.3 1.4 copy-start.2
  65.7 11.6 %copy-start.4 = (s32[1,1,32,8]{2,3,1,0:T(8,128)S(1)}, s32[1,1,32,8]{2,3,1,0:T(8,128)}, u32[]{:S(2)}) copy-start(s32[1,1,32,8]{2,3,1,0:T(8,128)} %param.9) | copy-start | bytes 3076
  67.6 27.0 %copy-start.5 = (s32[1,1,32,8]{2,3,1,0:T(8,128)S(1)}, s32[1,1,32,8]{2,3,1,0:T(8,128)}, u32[]{:S(2)}) copy-start(s32[1,1,32,8]{2,3,1,0:T(8,128)} %param.11) | copy-start | bytes 3076
  67.6 27.1 %copy-start.6 = (s32[1,1,32]{2,1,0:T(1,128)S(1)}, s32[1,1,32]{2,1,0:T(1,128)}, u32[]{:S(2)}) copy-start(s32[1,1,32]{2,1,0:T(1,128)} %param.10) | copy-start | bytes 388
  94.7 13.5 %copy-start.9 = (f32[1024,256]{1,0:T(8,128)S(1)}, f32[1024,256]{1,0:T(8,128)}, u32[]{:S(2)}) copy-start(f32[1024,256]{1,0:T(8,128)} %copy-done.8) | copy-start | bytes 3145732

commit v11 on v9

--- a/solution.py
+++ b/solution.py
@@ -298,6 +298,92 @@
     )(blocks)
 
 
+def _relay_kernel(n_o, n_i, axis, x_ref, o_ref, g1, g2, s1, r1, s2, r2, own):
+    me = lax.axis_index(axis)
+    zi = lax.rem(me, n_i)
+    xo = lax.div(me, n_i)
+
+    def device(x, z):
+        return {axis: x * n_i + z}
+
+    barrier = pltpu.get_barrier_semaphore()
+    for k in range(1, n_o):
+        pl.semaphore_signal(
+            barrier, inc=1, device_id=device(lax.rem(xo + k, n_o), zi), device_id_type=MESH
+        )
+    for k in range(1, n_i):
+        pl.semaphore_signal(
+            barrier, inc=1, device_id=device(xo, lax.rem(zi + k, n_i)), device_id_type=MESH
+        )
+    pl.semaphore_wait(barrier, n_o + n_i - 2)
+
+    def along_x(k, x, src_x):
+        return pltpu.make_async_remote_copy(
+            src_ref=x_ref.at[x],
+            dst_ref=g1.at[:, src_x],
+            send_sem=s1.at[k],
+            recv_sem=r1.at[k],
+            device_id=device(x, zi),
+            device_id_type=MESH,
+        )
+
+    def along_z(k, z, src_z):
+        return pltpu.make_async_remote_copy(
+            src_ref=g1.at[z],
+            dst_ref=g2.at[src_z],
+            send_sem=s2.at[k],
+            recv_sem=r2.at[k],
+            device_id=device(xo, z),
+            device_id_type=MESH,
+        )
+
+    first = [along_x(k, lax.rem(xo + k, n_o), xo) for k in range(1, n_o)]
+    for copy in first:
+        copy.start()
+    local = pltpu.make_async_copy(x_ref.at[xo], g1.at[:, xo], own)
+    local.start()
+    local.wait()
+    for k in range(1, n_o):
+        src = lax.rem(xo + n_o - k, n_o)
+        along_x(k, src, src).wait_recv()
+    second = [along_z(k, lax.rem(zi + k, n_i), zi) for k in range(1, n_i)]
+    for copy in second:
+        copy.start()
+    for x in range(n_o):
+        o_ref[x, zi] = g1[zi, x]
+    for k in range(1, n_i):
+        src = lax.rem(zi + n_i - k, n_i)
+        along_z(k, src, src).wait_recv()
+        for x in range(n_o):
+            o_ref[x, src] = g2[src, x]
+    for copy in first + second:
+        copy.wait_send()
+
+
+def all_to_all_2d(x, axis, inner, collective_id):
+    n = x.shape[0]
+    outer = n // inner
+    blocks = x.reshape((outer, inner) + x.shape[1:])
+    turned = (inner, outer) + x.shape[1:]
+    got = pl.pallas_call(
+        functools.partial(_relay_kernel, outer, inner, axis),
+        out_shape=jax.ShapeDtypeStruct(blocks.shape, x.dtype),
+        in_specs=[pl.BlockSpec(memory_space=pltpu.VMEM)],
+        out_specs=pl.BlockSpec(memory_space=pltpu.VMEM),
+        scratch_shapes=[
+            pltpu.VMEM(turned, x.dtype),
+            pltpu.VMEM(turned, x.dtype),
+            pltpu.SemaphoreType.DMA((outer,)),
+            pltpu.SemaphoreType.DMA((outer,)),
+            pltpu.SemaphoreType.DMA((inner,)),
+            pltpu.SemaphoreType.DMA((inner,)),
+            pltpu.SemaphoreType.DMA(()),
+        ],
+        compiler_params=pltpu.CompilerParams(collective_id=collective_id, has_side_effects=True),
+    )(blocks)
+    return got.reshape(x.shape)
+
+
 def inner_size(devices):
     coords = [tuple(getattr(d, "coords", ())) for d in devices]
     if len(coords) < 2 or not coords[0]:
@@ -332,7 +418,7 @@
         selector.astype(jnp.bfloat16), unit_b, preferred_element_type=jnp.float32
     ).astype(jnp.bfloat16)
     outgoing = mine.reshape(peers, slots, mine.shape[1])
-    incoming = exchange(outgoing, "mass", peers, 1)
+    incoming = all_to_all_2d(outgoing, "mass", mass_inner, 1)
     theirs = incoming.astype(jnp.float32)
     sim = jnp.sum(outgoing.astype(jnp.float32) * theirs, axis=-1)
     valid = jnp.arange(slots, dtype=jnp.int32)[None, :] < pair_counts.reshape(peers)[:, None]

time: 171 us -> 177 us (1.035)
  Pallas kernels: 145 us -> 148 us
  matrix products: 10.5 us -> 12.3 us
    pallas_call x0 -> x1, Pallas kernels: none -> 19 us  [all_to_all_2d(): pl.pallas_call(functools.partial(_relay_kernel, outer, inner, axis), out_...]
    pallas_call x3 -> x2, Pallas kernels: 34.3 us -> 17.8 us  [exchange(): pl.pallas_call(functools.partial(_exchange_kernel, n, stride, axis, gathe...]
    unnamed x27 -> x26, local copies, waits for them, and re-layouts: 6.29 us -> 6.2 us
where the time goes in v11:
time: 177 us; the launch traced here: 176 us
  Pallas kernels  148 us (84%)
  matrix products  12.3 us (7%)
  local copies, waits for them, and re-layouts  9.21 us (5%)
  other arithmetic  6.23 us (4%)
    pallas_call x2, Pallas kernels, all_gather(): pl.pallas_call(functools.partial(_gather_kernel, outer, inner, axis), out...  69.7 us
    pallas_call x1, Pallas kernels, reduce_scatter_2d(): pl.pallas_call(functools.partial(_reduce_kernel, outer, inner, chunks, ax...  41.4 us
    pallas_call x1, Pallas kernels, all_to_all_2d(): pl.pallas_call(functools.partial(_relay_kernel, outer, inner, axis), out_...  19 us
    pallas_call x2, Pallas kernels, exchange(): pl.pallas_call(functools.partial(_exchange_kernel, n, stride, axis, gathe...  17.8 us
    unnamed x26, local copies, waits for them, and re-layouts  6.2 us
    dot_general x1, matrix products, per_device(): lax.dot_general(grad_pre, shard_rows, (((0,), (0,)), ((), ())), preferred...  5.77 us

profile of v11, /device:TPU:1, one launch (start us, length us, event | category | flops | bytes accessed | tf_op | source)
XLA Modules:
  0.0 176.4 jit_solution(843721456679697793)
XLA Ops:
  0.7 1.4 copy-done.4
  2.0 55.3 %shard_map.77 = bf16[2,4,128,4096]{3,2,1,0:T(8,128)(2,1)S(1)} custom-call(bf16[128,4096]{1,0:T(8,128)(2,1)S(1)} %copy-done.4), custom_call_target="tpu_custom_call" | custom-call | tf_op jit(solution)/shard_map/pallas_call | solution.py:161
  57.4 2.3 %fusion.10 = f32[1024,256]{1,0:T(8,128)S(1)} fusion(bf16[1024,4096]{1,0:T(8,128)(2,1)S(1)} %bitcast.30, bf16[4096,256]{1,0:T(8,128)(2,1)S(1)} %copy-done), kind=kOutput, calls=%fused_computation.29 | convolution fusion | flops 2147483648 | bytes 11534336 | tf_op jit(solution)/shard_map/dot_general | solution.py:406
  59.7 0.8 copy-done.1
  60.6 0.5 fusion.9
  61.0 0.5 copy-done.10
  61.6 2.8 %shard_map.78 = f32[2,4,128,512]{3,2,1,0:T(8,128)S(1)} custom-call(f32[2,4,128,512]{3,2,1,0:T(8,128)S(1)} %bitcast.32), custom_call_target="tpu_custom_call" | custom-call | tf_op jit(solution)/shard_map/pallas_call | solution.py:58
  64.3 1.4 copy-done.2
  65.7 2.9 %reduce_sum.45.x_ref = f32[4,128,512]{2,1,0:T(8,128)} reduce(f32[2,4,128,512]{3,2,1,0:T(8,128)} %copy-done.2, f32[]{:T(128)} %constant.1.clone.1), dimensions={0}, to_apply=%region_0.1 | reduce | flops 262144 | bytes 3145732 | tf_op jit(solution)/shard_map/reduce_sum | solution.py:89
  68.6 1.2 copy-done.3
  69.8 15.0 %shard_map.79 = f32[4,128,512]{2,1,0:T(8,128)S(1)} custom-call(f32[4,128,512]{2,1,0:T(8,128)S(1)} %copy-done.3), custom_call_target="tpu_custom_call" | custom-call | tf_op jit(solution)/shard_map/pallas_call | solution.py:58
  84.8 0.1 reduce_sum.46
  84.9 0.1 multiply_reduce_fusion.1
  85.1 0.1 eq.15
  85.2 1.0 convolution_convert_fusion.2
  86.3 19.0 %shard_map.80 = bf16[4,8,8,512]{3,2,1,0:T(8,128)(2,1)} custom-call(bf16[4,8,8,512]{3,2,1,0:T(8,128)(2,1)} %bitcast.37), custom_call_target="tpu_custom_call" | custom-call | tf_op jit(solution)/shard_map/pallas_call | solution.py:368
  105.3 1.2 fusion.3
  106.5 0.1 copy.11
  106.6 0.1 convert_element_type.52
  106.7 0.1 lt.26
  106.9 1.6 multiply_reduce_fusion
  108.4 0.1 divide_convert_fusion.x_ref
  108.6 14.3 %shard_map.81 = bf16[2,4,128,512]{3,2,1,0:T(8,128)(2,1)S(1)} custom-call(bf16[128,512]{1,0:T(8,128)(2,1)S(1)} %divide_convert_fusion.x_ref), custom_call_target="tpu_custom_call" | custom-call | tf_op jit(solution)/shard_map/pallas_call | solution.py:161
  122.9 0.5 fusion.2
  123.5 5.8 %fusion = bf16[32,32,8,128]{3,2,1,0:T(8,128)(2,1)S(1)} fusion(bf16[1024,256]{1,0:T(8,128)(2,1)S(1)} %fusion.2, bf16[1024,4096]{1,0:T(8,128)(2,1)} %bitcast.31), kind=kOutput, calls=%fused_computation.3 | convolution fusion | flops 2148532224 | bytes 11010048 | tf_op jit(solution)/shard_map/dot_general | solution.py:447
  129.2 1.9 %copy.16 = bf16[32,32,8,128]{3,2,0,1:T(8,128)(2,1)} copy(bf16[32,32,8,128]{3,2,1,0:T(8,128)(2,1)S(1)} %fusion) | data formatting | bytes 4194304 | tf_op jit(solution)/shard_map/reshape | solution.py:457
  131.2 0.6 convolution_convert_fusion.1
  131.8 0.1 concatenate.9
  131.8 1.8 %pad_maximum_fusion.p_ref = bf16[4,8,288,128]{3,2,1,0:T(8,128)(2,1)S(1)} fusion(bf16[4,8,32,128]{3,2,1,0:T(8,128)(2,1)S(1)} %concatenate.9, bf16[4,8,256,128]{3,2,1,0:T(8,128)(2,1)} %bitcast.35), kind=kLoop, calls=%fused_computation.1 | loop fusion | flops 4718592 | bytes 4718592 | tf_op jit(solution)/shard_map/concatenate | solution.py:455
  133.6 41.4 %shard_map.82 = f32[288,128]{1,0:T(8,128)S(1)} custom-call(bf16[4,8,288,128]{3,2,1,0:T(8,128)(2,1)S(1)} %pad_maximum_fusion.p_ref), custom_call_target="tpu_custom_call" | custom-call | tf_op jit(solution)/shard_map/pallas_call | solution.py:279
  175.1 0.8 copy.13
  175.8 0.6 reshape.76
  (26 shorter events, 0.2 us)
Async XLA Ops:
  0.6 56.7 %copy-start = (bf16[4096,256]{1,0:T(8,128)(2,1)S(1)}, bf16[4096,256]{1,0:T(8,128)(2,1)}, u32[]{:S(2)}) copy-start(bf16[4096,256]{1,0:T(8,128)(2,1)} %param.7) | copy-start | bytes 6291460
  0.6 1.4 copy-start.4
  57.4 3.2 %copy-start.1 = (bf16[2,4,128,4096]{3,2,1,0:T(8,128)(2,1)}, bf16[2,4,128,4096]{3,2,1,0:T(8,128)(2,1)S(1)}, u32[]{:S(2)}) copy-start(bf16[2,4,128,4096]{3,2,1,0:T(8,128)(2,1)S(1)} %shard_map.77) | copy-start | bytes 25165828
  57.4 3.2 %copy-start.8 = (bf16[256,512]{1,0:T(8,128)(2,1)S(1)}, bf16[256,512]{1,0:T(8,128)(2,1)}, u32[]{:S(2)}) copy-start(bf16[256,512]{1,0:T(8,128)(2,1)} %param.8) | copy-start | bytes 786436
  60.6 1.0 copy-start.10
  64.3 1.4 copy-start.2
  68.6 1.2 copy-start.3
  69.8 15.2 %copy-start.5 = (s32[1,1,32,8]{2,3,1,0:T(8,128)S(1)}, s32[1,1,32,8]{2,3,1,0:T(8,128)}, u32[]{:S(2)}) copy-start(s32[1,1,32,8]{2,3,1,0:T(8,128)} %param.9) | copy-start | bytes 3076
  69.8 36.6 %copy-start.6 = (s32[1,1,32,8]{2,3,1,0:T(8,128)S(1)}, s32[1,1,32,8]{2,3,1,0:T(8,128)}, u32[]{:S(2)}) copy-start(s32[1,1,32,8]{2,3,1,0:T(8,128)} %param.11) | copy-start | bytes 3076
  84.8 21.8 %copy-start.7 = (s32[1,1,32]{2,1,0:T(1,128)S(1)}, s32[1,1,32]{2,1,0:T(1,128)}, u32[]{:S(2)}) copy-start(s32[1,1,32]{2,1,0:T(1,128)} %param.10) | copy-start | bytes 388
  86.2 36.6 %copy-start.9 = (bf16[256,512]{1,0:T(8,128)(2,1)S(1)}, bf16[256,512]{1,0:T(8,128)(2,1)}, u32[]{:S(2)}) copy-start(bf16[256,512]{1,0:T(8,128)(2,1)} %param.8) | copy-start | bytes 786436
  106.8 16.1 %copy-start.11 = (f32[1024,256]{1,0:T(8,128)S(1)}, f32[1024,256]{1,0:T(8,128)}, u32[]{:S(2)}) copy-start(f32[1024,256]{1,0:T(8,128)} %copy-done.10) | copy-start | bytes 3145732

commit v12 on v9

--- a/solution.py
+++ b/solution.py
@@ -177,14 +177,14 @@
     return got.reshape((n * x.shape[0],) + x.shape[1:])
 
 
-def _reduce_kernel(n_o, n_i, chunks, axis, p_ref, o_ref, g1, b_ref, g2, s1, r1, s2, r2):
+def _reduce_kernel(n_o, s_o, n_i, s_i, chunks, axis, p_ref, o_ref, g1, b_ref, g2, s1, r1, s2, r2):
     me = lax.axis_index(axis)
-    zi = lax.rem(me, n_i)
-    xo = lax.div(me, n_i)
+    zi = lax.rem(lax.div(me, s_i), n_i)
+    xo = lax.rem(lax.div(me, s_o), n_o)
     zc = n_i // chunks
 
     def device(x, z):
-        return {axis: x * n_i + z}
+        return {axis: me + (x - xo) * s_o + (z - zi) * s_i}
 
     barrier = pltpu.get_barrier_semaphore()
     for k in range(1, n_o):
@@ -271,31 +271,29 @@
             along_z(offset, z).wait_send()
 
 
-def reduce_scatter_2d(x, axis, inner):
-    n = x.shape[0]
-    outer = n // inner
-    chunks = next(c for c in (4, 2, 1) if inner % c == 0)
-    blocks = x.reshape((outer, inner) + x.shape[1:])
+def reduce_scatter_2d(x, axis, first, second, collective_id):
+    (n_o, s_o), (n_i, s_i) = first, second
+    chunks = next(c for c in (4, 2, 1) if n_i % c == 0)
     return pl.pallas_call(
-        functools.partial(_reduce_kernel, outer, inner, chunks, axis),
-        out_shape=jax.ShapeDtypeStruct(x.shape[1:], jnp.float32),
+        functools.partial(_reduce_kernel, n_o, s_o, n_i, s_i, chunks, axis),
+        out_shape=jax.ShapeDtypeStruct(x.shape[2:], jnp.float32),
         in_specs=[pl.BlockSpec(memory_space=pltpu.VMEM)],
         out_specs=pl.BlockSpec(memory_space=pltpu.VMEM),
         scratch_shapes=[
-            pltpu.VMEM(blocks.shape, x.dtype),
-            pltpu.VMEM((inner,) + x.shape[1:], x.dtype),
-            pltpu.VMEM((inner,) + x.shape[1:], x.dtype),
-            pltpu.SemaphoreType.DMA((outer, chunks)),
-            pltpu.SemaphoreType.DMA((outer, chunks)),
-            pltpu.SemaphoreType.DMA((inner,)),
-            pltpu.SemaphoreType.DMA((inner,)),
+            pltpu.VMEM(x.shape, x.dtype),
+            pltpu.VMEM(x.shape[1:], x.dtype),
+            pltpu.VMEM(x.shape[1:], x.dtype),
+            pltpu.SemaphoreType.DMA((n_o, chunks)),
+            pltpu.SemaphoreType.DMA((n_o, chunks)),
+            pltpu.SemaphoreType.DMA((n_i,)),
+            pltpu.SemaphoreType.DMA((n_i,)),
         ],
         compiler_params=pltpu.CompilerParams(
-            collective_id=8,
+            collective_id=collective_id,
             has_side_effects=True,
             vmem_limit_bytes=min(4 * x.dtype.itemsize * x.size + (8 << 20), 60 << 20),
         ),
-    )(blocks)
+    )(x)
 
 
 def inner_size(devices):
@@ -320,8 +318,13 @@
     pre = jnp.dot(shard_rows, w_in, preferred_element_type=jnp.float32)
     hidden = jax.nn.silu(pre).astype(jnp.bfloat16)
     embed_part = jnp.dot(hidden, w_out, preferred_element_type=jnp.float32)
-    embed = reduce_scatter(
-        embed_part.reshape(n_sub, own_rows, embed_part.shape[1]), "sub", sub_inner, True, 4
+    sub_outer = n_sub // sub_inner
+    embed = reduce_scatter_2d(
+        embed_part.reshape(sub_inner, sub_outer, own_rows, embed_part.shape[1]),
+        "sub",
+        (sub_inner, 1),
+        (sub_outer, sub_inner),
+        4,
     )
     norm = jnp.sqrt(jnp.sum(embed * embed, axis=-1, keepdims=True) + 1e-06)
     unit = embed / norm
@@ -373,7 +376,14 @@
         ],
         axis=1,
     )
-    summed = reduce_scatter_2d(partial, "mass", mass_inner)
+    mass_outer = n_mass // mass_inner
+    summed = reduce_scatter_2d(
+        partial.reshape((mass_outer, mass_inner) + partial.shape[1:]),
+        "mass",
+        (mass_outer, mass_inner),
+        (mass_inner, 1),
+        8,
+    )
     grad_in = summed[:hid].T
     grad_out_t = summed[hid:].reshape(out_rows, hid)
     return (grad_in, grad_out_t)

time: 171 us -> 165 us (0.965)
  other arithmetic: 5.18 us -> 0.64 us
  local copies, waits for them, and re-layouts: 9.03 us -> 6.06 us
  matrix products: 10.5 us -> 12.5 us
    pallas_call x3 -> x1, Pallas kernels: 34.3 us -> 17 us  [exchange(): pl.pallas_call(functools.partial(_exchange_kernel, n, stride, axis, gathe...]
    pallas_call x1 -> x2, Pallas kernels: 42.7 us -> 59.1 us  [reduce_scatter_2d(): pl.pallas_call(functools.partial(_reduce_kernel, n_o, s_o, n_i, s_i, chun...]
    reduce_sum x2 -> x0, other arithmetic: 2.96 us -> none  [reduce_scatter(): blocks = jnp.sum(got.astype(jnp.float32), axis=0)]
    unnamed x27 -> x21, local copies, waits for them, and re-layouts: 6.29 us -> 3.73 us
where the time goes in v12:
time: 165 us
  Pallas kernels  145 us (88%)
  matrix products  12.5 us (8%)
  local copies, waits for them, and re-layouts  6.06 us (4%)
    pallas_call x2, Pallas kernels, all_gather(): pl.pallas_call(functools.partial(_gather_kernel, outer, inner, axis), out...  68.7 us
    pallas_call x2, Pallas kernels, reduce_scatter_2d(): pl.pallas_call(functools.partial(_reduce_kernel, n_o, s_o, n_i, s_i, chun...  59.1 us
    pallas_call x1, Pallas kernels, exchange(): pl.pallas_call(functools.partial(_exchange_kernel, n, stride, axis, gathe...  17 us
    dot_general x1, matrix products, per_device(): lax.dot_general(grad_pre, shard_rows, (((0,), (0,)), ((), ())), preferred...  5.77 us
    unnamed x21, local copies, waits for them, and re-layouts  3.73 us

profile of v12, /device:TPU:1, one launch (start us, length us, event | category | flops | bytes accessed | tf_op | source)
XLA Modules:
  0.0 164.9 jit_solution(3804234547922019097)
XLA Ops:
  0.6 0.0 copy-start
  0.6 0.0 copy-start.2
  0.7 1.4 copy-done.2
  2.0 55.3 %shard_map.77 = bf16[2,4,128,4096]{3,2,1,0:T(8,128)(2,1)S(1)} custom-call(bf16[128,4096]{1,0:T(8,128)(2,1)S(1)} %copy-done.2), custom_call_target="tpu_custom_call" | custom-call | tf_op jit(solution)/shard_map/pallas_call | solution.py:161
  57.4 0.0 copy-start.6
  57.4 2.3 %fusion.15 = f32[1024,256]{1,0:T(8,128)S(1)} fusion(bf16[1024,4096]{1,0:T(8,128)(2,1)S(1)} %bitcast.37, bf16[4096,256]{1,0:T(8,128)(2,1)S(1)} %copy-done), kind=kOutput, calls=%fused_computation.33 | convolution fusion | flops 2147483648 | bytes 11534336 | tf_op jit(solution)/shard_map/dot_general | solution.py:318
  59.7 0.8 copy-done.1
  60.6 0.5 fusion.14
  61.0 0.6 copy-done.7
  61.6 16.4 %shard_map.78 = f32[128,512]{1,0:T(8,128)S(1)} custom-call(f32[2,4,128,512]{3,2,1,0:T(8,128)S(1)} %bitcast.39), custom_call_target="tpu_custom_call" | custom-call | tf_op jit(solution)/shard_map/pallas_call | solution.py:277
  78.1 0.1 multiply_reduce_fusion.1
  78.2 0.1 copy.15
  78.3 0.1 eq.15
  78.4 0.3 fusion.3.x_ref
  78.7 17.0 %shard_map.79 = bf16[32,8,512]{2,1,0:T(8,128)(2,1)S(1)} custom-call(bf16[32,8,512]{2,1,0:T(8,128)(2,1)S(1)} %fusion.3.x_ref), custom_call_target="tpu_custom_call" | custom-call | tf_op jit(solution)/shard_map/pallas_call | solution.py:58
  95.7 0.1 fusion.4
  95.8 0.0 copy-done.4
  95.8 0.1 copy.16
  95.9 0.1 fusion.13
  96.0 0.5 multiply_reduce_fusion
  96.5 0.1 divide_convert_fusion.x_ref
  96.7 13.4 %shard_map.80 = bf16[2,4,128,512]{3,2,1,0:T(8,128)(2,1)S(1)} custom-call(bf16[128,512]{1,0:T(8,128)(2,1)S(1)} %divide_convert_fusion.x_ref), custom_call_target="tpu_custom_call" | custom-call | tf_op jit(solution)/shard_map/pallas_call | solution.py:161
  110.1 0.0 copy-done.8
  110.1 1.3 convolution_convert_fusion.1
  111.4 1.0 concatenate.9
  112.4 1.9 %fusion.2 = bf16[1024,256]{1,0:T(8,128)(2,1)S(1)} fusion(bf16[1024,512]{1,0:T(8,128)(2,1)S(1)} %bitcast.41, bf16[256,512]{1,0:T(8,128)(2,1)} %param.8, f32[1024,256]{1,0:T(8,128)} %copy-done.7), kind=kOutput, calls=%fused_computation.6 | convolution fusion | flops 270794752 | bytes 2883584 | tf_op jit(solution)/shard_map/dot_general | solution.py:354
  114.3 5.8 %fusion = bf16[32,32,8,128]{3,2,1,0:T(8,128)(2,1)S(1)} fusion(bf16[1024,256]{1,0:T(8,128)(2,1)S(1)} %fusion.2, bf16[1024,4096]{1,0:T(8,128)(2,1)} %bitcast.38), kind=kOutput, calls=%fused_computation.3 | convolution fusion | flops 2148532224 | bytes 11010048 | tf_op jit(solution)/shard_map/dot_general | solution.py:364
  120.0 0.6 copy.21
  120.6 0.2 pad_maximum_fusion.p_ref
  120.8 42.7 %shard_map.81 = f32[288,128]{1,0:T(8,128)S(1)} custom-call(bf16[4,8,288,128]{3,2,1,0:T(8,128)(2,1)S(1)} %pad_maximum_fusion.p_ref), custom_call_target="tpu_custom_call" | custom-call | tf_op jit(solution)/shard_map/pallas_call | solution.py:277
  163.5 0.8 copy.18
  164.3 0.6 reshape.80
  (13 shorter events, 0.0 us)
Async XLA Ops:
  0.6 56.7 %copy-start = (bf16[4096,256]{1,0:T(8,128)(2,1)S(1)}, bf16[4096,256]{1,0:T(8,128)(2,1)}, u32[]{:S(2)}) copy-start(bf16[4096,256]{1,0:T(8,128)(2,1)} %param.7) | copy-start | bytes 6291460
  0.6 1.4 copy-start.2
  57.4 3.2 %copy-start.1 = (bf16[2,4,128,4096]{3,2,1,0:T(8,128)(2,1)}, bf16[2,4,128,4096]{3,2,1,0:T(8,128)(2,1)S(1)}, u32[]{:S(2)}) copy-start(bf16[2,4,128,4096]{3,2,1,0:T(8,128)(2,1)S(1)} %shard_map.77) | copy-start | bytes 25165828
  57.4 3.2 %copy-start.6 = (bf16[256,512]{1,0:T(8,128)(2,1)S(1)}, bf16[256,512]{1,0:T(8,128)(2,1)}, u32[]{:S(2)}) copy-start(bf16[256,512]{1,0:T(8,128)(2,1)} %param.8) | copy-start | bytes 786436
  60.6 1.0 copy-start.7
  61.6 16.6 %copy-start.3 = (s32[1,1,32,8]{2,3,1,0:T(8,128)S(1)}, s32[1,1,32,8]{2,3,1,0:T(8,128)}, u32[]{:S(2)}) copy-start(s32[1,1,32,8]{2,3,1,0:T(8,128)} %param.9) | copy-start | bytes 3076
  61.6 34.2 %copy-start.4 = (s32[1,1,32,8]{2,3,1,0:T(8,128)S(1)}, s32[1,1,32,8]{2,3,1,0:T(8,128)}, u32[]{:S(2)}) copy-start(s32[1,1,32,8]{2,3,1,0:T(8,128)} %param.11) | copy-start | bytes 3076
  61.6 34.3 %copy-start.5 = (s32[1,1,32]{2,1,0:T(1,128)S(1)}, s32[1,1,32]{2,1,0:T(1,128)}, u32[]{:S(2)}) copy-start(s32[1,1,32]{2,1,0:T(1,128)} %param.10) | copy-start | bytes 388
  95.9 14.2 %copy-start.8 = (f32[1024,256]{1,0:T(8,128)S(1)}, f32[1024,256]{1,0:T(8,128)}, u32[]{:S(2)}) copy-start(f32[1024,256]{1,0:T(8,128)} %copy-done.7) | copy-start | bytes 3145732

commit v13 on v12

--- a/solution.py
+++ b/solution.py
@@ -273,7 +273,7 @@
 
 def reduce_scatter_2d(x, axis, first, second, collective_id):
     (n_o, s_o), (n_i, s_i) = first, second
-    chunks = next(c for c in (4, 2, 1) if n_i % c == 0)
+    chunks = next(c for c in (8, 4, 2, 1) if n_i % c == 0)
     return pl.pallas_call(
         functools.partial(_reduce_kernel, n_o, s_o, n_i, s_i, chunks, axis),
         out_shape=jax.ShapeDtypeStruct(x.shape[2:], jnp.float32),

time: 165 us -> 162 us (0.982)
  Pallas kernels: 145 us -> 142 us
    pallas_call x2, Pallas kernels: 59.1 us -> 56.1 us  [reduce_scatter_2d(): pl.pallas_call(functools.partial(_reduce_kernel, n_o, s_o, n_i, s_i, chun...]
where the time goes in v13:
time: 162 us
  Pallas kernels  142 us (88%)
  matrix products  12.5 us (8%)
  local copies, waits for them, and re-layouts  6.06 us (4%)
    pallas_call x2, Pallas kernels, all_gather(): pl.pallas_call(functools.partial(_gather_kernel, outer, inner, axis), out...  68.7 us
    pallas_call x2, Pallas kernels, reduce_scatter_2d(): pl.pallas_call(functools.partial(_reduce_kernel, n_o, s_o, n_i, s_i, chun...  56.1 us
    pallas_call x1, Pallas kernels, exchange(): pl.pallas_call(functools.partial(_exchange_kernel, n, stride, axis, gathe...  17 us
    dot_general x1, matrix products, per_device(): lax.dot_general(grad_pre, shard_rows, (((0,), (0,)), ((), ())), preferred...  5.77 us
    unnamed x21, local copies, waits for them, and re-layouts  3.74 us

profile of v13, /device:TPU:1, one launch (start us, length us, event | category | flops | bytes accessed | tf_op | source)
XLA Modules:
  0.0 161.9 jit_solution(15403386952355807440)
XLA Ops:
  0.6 0.0 copy-start
  0.6 0.0 copy-start.2
  0.7 1.4 copy-done.2
  2.0 55.3 %shard_map.77 = bf16[2,4,128,4096]{3,2,1,0:T(8,128)(2,1)S(1)} custom-call(bf16[128,4096]{1,0:T(8,128)(2,1)S(1)} %copy-done.2), custom_call_target="tpu_custom_call" | custom-call | tf_op jit(solution)/shard_map/pallas_call | solution.py:161
  57.4 0.0 copy-start.6
  57.4 2.3 %fusion.15 = f32[1024,256]{1,0:T(8,128)S(1)} fusion(bf16[1024,4096]{1,0:T(8,128)(2,1)S(1)} %bitcast.37, bf16[4096,256]{1,0:T(8,128)(2,1)S(1)} %copy-done), kind=kOutput, calls=%fused_computation.33 | convolution fusion | flops 2147483648 | bytes 11534336 | tf_op jit(solution)/shard_map/dot_general | solution.py:318
  59.7 0.8 copy-done.1
  60.6 0.5 fusion.14
  61.0 0.6 copy-done.7
  61.6 16.4 %shard_map.78 = f32[128,512]{1,0:T(8,128)S(1)} custom-call(f32[2,4,128,512]{3,2,1,0:T(8,128)S(1)} %bitcast.39), custom_call_target="tpu_custom_call" | custom-call | tf_op jit(solution)/shard_map/pallas_call | solution.py:277
  78.1 0.1 multiply_reduce_fusion.1
  78.2 0.1 copy.15
  78.3 0.1 eq.15
  78.4 0.3 fusion.3.x_ref
  78.7 17.0 %shard_map.79 = bf16[32,8,512]{2,1,0:T(8,128)(2,1)S(1)} custom-call(bf16[32,8,512]{2,1,0:T(8,128)(2,1)S(1)} %fusion.3.x_ref), custom_call_target="tpu_custom_call" | custom-call | tf_op jit(solution)/shard_map/pallas_call | solution.py:58
  95.7 0.1 fusion.4
  95.8 0.0 copy-done.4
  95.8 0.1 copy.16
  95.9 0.1 fusion.13
  96.0 0.5 multiply_reduce_fusion
  96.5 0.1 divide_convert_fusion.x_ref
  96.7 13.4 %shard_map.80 = bf16[2,4,128,512]{3,2,1,0:T(8,128)(2,1)S(1)} custom-call(bf16[128,512]{1,0:T(8,128)(2,1)S(1)} %divide_convert_fusion.x_ref), custom_call_target="tpu_custom_call" | custom-call | tf_op jit(solution)/shard_map/pallas_call | solution.py:161
  110.1 0.0 copy-done.8
  110.1 1.3 convolution_convert_fusion.1
  111.4 1.0 concatenate.9
  112.4 1.9 %fusion.2 = bf16[1024,256]{1,0:T(8,128)(2,1)S(1)} fusion(bf16[1024,512]{1,0:T(8,128)(2,1)S(1)} %bitcast.41, bf16[256,512]{1,0:T(8,128)(2,1)} %param.8, f32[1024,256]{1,0:T(8,128)} %copy-done.7), kind=kOutput, calls=%fused_computation.6 | convolution fusion | flops 270794752 | bytes 2883584 | tf_op jit(solution)/shard_map/dot_general | solution.py:354
  114.3 5.8 %fusion = bf16[32,32,8,128]{3,2,1,0:T(8,128)(2,1)S(1)} fusion(bf16[1024,256]{1,0:T(8,128)(2,1)S(1)} %fusion.2, bf16[1024,4096]{1,0:T(8,128)(2,1)} %bitcast.38), kind=kOutput, calls=%fused_computation.3 | convolution fusion | flops 2148532224 | bytes 11010048 | tf_op jit(solution)/shard_map/dot_general | solution.py:364
  120.0 0.6 copy.21
  120.6 0.2 pad_maximum_fusion.p_ref
  120.8 39.7 %shard_map.81 = f32[288,128]{1,0:T(8,128)S(1)} custom-call(bf16[4,8,288,128]{3,2,1,0:T(8,128)(2,1)S(1)} %pad_maximum_fusion.p_ref), custom_call_target="tpu_custom_call" | custom-call | tf_op jit(solution)/shard_map/pallas_call | solution.py:277
  160.6 0.8 copy.18
  161.3 0.6 reshape.80
  (13 shorter events, 0.0 us)
Async XLA Ops:
  0.6 56.7 %copy-start = (bf16[4096,256]{1,0:T(8,128)(2,1)S(1)}, bf16[4096,256]{1,0:T(8,128)(2,1)}, u32[]{:S(2)}) copy-start(bf16[4096,256]{1,0:T(8,128)(2,1)} %param.7) | copy-start | bytes 6291460
  0.6 1.4 copy-start.2
  57.4 3.2 %copy-start.1 = (bf16[2,4,128,4096]{3,2,1,0:T(8,128)(2,1)}, bf16[2,4,128,4096]{3,2,1,0:T(8,128)(2,1)S(1)}, u32[]{:S(2)}) copy-start(bf16[2,4,128,4096]{3,2,1,0:T(8,128)(2,1)S(1)} %shard_map.77) | copy-start | bytes 25165828
  57.4 3.2 %copy-start.6 = (bf16[256,512]{1,0:T(8,128)(2,1)S(1)}, bf16[256,512]{1,0:T(8,128)(2,1)}, u32[]{:S(2)}) copy-start(bf16[256,512]{1,0:T(8,128)(2,1)} %param.8) | copy-start | bytes 786436
  60.6 1.0 copy-start.7
  61.6 16.6 %copy-start.3 = (s32[1,1,32,8]{2,3,1,0:T(8,128)S(1)}, s32[1,1,32,8]{2,3,1,0:T(8,128)}, u32[]{:S(2)}) copy-start(s32[1,1,32,8]{2,3,1,0:T(8,128)} %param.9) | copy-start | bytes 3076
  61.6 34.2 %copy-start.4 = (s32[1,1,32,8]{2,3,1,0:T(8,128)S(1)}, s32[1,1,32,8]{2,3,1,0:T(8,128)}, u32[]{:S(2)}) copy-start(s32[1,1,32,8]{2,3,1,0:T(8,128)} %param.11) | copy-start | bytes 3076
  61.6 34.3 %copy-start.5 = (s32[1,1,32]{2,1,0:T(1,128)S(1)}, s32[1,1,32]{2,1,0:T(1,128)}, u32[]{:S(2)}) copy-start(s32[1,1,32]{2,1,0:T(1,128)} %param.10) | copy-start | bytes 388
  95.9 14.2 %copy-start.8 = (f32[1024,256]{1,0:T(8,128)S(1)}, f32[1024,256]{1,0:T(8,128)}, u32[]{:S(2)}) copy-start(f32[1024,256]{1,0:T(8,128)} %copy-done.7) | copy-start | bytes 3145732

commit v14 on v13

--- a/solution.py
+++ b/solution.py
@@ -90,7 +90,7 @@
     return blocks
 
 
-def _gather_kernel(n_outer, n_inner, axis, x_ref, o_ref, got, send_sems, recv_sems):
+def _gather_kernel(n_outer, n_inner, axis, x_ref, o_ref, got, send_sems, recv_sems, local_sems):
     me = lax.axis_index(axis)
     ci = lax.rem(me, n_inner)
     yo = lax.div(me, n_inner)
@@ -134,25 +134,34 @@
             device_id_type=MESH,
         ).wait_recv()
 
+    locals_ = []
+
+    def keep(src, c, y):
+        copy = pltpu.make_async_copy(src, o_ref.at[c, y], local_sems.at[slot(c, y)])
+        copy.start()
+        locals_.append(copy)
+
     for y in outer_peers:
         send(x_ref, ci, yo, device(ci, y))
     for c in inner_peers:
         send(x_ref, ci, yo, device(c, yo))
-    o_ref[ci, yo] = x_ref[...]
+    keep(x_ref, ci, yo)
     for k in range(1, n_outer):
         y = lax.rem(yo + n_outer - k, n_outer)
         receive(ci, y)
         for c in inner_peers:
             send(got.at[ci, y], ci, y, device(c, yo))
-        o_ref[ci, y] = got[ci, y]
+        keep(got.at[ci, y], ci, y)
     for j in range(1, n_inner):
         c = lax.rem(ci + n_inner - j, n_inner)
         for k in range(n_outer):
             y = lax.rem(yo + k, n_outer)
             receive(c, y)
-            o_ref[c, y] = got[c, y]
+            keep(got.at[c, y], c, y)
     for copy in sends:
         copy.wait_send()
+    for copy in locals_:
+        copy.wait()
 
 
 def all_gather(x, axis, n, inner, collective_id):
@@ -165,6 +174,7 @@
         out_specs=pl.BlockSpec(memory_space=pltpu.VMEM),
         scratch_shapes=[
             pltpu.VMEM(shape, x.dtype),
+            pltpu.SemaphoreType.DMA((n,)),
             pltpu.SemaphoreType.DMA((n,)),
             pltpu.SemaphoreType.DMA((n,)),
         ],

time: 162 us -> 163 us (level)
  no operation moved by 1% of the time
where the time goes in v14:
time: 163 us
  Pallas kernels  143 us (88%)
  matrix products  12.5 us (8%)
  local copies, waits for them, and re-layouts  6.06 us (4%)
    pallas_call x2, Pallas kernels, all_gather(): pl.pallas_call(functools.partial(_gather_kernel, outer, inner, axis), out...  69.3 us
    pallas_call x2, Pallas kernels, reduce_scatter_2d(): pl.pallas_call(functools.partial(_reduce_kernel, n_o, s_o, n_i, s_i, chun...  56.6 us
    pallas_call x1, Pallas kernels, exchange(): pl.pallas_call(functools.partial(_exchange_kernel, n, stride, axis, gathe...  17 us
    dot_general x1, matrix products, per_device(): lax.dot_general(grad_pre, shard_rows, (((0,), (0,)), ((), ())), preferred...  5.77 us
    unnamed x21, local copies, waits for them, and re-layouts  3.73 us

profile of v14, /device:TPU:1, one launch (start us, length us, event | category | flops | bytes accessed | tf_op | source)
XLA Modules:
  0.0 163.0 jit_solution(13532145762264128421)
XLA Ops:
  0.6 0.0 copy-start
  0.6 0.0 copy-start.2
  0.7 1.4 copy-done.2
  2.0 55.4 %shard_map.77 = bf16[2,4,128,4096]{3,2,1,0:T(8,128)(2,1)S(1)} custom-call(bf16[128,4096]{1,0:T(8,128)(2,1)S(1)} %copy-done.2), custom_call_target="tpu_custom_call" | custom-call | tf_op jit(solution)/shard_map/pallas_call | solution.py:170
  57.5 0.0 copy-start.1
  57.5 0.0 copy-done
  57.5 0.0 copy-start.6
  57.5 2.3 %fusion.15 = f32[1024,256]{1,0:T(8,128)S(1)} fusion(bf16[1024,4096]{1,0:T(8,128)(2,1)S(1)} %bitcast.37, bf16[4096,256]{1,0:T(8,128)(2,1)S(1)} %copy-done), kind=kOutput, calls=%fused_computation.33 | convolution fusion | flops 2147483648 | bytes 11534336 | tf_op jit(solution)/shard_map/dot_general | solution.py:328
  59.8 0.8 copy-done.1
  60.7 0.5 fusion.14
  61.1 0.6 copy-done.7
  61.7 16.4 %shard_map.78 = f32[128,512]{1,0:T(8,128)S(1)} custom-call(f32[2,4,128,512]{3,2,1,0:T(8,128)S(1)} %bitcast.39), custom_call_target="tpu_custom_call" | custom-call | tf_op jit(solution)/shard_map/pallas_call | solution.py:287
  78.1 0.1 multiply_reduce_fusion.1
  78.3 0.1 copy.15
  78.3 0.1 eq.15
  78.4 0.3 fusion.3.x_ref
  78.7 17.0 %shard_map.79 = bf16[32,8,512]{2,1,0:T(8,128)(2,1)S(1)} custom-call(bf16[32,8,512]{2,1,0:T(8,128)(2,1)S(1)} %fusion.3.x_ref), custom_call_target="tpu_custom_call" | custom-call | tf_op jit(solution)/shard_map/pallas_call | solution.py:58
  95.8 0.1 fusion.4
  95.9 0.1 copy.16
  96.0 0.1 fusion.13
  96.1 0.5 multiply_reduce_fusion
  96.6 0.1 divide_convert_fusion.x_ref
  96.7 13.9 %shard_map.80 = bf16[2,4,128,512]{3,2,1,0:T(8,128)(2,1)S(1)} custom-call(bf16[128,512]{1,0:T(8,128)(2,1)S(1)} %divide_convert_fusion.x_ref), custom_call_target="tpu_custom_call" | custom-call | tf_op jit(solution)/shard_map/pallas_call | solution.py:170
  110.7 1.3 convolution_convert_fusion.1
  112.0 1.0 concatenate.9
  113.0 1.9 %fusion.2 = bf16[1024,256]{1,0:T(8,128)(2,1)S(1)} fusion(bf16[1024,512]{1,0:T(8,128)(2,1)S(1)} %bitcast.41, bf16[256,512]{1,0:T(8,128)(2,1)} %param.8, f32[1024,256]{1,0:T(8,128)} %copy-done.7), kind=kOutput, calls=%fused_computation.6 | convolution fusion | flops 270794752 | bytes 2883584 | tf_op jit(solution)/shard_map/dot_general | solution.py:364
  114.9 5.8 %fusion = bf16[32,32,8,128]{3,2,1,0:T(8,128)(2,1)S(1)} fusion(bf16[1024,256]{1,0:T(8,128)(2,1)S(1)} %fusion.2, bf16[1024,4096]{1,0:T(8,128)(2,1)} %bitcast.38), kind=kOutput, calls=%fused_computation.3 | convolution fusion | flops 2148532224 | bytes 11010048 | tf_op jit(solution)/shard_map/dot_general | solution.py:374
  120.6 0.6 copy.21
  121.2 0.2 pad_maximum_fusion.p_ref
  121.4 40.2 %shard_map.81 = f32[288,128]{1,0:T(8,128)S(1)} custom-call(bf16[4,8,288,128]{3,2,1,0:T(8,128)(2,1)S(1)} %pad_maximum_fusion.p_ref), custom_call_target="tpu_custom_call" | custom-call | tf_op jit(solution)/shard_map/pallas_call | solution.py:287
  161.7 0.8 copy.18
  162.4 0.6 reshape.80
  (13 shorter events, 0.0 us)
Async XLA Ops:
  0.6 56.8 %copy-start = (bf16[4096,256]{1,0:T(8,128)(2,1)S(1)}, bf16[4096,256]{1,0:T(8,128)(2,1)}, u32[]{:S(2)}) copy-start(bf16[4096,256]{1,0:T(8,128)(2,1)} %param.7) | copy-start | bytes 6291460
  0.6 1.4 copy-start.2
  57.5 3.2 %copy-start.1 = (bf16[2,4,128,4096]{3,2,1,0:T(8,128)(2,1)}, bf16[2,4,128,4096]{3,2,1,0:T(8,128)(2,1)S(1)}, u32[]{:S(2)}) copy-start(bf16[2,4,128,4096]{3,2,1,0:T(8,128)(2,1)S(1)} %shard_map.77) | copy-start | bytes 25165828
  57.5 3.2 %copy-start.6 = (bf16[256,512]{1,0:T(8,128)(2,1)S(1)}, bf16[256,512]{1,0:T(8,128)(2,1)}, u32[]{:S(2)}) copy-start(bf16[256,512]{1,0:T(8,128)(2,1)} %param.8) | copy-start | bytes 786436
  60.7 1.0 copy-start.7
  61.7 16.5 %copy-start.3 = (s32[1,1,32,8]{2,3,1,0:T(8,128)S(1)}, s32[1,1,32,8]{2,3,1,0:T(8,128)}, u32[]{:S(2)}) copy-start(s32[1,1,32,8]{2,3,1,0:T(8,128)} %param.9) | copy-start | bytes 3076
  61.7 34.2 %copy-start.4 = (s32[1,1,32,8]{2,3,1,0:T(8,128)S(1)}, s32[1,1,32,8]{2,3,1,0:T(8,128)}, u32[]{:S(2)}) copy-start(s32[1,1,32,8]{2,3,1,0:T(8,128)} %param.11) | copy-start | bytes 3076
  61.7 34.3 %copy-start.5 = (s32[1,1,32]{2,1,0:T(1,128)S(1)}, s32[1,1,32]{2,1,0:T(1,128)}, u32[]{:S(2)}) copy-start(s32[1,1,32]{2,1,0:T(1,128)} %param.10) | copy-start | bytes 388
  96.0 14.7 %copy-start.8 = (f32[1024,256]{1,0:T(8,128)S(1)}, f32[1024,256]{1,0:T(8,128)}, u32[]{:S(2)}) copy-start(f32[1024,256]{1,0:T(8,128)} %copy-done.7) | copy-start | bytes 3145732

commit v15 on v13

--- a/solution.py
+++ b/solution.py
@@ -90,7 +90,7 @@
     return blocks
 
 
-def _gather_kernel(n_outer, n_inner, axis, x_ref, o_ref, got, send_sems, recv_sems):
+def _gather_kernel(n_outer, n_inner, axis, x_ref, o_ref, got, send_sems, recv_sems, own):
     me = lax.axis_index(axis)
     ci = lax.rem(me, n_inner)
     yo = lax.div(me, n_inner)
@@ -138,7 +138,8 @@
         send(x_ref, ci, yo, device(ci, y))
     for c in inner_peers:
         send(x_ref, ci, yo, device(c, yo))
-    o_ref[ci, yo] = x_ref[...]
+    mine = pltpu.make_async_copy(x_ref, o_ref.at[ci, yo], own)
+    mine.start()
     for k in range(1, n_outer):
         y = lax.rem(yo + n_outer - k, n_outer)
         receive(ci, y)
@@ -153,6 +154,7 @@
             o_ref[c, y] = got[c, y]
     for copy in sends:
         copy.wait_send()
+    mine.wait()
 
 
 def all_gather(x, axis, n, inner, collective_id):
@@ -161,12 +163,13 @@
     got = pl.pallas_call(
         functools.partial(_gather_kernel, outer, inner, axis),
         out_shape=jax.ShapeDtypeStruct(shape, x.dtype),
-        in_specs=[pl.BlockSpec(memory_space=pltpu.VMEM)],
+        in_specs=[pl.BlockSpec(memory_space=pl.ANY)],
         out_specs=pl.BlockSpec(memory_space=pltpu.VMEM),
         scratch_shapes=[
             pltpu.VMEM(shape, x.dtype),
             pltpu.SemaphoreType.DMA((n,)),
             pltpu.SemaphoreType.DMA((n,)),
+            pltpu.SemaphoreType.DMA(()),
         ],
         compiler_params=pltpu.CompilerParams(
             collective_id=collective_id,

time: 162 us -> 162 us (level)
  no operation moved by 1% of the time
where the time goes in v15:
time: 162 us
  Pallas kernels  142 us (88%)
  matrix products  12.5 us (8%)
  local copies, waits for them, and re-layouts  6.06 us (4%)
    pallas_call x2, Pallas kernels, all_gather(): pl.pallas_call(functools.partial(_gather_kernel, outer, inner, axis), out...  68.8 us
    pallas_call x2, Pallas kernels, reduce_scatter_2d(): pl.pallas_call(functools.partial(_reduce_kernel, n_o, s_o, n_i, s_i, chun...  56.3 us
    pallas_call x1, Pallas kernels, exchange(): pl.pallas_call(functools.partial(_exchange_kernel, n, stride, axis, gathe...  17 us
    dot_general x1, matrix products, per_device(): lax.dot_general(grad_pre, shard_rows, (((0,), (0,)), ((), ())), preferred...  5.77 us
    unnamed x21, local copies, waits for them, and re-layouts  3.73 us

profile of v15, /device:TPU:1, one launch (start us, length us, event | category | flops | bytes accessed | tf_op | source)
XLA Modules:
  0.0 162.1 jit_solution(12430728885739046712)
XLA Ops:
  0.6 0.0 copy-start
  0.6 0.0 copy-start.2
  0.7 1.4 copy-done.2
  2.0 55.3 %shard_map.77 = bf16[2,4,128,4096]{3,2,1,0:T(8,128)(2,1)S(1)} custom-call(bf16[128,4096]{1,0:T(8,128)(2,1)S(1)} %copy-done.2), custom_call_target="tpu_custom_call" | custom-call | tf_op jit(solution)/shard_map/pallas_call | solution.py:163
  57.4 0.0 copy-start.6
  57.4 2.3 %fusion.15 = f32[1024,256]{1,0:T(8,128)S(1)} fusion(bf16[1024,4096]{1,0:T(8,128)(2,1)S(1)} %bitcast.37, bf16[4096,256]{1,0:T(8,128)(2,1)S(1)} %copy-done), kind=kOutput, calls=%fused_computation.33 | convolution fusion | flops 2147483648 | bytes 11534336 | tf_op jit(solution)/shard_map/dot_general | solution.py:321
  59.7 0.8 copy-done.1
  60.6 0.5 fusion.14
  61.0 0.6 copy-done.7
  61.6 16.4 %shard_map.78 = f32[128,512]{1,0:T(8,128)S(1)} custom-call(f32[2,4,128,512]{3,2,1,0:T(8,128)S(1)} %bitcast.39), custom_call_target="tpu_custom_call" | custom-call | tf_op jit(solution)/shard_map/pallas_call | solution.py:280
  78.1 0.1 multiply_reduce_fusion.1
  78.2 0.0 copy-done.3
  78.2 0.1 copy.15
  78.3 0.1 eq.15
  78.4 0.3 fusion.3.x_ref
  78.7 17.0 %shard_map.79 = bf16[32,8,512]{2,1,0:T(8,128)(2,1)S(1)} custom-call(bf16[32,8,512]{2,1,0:T(8,128)(2,1)S(1)} %fusion.3.x_ref), custom_call_target="tpu_custom_call" | custom-call | tf_op jit(solution)/shard_map/pallas_call | solution.py:58
  95.7 0.1 fusion.4
  95.8 0.1 copy.16
  95.9 0.1 fusion.13
  96.0 0.5 multiply_reduce_fusion
  96.5 0.1 divide_convert_fusion.x_ref
  96.7 13.4 %shard_map.80 = bf16[2,4,128,512]{3,2,1,0:T(8,128)(2,1)S(1)} custom-call(bf16[128,512]{1,0:T(8,128)(2,1)S(1)} %divide_convert_fusion.x_ref), custom_call_target="tpu_custom_call" | custom-call | tf_op jit(solution)/shard_map/pallas_call | solution.py:163
  110.1 0.0 copy-done.8
  110.1 1.3 convolution_convert_fusion.1
  111.4 1.0 concatenate.9
  112.4 1.9 %fusion.2 = bf16[1024,256]{1,0:T(8,128)(2,1)S(1)} fusion(bf16[1024,512]{1,0:T(8,128)(2,1)S(1)} %bitcast.41, bf16[256,512]{1,0:T(8,128)(2,1)} %param.8, f32[1024,256]{1,0:T(8,128)} %copy-done.7), kind=kOutput, calls=%fused_computation.6 | convolution fusion | flops 270794752 | bytes 2883584 | tf_op jit(solution)/shard_map/dot_general | solution.py:357
  114.3 5.8 %fusion = bf16[32,32,8,128]{3,2,1,0:T(8,128)(2,1)S(1)} fusion(bf16[1024,256]{1,0:T(8,128)(2,1)S(1)} %fusion.2, bf16[1024,4096]{1,0:T(8,128)(2,1)} %bitcast.38), kind=kOutput, calls=%fused_computation.3 | convolution fusion | flops 2148532224 | bytes 11010048 | tf_op jit(solution)/shard_map/dot_general | solution.py:367
  120.1 0.6 copy.21
  120.6 0.2 pad_maximum_fusion.p_ref
  120.8 39.9 %shard_map.81 = f32[288,128]{1,0:T(8,128)S(1)} custom-call(bf16[4,8,288,128]{3,2,1,0:T(8,128)(2,1)S(1)} %pad_maximum_fusion.p_ref), custom_call_target="tpu_custom_call" | custom-call | tf_op jit(solution)/shard_map/pallas_call | solution.py:280
  160.7 0.8 copy.18
  161.5 0.6 reshape.80
  (13 shorter events, 0.0 us)
Async XLA Ops:
  0.6 56.8 %copy-start = (bf16[4096,256]{1,0:T(8,128)(2,1)S(1)}, bf16[4096,256]{1,0:T(8,128)(2,1)}, u32[]{:S(2)}) copy-start(bf16[4096,256]{1,0:T(8,128)(2,1)} %param.7) | copy-start | bytes 6291460
  0.6 1.4 copy-start.2
  57.4 3.2 %copy-start.1 = (bf16[2,4,128,4096]{3,2,1,0:T(8,128)(2,1)}, bf16[2,4,128,4096]{3,2,1,0:T(8,128)(2,1)S(1)}, u32[]{:S(2)}) copy-start(bf16[2,4,128,4096]{3,2,1,0:T(8,128)(2,1)S(1)} %shard_map.77) | copy-start | bytes 25165828
  57.4 3.2 %copy-start.6 = (bf16[256,512]{1,0:T(8,128)(2,1)S(1)}, bf16[256,512]{1,0:T(8,128)(2,1)}, u32[]{:S(2)}) copy-start(bf16[256,512]{1,0:T(8,128)(2,1)} %param.8) | copy-start | bytes 786436
  60.6 1.0 copy-start.7
  61.6 16.6 %copy-start.3 = (s32[1,1,32,8]{2,3,1,0:T(8,128)S(1)}, s32[1,1,32,8]{2,3,1,0:T(8,128)}, u32[]{:S(2)}) copy-start(s32[1,1,32,8]{2,3,1,0:T(8,128)} %param.9) | copy-start | bytes 3076
  61.6 34.2 %copy-start.4 = (s32[1,1,32,8]{2,3,1,0:T(8,128)S(1)}, s32[1,1,32,8]{2,3,1,0:T(8,128)}, u32[]{:S(2)}) copy-start(s32[1,1,32,8]{2,3,1,0:T(8,128)} %param.11) | copy-start | bytes 3076
  61.6 34.3 %copy-start.5 = (s32[1,1,32]{2,1,0:T(1,128)S(1)}, s32[1,1,32]{2,1,0:T(1,128)}, u32[]{:S(2)}) copy-start(s32[1,1,32]{2,1,0:T(1,128)} %param.10) | copy-start | bytes 388
  95.9 14.2 %copy-start.8 = (f32[1024,256]{1,0:T(8,128)S(1)}, f32[1024,256]{1,0:T(8,128)}, u32[]{:S(2)}) copy-start(f32[1024,256]{1,0:T(8,128)} %copy-done.7) | copy-start | bytes 3145732

commit v16 on v13

--- a/solution.py
+++ b/solution.py
@@ -40,7 +40,6 @@
         sends.append(copy)
     o_ref[mine] = x_ref[...] if gather else x_ref[mine]
     for k in range(1, n):
-        sends[k - 1].wait_send()
         source = lax.rem(mine + n - k, n)
         pltpu.make_async_remote_copy(
             src_ref=x_ref if gather else x_ref.at[source],
@@ -51,6 +50,8 @@
             device_id_type=MESH,
         ).wait_recv()
         o_ref[source] = got[source]
+    for copy in sends:
+        copy.wait_send()
 
 
 def exchange(x, axis, n, collective_id, gather=False, stride=1):

time: 162 us -> 162 us (level)
  no operation moved by 1% of the time
where the time goes in v16:
time: 162 us
  Pallas kernels  142 us (88%)
  matrix products  12.5 us (8%)
  local copies, waits for them, and re-layouts  6.06 us (4%)
    pallas_call x2, Pallas kernels, all_gather(): pl.pallas_call(functools.partial(_gather_kernel, outer, inner, axis), out...  68.7 us
    pallas_call x2, Pallas kernels, reduce_scatter_2d(): pl.pallas_call(functools.partial(_reduce_kernel, n_o, s_o, n_i, s_i, chun...  56.1 us
    pallas_call x1, Pallas kernels, exchange(): pl.pallas_call(functools.partial(_exchange_kernel, n, stride, axis, gathe...  17.1 us
    dot_general x1, matrix products, per_device(): lax.dot_general(grad_pre, shard_rows, (((0,), (0,)), ((), ())), preferred...  5.77 us
    unnamed x21, local copies, waits for them, and re-layouts  3.74 us

profile of v16, /device:TPU:1, one launch (start us, length us, event | category | flops | bytes accessed | tf_op | source)
XLA Modules:
  0.0 162.0 jit_solution(10511591099475479314)
XLA Ops:
  0.6 0.0 copy-start
  0.6 0.0 copy-start.2
  0.7 1.4 copy-done.2
  2.0 55.3 %shard_map.77 = bf16[2,4,128,4096]{3,2,1,0:T(8,128)(2,1)S(1)} custom-call(bf16[128,4096]{1,0:T(8,128)(2,1)S(1)} %copy-done.2), custom_call_target="tpu_custom_call" | custom-call | tf_op jit(solution)/shard_map/pallas_call | solution.py:162
  57.4 0.0 copy-start.1
  57.4 0.0 copy-start.6
  57.4 2.3 %fusion.15 = f32[1024,256]{1,0:T(8,128)S(1)} fusion(bf16[1024,4096]{1,0:T(8,128)(2,1)S(1)} %bitcast.37, bf16[4096,256]{1,0:T(8,128)(2,1)S(1)} %copy-done), kind=kOutput, calls=%fused_computation.33 | convolution fusion | flops 2147483648 | bytes 11534336 | tf_op jit(solution)/shard_map/dot_general | solution.py:319
  59.7 0.8 copy-done.1
  60.6 0.5 fusion.14
  61.0 0.6 copy-done.7
  61.6 16.4 %shard_map.78 = f32[128,512]{1,0:T(8,128)S(1)} custom-call(f32[2,4,128,512]{3,2,1,0:T(8,128)S(1)} %bitcast.39), custom_call_target="tpu_custom_call" | custom-call | tf_op jit(solution)/shard_map/pallas_call | solution.py:278
  78.1 0.1 multiply_reduce_fusion.1
  78.2 0.1 copy.15
  78.3 0.1 eq.15
  78.4 0.3 fusion.3.x_ref
  78.7 17.1 %shard_map.79 = bf16[32,8,512]{2,1,0:T(8,128)(2,1)S(1)} custom-call(bf16[32,8,512]{2,1,0:T(8,128)(2,1)S(1)} %fusion.3.x_ref), custom_call_target="tpu_custom_call" | custom-call | tf_op jit(solution)/shard_map/pallas_call | solution.py:59
  95.7 0.1 fusion.4
  95.9 0.1 copy.16
  96.0 0.1 fusion.13
  96.0 0.5 multiply_reduce_fusion
  96.6 0.1 divide_convert_fusion.x_ref
  96.7 13.4 %shard_map.80 = bf16[2,4,128,512]{3,2,1,0:T(8,128)(2,1)S(1)} custom-call(bf16[128,512]{1,0:T(8,128)(2,1)S(1)} %divide_convert_fusion.x_ref), custom_call_target="tpu_custom_call" | custom-call | tf_op jit(solution)/shard_map/pallas_call | solution.py:162
  110.1 0.0 copy-done.8
  110.1 1.3 convolution_convert_fusion.1
  111.4 1.0 concatenate.9
  112.5 1.9 %fusion.2 = bf16[1024,256]{1,0:T(8,128)(2,1)S(1)} fusion(bf16[1024,512]{1,0:T(8,128)(2,1)S(1)} %bitcast.41, bf16[256,512]{1,0:T(8,128)(2,1)} %param.8, f32[1024,256]{1,0:T(8,128)} %copy-done.7), kind=kOutput, calls=%fused_computation.6 | convolution fusion | flops 270794752 | bytes 2883584 | tf_op jit(solution)/shard_map/dot_general | solution.py:355
  114.3 5.8 %fusion = bf16[32,32,8,128]{3,2,1,0:T(8,128)(2,1)S(1)} fusion(bf16[1024,256]{1,0:T(8,128)(2,1)S(1)} %fusion.2, bf16[1024,4096]{1,0:T(8,128)(2,1)} %bitcast.38), kind=kOutput, calls=%fused_computation.3 | convolution fusion | flops 2148532224 | bytes 11010048 | tf_op jit(solution)/shard_map/dot_general | solution.py:365
  120.1 0.6 copy.21
  120.7 0.2 pad_maximum_fusion.p_ref
  120.9 39.7 %shard_map.81 = f32[288,128]{1,0:T(8,128)S(1)} custom-call(bf16[4,8,288,128]{3,2,1,0:T(8,128)(2,1)S(1)} %pad_maximum_fusion.p_ref), custom_call_target="tpu_custom_call" | custom-call | tf_op jit(solution)/shard_map/pallas_call | solution.py:278
  160.6 0.8 copy.18
  161.3 0.6 reshape.80
  (13 shorter events, 0.0 us)
Async XLA Ops:
  0.6 56.7 %copy-start = (bf16[4096,256]{1,0:T(8,128)(2,1)S(1)}, bf16[4096,256]{1,0:T(8,128)(2,1)}, u32[]{:S(2)}) copy-start(bf16[4096,256]{1,0:T(8,128)(2,1)} %param.7) | copy-start | bytes 6291460
  0.6 1.4 copy-start.2
  57.4 3.2 %copy-start.1 = (bf16[2,4,128,4096]{3,2,1,0:T(8,128)(2,1)}, bf16[2,4,128,4096]{3,2,1,0:T(8,128)(2,1)S(1)}, u32[]{:S(2)}) copy-start(bf16[2,4,128,4096]{3,2,1,0:T(8,128)(2,1)S(1)} %shard_map.77) | copy-start | bytes 25165828
  57.4 3.2 %copy-start.6 = (bf16[256,512]{1,0:T(8,128)(2,1)S(1)}, bf16[256,512]{1,0:T(8,128)(2,1)}, u32[]{:S(2)}) copy-start(bf16[256,512]{1,0:T(8,128)(2,1)} %param.8) | copy-start | bytes 786436
  60.6 1.0 copy-start.7
  61.6 16.6 %copy-start.3 = (s32[1,1,32,8]{2,3,1,0:T(8,128)S(1)}, s32[1,1,32,8]{2,3,1,0:T(8,128)}, u32[]{:S(2)}) copy-start(s32[1,1,32,8]{2,3,1,0:T(8,128)} %param.9) | copy-start | bytes 3076
  61.6 34.2 %copy-start.4 = (s32[1,1,32,8]{2,3,1,0:T(8,128)S(1)}, s32[1,1,32,8]{2,3,1,0:T(8,128)}, u32[]{:S(2)}) copy-start(s32[1,1,32,8]{2,3,1,0:T(8,128)} %param.11) | copy-start | bytes 3076
  61.6 34.3 %copy-start.5 = (s32[1,1,32]{2,1,0:T(1,128)S(1)}, s32[1,1,32]{2,1,0:T(1,128)}, u32[]{:S(2)}) copy-start(s32[1,1,32]{2,1,0:T(1,128)} %param.10) | copy-start | bytes 388
  96.0 14.2 %copy-start.8 = (f32[1024,256]{1,0:T(8,128)S(1)}, f32[1024,256]{1,0:T(8,128)}, u32[]{:S(2)}) copy-start(f32[1024,256]{1,0:T(8,128)} %copy-done.7) | copy-start | bytes 3145732

commit v17 on v13

--- a/solution.py
+++ b/solution.py
@@ -90,16 +90,20 @@
     return blocks
 
 
-def _gather_kernel(n_outer, n_inner, axis, x_ref, o_ref, got, send_sems, recv_sems):
+def _gather_kernel(n_outer, n_inner, parts, axis, x_ref, o_ref, got, send_sems, recv_sems):
     me = lax.axis_index(axis)
     ci = lax.rem(me, n_inner)
     yo = lax.div(me, n_inner)
+    rows = x_ref.shape[0] // parts
 
     def device(c, y):
         return {axis: y * n_inner + c}
 
-    def slot(c, y):
-        return c * n_outer + y
+    def slot(c, y, p):
+        return (c * n_outer + y) * parts + p
+
+    def piece(p):
+        return pl.ds(p * rows, rows)
 
     outer_peers = [lax.rem(yo + k, n_outer) for k in range(1, n_outer)]
     inner_peers = [lax.rem(ci + j, n_inner) for j in range(1, n_inner)]
@@ -112,45 +116,48 @@
 
     sends = []
 
-    def send(src, c, y, to):
+    def send(src, c, y, p, to):
         copy = pltpu.make_async_remote_copy(
             src_ref=src,
-            dst_ref=got.at[c, y],
+            dst_ref=got.at[c, y, piece(p)],
             send_sem=send_sems.at[len(sends)],
-            recv_sem=recv_sems.at[slot(c, y)],
+            recv_sem=recv_sems.at[slot(c, y, p)],
             device_id=to,
             device_id_type=MESH,
         )
         copy.start()
         sends.append(copy)
 
-    def receive(c, y):
+    def receive(c, y, p):
         pltpu.make_async_remote_copy(
-            src_ref=x_ref,
-            dst_ref=got.at[c, y],
+            src_ref=x_ref.at[piece(p)],
+            dst_ref=got.at[c, y, piece(p)],
             send_sem=send_sems.at[0],
-            recv_sem=recv_sems.at[slot(c, y)],
+            recv_sem=recv_sems.at[slot(c, y, p)],
             device_id=device(c, y),
             device_id_type=MESH,
         ).wait_recv()
 
-    for y in outer_peers:
-        send(x_ref, ci, yo, device(ci, y))
-    for c in inner_peers:
-        send(x_ref, ci, yo, device(c, yo))
+    for p in range(parts):
+        for y in outer_peers:
+            send(x_ref.at[piece(p)], ci, yo, p, device(ci, y))
+        for c in inner_peers:
+            send(x_ref.at[piece(p)], ci, yo, p, device(c, yo))
     o_ref[ci, yo] = x_ref[...]
-    for k in range(1, n_outer):
-        y = lax.rem(yo + n_outer - k, n_outer)
-        receive(ci, y)
-        for c in inner_peers:
-            send(got.at[ci, y], ci, y, device(c, yo))
-        o_ref[ci, y] = got[ci, y]
+    for p in range(parts):
+        for k in range(1, n_outer):
+            y = lax.rem(yo + n_outer - k, n_outer)
+            receive(ci, y, p)
+            for c in inner_peers:
+                send(got.at[ci, y, piece(p)], ci, y, p, device(c, yo))
+            o_ref[ci, y, piece(p)] = got[ci, y, piece(p)]
     for j in range(1, n_inner):
         c = lax.rem(ci + n_inner - j, n_inner)
-        for k in range(n_outer):
-            y = lax.rem(yo + k, n_outer)
-            receive(c, y)
-            o_ref[c, y] = got[c, y]
+        for p in range(parts):
+            for k in range(n_outer):
+                y = lax.rem(yo + k, n_outer)
+                receive(c, y, p)
+                o_ref[c, y, piece(p)] = got[c, y, piece(p)]
     for copy in sends:
         copy.wait_send()
 
@@ -158,15 +165,16 @@
 def all_gather(x, axis, n, inner, collective_id):
     outer = n // inner
     shape = (inner, outer) + x.shape
+    parts = 2 if x.shape[0] % 32 == 0 else 1
     got = pl.pallas_call(
-        functools.partial(_gather_kernel, outer, inner, axis),
+        functools.partial(_gather_kernel, outer, inner, parts, axis),
         out_shape=jax.ShapeDtypeStruct(shape, x.dtype),
         in_specs=[pl.BlockSpec(memory_space=pltpu.VMEM)],
         out_specs=pl.BlockSpec(memory_space=pltpu.VMEM),
         scratch_shapes=[
             pltpu.VMEM(shape, x.dtype),
-            pltpu.SemaphoreType.DMA((n,)),
-            pltpu.SemaphoreType.DMA((n,)),
+            pltpu.SemaphoreType.DMA((n * parts,)),
+            pltpu.SemaphoreType.DMA((n * parts,)),
         ],
         compiler_params=pltpu.CompilerParams(
             collective_id=collective_id,

time: 162 us -> 161 us (level)
  no operation moved by 1% of the time
where the time goes in v17:
time: 161 us
  Pallas kernels  141 us (88%)
  matrix products  12.5 us (8%)
  local copies, waits for them, and re-layouts  6.05 us (4%)
    pallas_call x2, Pallas kernels, all_gather(): pl.pallas_call(functools.partial(_gather_kernel, outer, inner, parts, axi...  67.3 us
    pallas_call x2, Pallas kernels, reduce_scatter_2d(): pl.pallas_call(functools.partial(_reduce_kernel, n_o, s_o, n_i, s_i, chun...  56.4 us
    pallas_call x1, Pallas kernels, exchange(): pl.pallas_call(functools.partial(_exchange_kernel, n, stride, axis, gathe...  17 us
    dot_general x1, matrix products, per_device(): lax.dot_general(grad_pre, shard_rows, (((0,), (0,)), ((), ())), preferred...  5.77 us
    unnamed x21, local copies, waits for them, and re-layouts  3.73 us

profile of v17, /device:TPU:1, one launch (start us, length us, event | category | flops | bytes accessed | tf_op | source)
XLA Modules:
  0.0 160.7 jit_solution(14445044284742006791)
XLA Ops:
  0.6 0.0 copy-start
  0.7 1.4 copy-done.2
  2.0 53.9 %shard_map.77 = bf16[2,4,128,4096]{3,2,1,0:T(8,128)(2,1)S(1)} custom-call(bf16[128,4096]{1,0:T(8,128)(2,1)S(1)} %copy-done.2), custom_call_target="tpu_custom_call" | custom-call | tf_op jit(solution)/shard_map/pallas_call | solution.py:169
  56.0 0.0 copy-start.1
  56.0 0.0 copy-done
  56.0 0.0 copy-start.6
  56.0 2.3 %fusion.15 = f32[1024,256]{1,0:T(8,128)S(1)} fusion(bf16[1024,4096]{1,0:T(8,128)(2,1)S(1)} %bitcast.37, bf16[4096,256]{1,0:T(8,128)(2,1)S(1)} %copy-done), kind=kOutput, calls=%fused_computation.33 | convolution fusion | flops 2147483648 | bytes 11534336 | tf_op jit(solution)/shard_map/dot_general | solution.py:326
  58.3 0.8 copy-done.1
  59.2 0.0 copy-done.6
  59.2 0.5 fusion.14
  59.6 0.6 copy-done.7
  60.2 16.5 %shard_map.78 = f32[128,512]{1,0:T(8,128)S(1)} custom-call(f32[2,4,128,512]{3,2,1,0:T(8,128)S(1)} %bitcast.39), custom_call_target="tpu_custom_call" | custom-call | tf_op jit(solution)/shard_map/pallas_call | solution.py:285
  76.8 0.1 multiply_reduce_fusion.1
  76.9 0.1 copy.15
  77.0 0.1 eq.15
  77.1 0.3 fusion.3.x_ref
  77.4 17.0 %shard_map.79 = bf16[32,8,512]{2,1,0:T(8,128)(2,1)S(1)} custom-call(bf16[32,8,512]{2,1,0:T(8,128)(2,1)S(1)} %fusion.3.x_ref), custom_call_target="tpu_custom_call" | custom-call | tf_op jit(solution)/shard_map/pallas_call | solution.py:58
  94.4 0.1 fusion.4
  94.5 0.1 copy.16
  94.6 0.1 fusion.13
  94.7 0.5 multiply_reduce_fusion
  95.2 0.1 divide_convert_fusion.x_ref
  95.4 13.4 %shard_map.80 = bf16[2,4,128,512]{3,2,1,0:T(8,128)(2,1)S(1)} custom-call(bf16[128,512]{1,0:T(8,128)(2,1)S(1)} %divide_convert_fusion.x_ref), custom_call_target="tpu_custom_call" | custom-call | tf_op jit(solution)/shard_map/pallas_call | solution.py:169
  108.8 1.3 convolution_convert_fusion.1
  110.0 1.0 concatenate.9
  111.1 1.9 %fusion.2 = bf16[1024,256]{1,0:T(8,128)(2,1)S(1)} fusion(bf16[1024,512]{1,0:T(8,128)(2,1)S(1)} %bitcast.41, bf16[256,512]{1,0:T(8,128)(2,1)} %param.8, f32[1024,256]{1,0:T(8,128)} %copy-done.7), kind=kOutput, calls=%fused_computation.6 | convolution fusion | flops 270794752 | bytes 2883584 | tf_op jit(solution)/shard_map/dot_general | solution.py:362
  112.9 5.8 %fusion = bf16[32,32,8,128]{3,2,1,0:T(8,128)(2,1)S(1)} fusion(bf16[1024,256]{1,0:T(8,128)(2,1)S(1)} %fusion.2, bf16[1024,4096]{1,0:T(8,128)(2,1)} %bitcast.38), kind=kOutput, calls=%fused_computation.3 | convolution fusion | flops 2148532224 | bytes 11010048 | tf_op jit(solution)/shard_map/dot_general | solution.py:372
  118.7 0.6 copy.21
  119.3 0.2 pad_maximum_fusion.p_ref
  119.5 39.9 %shard_map.81 = f32[288,128]{1,0:T(8,128)S(1)} custom-call(bf16[4,8,288,128]{3,2,1,0:T(8,128)(2,1)S(1)} %pad_maximum_fusion.p_ref), custom_call_target="tpu_custom_call" | custom-call | tf_op jit(solution)/shard_map/pallas_call | solution.py:285
  159.4 0.8 copy.18
  160.1 0.6 reshape.80
  (13 shorter events, 0.0 us)
Async XLA Ops:
  0.6 55.3 %copy-start = (bf16[4096,256]{1,0:T(8,128)(2,1)S(1)}, bf16[4096,256]{1,0:T(8,128)(2,1)}, u32[]{:S(2)}) copy-start(bf16[4096,256]{1,0:T(8,128)(2,1)} %param.7) | copy-start | bytes 6291460
  0.6 1.4 copy-start.2
  56.0 3.2 %copy-start.1 = (bf16[2,4,128,4096]{3,2,1,0:T(8,128)(2,1)}, bf16[2,4,128,4096]{3,2,1,0:T(8,128)(2,1)S(1)}, u32[]{:S(2)}) copy-start(bf16[2,4,128,4096]{3,2,1,0:T(8,128)(2,1)S(1)} %shard_map.77) | copy-start | bytes 25165828
  56.0 3.2 %copy-start.6 = (bf16[256,512]{1,0:T(8,128)(2,1)S(1)}, bf16[256,512]{1,0:T(8,128)(2,1)}, u32[]{:S(2)}) copy-start(bf16[256,512]{1,0:T(8,128)(2,1)} %param.8) | copy-start | bytes 786436
  59.2 1.0 copy-start.7
  60.2 16.7 %copy-start.3 = (s32[1,1,32,8]{2,3,1,0:T(8,128)S(1)}, s32[1,1,32,8]{2,3,1,0:T(8,128)}, u32[]{:S(2)}) copy-start(s32[1,1,32,8]{2,3,1,0:T(8,128)} %param.9) | copy-start | bytes 3076
  60.2 34.3 %copy-start.4 = (s32[1,1,32,8]{2,3,1,0:T(8,128)S(1)}, s32[1,1,32,8]{2,3,1,0:T(8,128)}, u32[]{:S(2)}) copy-start(s32[1,1,32,8]{2,3,1,0:T(8,128)} %param.11) | copy-start | bytes 3076
  60.2 34.4 %copy-start.5 = (s32[1,1,32]{2,1,0:T(1,128)S(1)}, s32[1,1,32]{2,1,0:T(1,128)}, u32[]{:S(2)}) copy-start(s32[1,1,32]{2,1,0:T(1,128)} %param.10) | copy-start | bytes 388
  94.6 14.1 %copy-start.8 = (f32[1024,256]{1,0:T(8,128)S(1)}, f32[1024,256]{1,0:T(8,128)}, u32[]{:S(2)}) copy-start(f32[1024,256]{1,0:T(8,128)} %copy-done.7) | copy-start | bytes 3145732

commit v18 on v17

--- a/solution.py
+++ b/solution.py
@@ -165,7 +165,7 @@
 def all_gather(x, axis, n, inner, collective_id):
     outer = n // inner
     shape = (inner, outer) + x.shape
-    parts = 2 if x.shape[0] % 32 == 0 else 1
+    parts = next(p for p in (4, 2, 1) if x.shape[0] % (16 * p) == 0)
     got = pl.pallas_call(
         functools.partial(_gather_kernel, outer, inner, parts, axis),
         out_shape=jax.ShapeDtypeStruct(shape, x.dtype),

time: 161 us -> 161 us (level)
  no operation moved by 1% of the time
where the time goes in v18:
time: 161 us; the launch traced here: 160 us
  Pallas kernels  140 us (87%)
  matrix products  12.5 us (8%)
  local copies, waits for them, and re-layouts  6.05 us (4%)
    pallas_call x2, Pallas kernels, all_gather(): pl.pallas_call(functools.partial(_gather_kernel, outer, inner, parts, axi...  67 us
    pallas_call x2, Pallas kernels, reduce_scatter_2d(): pl.pallas_call(functools.partial(_reduce_kernel, n_o, s_o, n_i, s_i, chun...  56.4 us
    pallas_call x1, Pallas kernels, exchange(): pl.pallas_call(functools.partial(_exchange_kernel, n, stride, axis, gathe...  17 us
    dot_general x1, matrix products, per_device(): lax.dot_general(grad_pre, shard_rows, (((0,), (0,)), ((), ())), preferred...  5.77 us
    unnamed x21, local copies, waits for them, and re-layouts  3.73 us

profile of v18, /device:TPU:1, one launch (start us, length us, event | category | flops | bytes accessed | tf_op | source)
XLA Modules:
  0.0 160.5 jit_solution(8971516281322078121)
XLA Ops:
  0.6 0.0 copy-start
  0.6 0.0 copy-start.2
  0.7 1.4 copy-done.2
  2.0 53.5 %shard_map.77 = bf16[2,4,128,4096]{3,2,1,0:T(8,128)(2,1)S(1)} custom-call(bf16[128,4096]{1,0:T(8,128)(2,1)S(1)} %copy-done.2), custom_call_target="tpu_custom_call" | custom-call | tf_op jit(solution)/shard_map/pallas_call | solution.py:169
  55.6 0.0 copy-start.1
  55.6 0.0 copy-done
  55.6 0.0 copy-start.6
  55.6 2.3 %fusion.15 = f32[1024,256]{1,0:T(8,128)S(1)} fusion(bf16[1024,4096]{1,0:T(8,128)(2,1)S(1)} %bitcast.37, bf16[4096,256]{1,0:T(8,128)(2,1)S(1)} %copy-done), kind=kOutput, calls=%fused_computation.33 | convolution fusion | flops 2147483648 | bytes 11534336 | tf_op jit(solution)/shard_map/dot_general | solution.py:326
  57.9 0.8 copy-done.1
  58.8 0.5 fusion.14
  59.2 0.6 copy-done.7
  59.8 16.6 %shard_map.78 = f32[128,512]{1,0:T(8,128)S(1)} custom-call(f32[2,4,128,512]{3,2,1,0:T(8,128)S(1)} %bitcast.39), custom_call_target="tpu_custom_call" | custom-call | tf_op jit(solution)/shard_map/pallas_call | solution.py:285
  76.4 0.1 multiply_reduce_fusion.1
  76.5 0.1 copy.15
  76.6 0.1 eq.15
  76.7 0.3 fusion.3.x_ref
  77.0 17.0 %shard_map.79 = bf16[32,8,512]{2,1,0:T(8,128)(2,1)S(1)} custom-call(bf16[32,8,512]{2,1,0:T(8,128)(2,1)S(1)} %fusion.3.x_ref), custom_call_target="tpu_custom_call" | custom-call | tf_op jit(solution)/shard_map/pallas_call | solution.py:58
  94.0 0.1 fusion.4
  94.2 0.1 copy.16
  94.3 0.1 fusion.13
  94.3 0.5 multiply_reduce_fusion
  94.9 0.1 divide_convert_fusion.x_ref
  95.0 13.5 %shard_map.80 = bf16[2,4,128,512]{3,2,1,0:T(8,128)(2,1)S(1)} custom-call(bf16[128,512]{1,0:T(8,128)(2,1)S(1)} %divide_convert_fusion.x_ref), custom_call_target="tpu_custom_call" | custom-call | tf_op jit(solution)/shard_map/pallas_call | solution.py:169
  108.5 1.3 convolution_convert_fusion.1
  109.8 1.0 concatenate.9
  110.8 1.9 %fusion.2 = bf16[1024,256]{1,0:T(8,128)(2,1)S(1)} fusion(bf16[1024,512]{1,0:T(8,128)(2,1)S(1)} %bitcast.41, bf16[256,512]{1,0:T(8,128)(2,1)} %param.8, f32[1024,256]{1,0:T(8,128)} %copy-done.7), kind=kOutput, calls=%fused_computation.6 | convolution fusion | flops 270794752 | bytes 2883584 | tf_op jit(solution)/shard_map/dot_general | solution.py:362
  112.7 5.8 %fusion = bf16[32,32,8,128]{3,2,1,0:T(8,128)(2,1)S(1)} fusion(bf16[1024,256]{1,0:T(8,128)(2,1)S(1)} %fusion.2, bf16[1024,4096]{1,0:T(8,128)(2,1)} %bitcast.38), kind=kOutput, calls=%fused_computation.3 | convolution fusion | flops 2148532224 | bytes 11010048 | tf_op jit(solution)/shard_map/dot_general | solution.py:372
  118.5 0.6 copy.21
  119.0 0.2 pad_maximum_fusion.p_ref
  119.2 39.8 %shard_map.81 = f32[288,128]{1,0:T(8,128)S(1)} custom-call(bf16[4,8,288,128]{3,2,1,0:T(8,128)(2,1)S(1)} %pad_maximum_fusion.p_ref), custom_call_target="tpu_custom_call" | custom-call | tf_op jit(solution)/shard_map/pallas_call | solution.py:285
  159.1 0.8 copy.18
  159.9 0.6 reshape.80
  (13 shorter events, 0.0 us)
Async XLA Ops:
  0.6 54.9 %copy-start = (bf16[4096,256]{1,0:T(8,128)(2,1)S(1)}, bf16[4096,256]{1,0:T(8,128)(2,1)}, u32[]{:S(2)}) copy-start(bf16[4096,256]{1,0:T(8,128)(2,1)} %param.7) | copy-start | bytes 6291460
  0.6 1.4 copy-start.2
  55.6 3.2 %copy-start.1 = (bf16[2,4,128,4096]{3,2,1,0:T(8,128)(2,1)}, bf16[2,4,128,4096]{3,2,1,0:T(8,128)(2,1)S(1)}, u32[]{:S(2)}) copy-start(bf16[2,4,128,4096]{3,2,1,0:T(8,128)(2,1)S(1)} %shard_map.77) | copy-start | bytes 25165828
  55.6 3.2 %copy-start.6 = (bf16[256,512]{1,0:T(8,128)(2,1)S(1)}, bf16[256,512]{1,0:T(8,128)(2,1)}, u32[]{:S(2)}) copy-start(bf16[256,512]{1,0:T(8,128)(2,1)} %param.8) | copy-start | bytes 786436
  58.8 1.0 copy-start.7
  59.8 16.7 %copy-start.3 = (s32[1,1,32,8]{2,3,1,0:T(8,128)S(1)}, s32[1,1,32,8]{2,3,1,0:T(8,128)}, u32[]{:S(2)}) copy-start(s32[1,1,32,8]{2,3,1,0:T(8,128)} %param.9) | copy-start | bytes 3076
  59.8 34.4 %copy-start.4 = (s32[1,1,32,8]{2,3,1,0:T(8,128)S(1)}, s32[1,1,32,8]{2,3,1,0:T(8,128)}, u32[]{:S(2)}) copy-start(s32[1,1,32,8]{2,3,1,0:T(8,128)} %param.11) | copy-start | bytes 3076
  59.8 34.5 %copy-start.5 = (s32[1,1,32]{2,1,0:T(1,128)S(1)}, s32[1,1,32]{2,1,0:T(1,128)}, u32[]{:S(2)}) copy-start(s32[1,1,32]{2,1,0:T(1,128)} %param.10) | copy-start | bytes 388
  94.3 14.2 %copy-start.8 = (f32[1024,256]{1,0:T(8,128)S(1)}, f32[1024,256]{1,0:T(8,128)}, u32[]{:S(2)}) copy-start(f32[1024,256]{1,0:T(8,128)} %copy-done.7) | copy-start | bytes 3145732

commit v19 on v18

--- a/solution.py
+++ b/solution.py
@@ -165,7 +165,7 @@
 def all_gather(x, axis, n, inner, collective_id):
     outer = n // inner
     shape = (inner, outer) + x.shape
-    parts = next(p for p in (4, 2, 1) if x.shape[0] % (16 * p) == 0)
+    parts = next(p for p in (8, 4, 2, 1) if x.shape[0] % (16 * p) == 0)
     got = pl.pallas_call(
         functools.partial(_gather_kernel, outer, inner, parts, axis),
         out_shape=jax.ShapeDtypeStruct(shape, x.dtype),

time: 161 us -> 161 us (level)
  no operation moved by 1% of the time
where the time goes in v19:
time: 161 us
  Pallas kernels  141 us (88%)
  matrix products  12.5 us (8%)
  local copies, waits for them, and re-layouts  6.05 us (4%)
    pallas_call x2, Pallas kernels, all_gather(): pl.pallas_call(functools.partial(_gather_kernel, outer, inner, parts, axi...  67.8 us
    pallas_call x2, Pallas kernels, reduce_scatter_2d(): pl.pallas_call(functools.partial(_reduce_kernel, n_o, s_o, n_i, s_i, chun...  56.4 us
    pallas_call x1, Pallas kernels, exchange(): pl.pallas_call(functools.partial(_exchange_kernel, n, stride, axis, gathe...  16.7 us
    dot_general x1, matrix products, per_device(): lax.dot_general(grad_pre, shard_rows, (((0,), (0,)), ((), ())), preferred...  5.77 us
    unnamed x21, local copies, waits for them, and re-layouts  3.73 us

profile of v19, /device:TPU:1, one launch (start us, length us, event | category | flops | bytes accessed | tf_op | source)
XLA Modules:
  0.0 161.0 jit_solution(2153379776358891143)
XLA Ops:
  0.6 0.0 copy-start
  0.6 0.0 copy-start.2
  0.7 1.4 copy-done.2
  2.0 53.9 %shard_map.77 = bf16[2,4,128,4096]{3,2,1,0:T(8,128)(2,1)S(1)} custom-call(bf16[128,4096]{1,0:T(8,128)(2,1)S(1)} %copy-done.2), custom_call_target="tpu_custom_call" | custom-call | tf_op jit(solution)/shard_map/pallas_call | solution.py:169
  55.9 0.0 copy-start.1
  56.0 0.0 copy-start.6
  56.0 2.3 %fusion.15 = f32[1024,256]{1,0:T(8,128)S(1)} fusion(bf16[1024,4096]{1,0:T(8,128)(2,1)S(1)} %bitcast.37, bf16[4096,256]{1,0:T(8,128)(2,1)S(1)} %copy-done), kind=kOutput, calls=%fused_computation.33 | convolution fusion | flops 2147483648 | bytes 11534336 | tf_op jit(solution)/shard_map/dot_general | solution.py:326
  58.3 0.8 copy-done.1
  59.2 0.5 fusion.14
  59.6 0.6 copy-done.7
  60.2 16.5 %shard_map.78 = f32[128,512]{1,0:T(8,128)S(1)} custom-call(f32[2,4,128,512]{3,2,1,0:T(8,128)S(1)} %bitcast.39), custom_call_target="tpu_custom_call" | custom-call | tf_op jit(solution)/shard_map/pallas_call | solution.py:285
  76.8 0.1 multiply_reduce_fusion.1
  76.9 0.0 copy-done.3
  76.9 0.1 copy.15
  77.0 0.1 eq.15
  77.1 0.3 fusion.3.x_ref
  77.4 16.7 %shard_map.79 = bf16[32,8,512]{2,1,0:T(8,128)(2,1)S(1)} custom-call(bf16[32,8,512]{2,1,0:T(8,128)(2,1)S(1)} %fusion.3.x_ref), custom_call_target="tpu_custom_call" | custom-call | tf_op jit(solution)/shard_map/pallas_call | solution.py:58
  94.1 0.1 fusion.4
  94.2 0.1 copy.16
  94.3 0.1 fusion.13
  94.4 0.5 multiply_reduce_fusion
  94.9 0.1 divide_convert_fusion.x_ref
  95.1 13.9 %shard_map.80 = bf16[2,4,128,512]{3,2,1,0:T(8,128)(2,1)S(1)} custom-call(bf16[128,512]{1,0:T(8,128)(2,1)S(1)} %divide_convert_fusion.x_ref), custom_call_target="tpu_custom_call" | custom-call | tf_op jit(solution)/shard_map/pallas_call | solution.py:169
  109.0 1.3 convolution_convert_fusion.1
  110.3 1.0 concatenate.9
  111.3 1.9 %fusion.2 = bf16[1024,256]{1,0:T(8,128)(2,1)S(1)} fusion(bf16[1024,512]{1,0:T(8,128)(2,1)S(1)} %bitcast.41, bf16[256,512]{1,0:T(8,128)(2,1)} %param.8, f32[1024,256]{1,0:T(8,128)} %copy-done.7), kind=kOutput, calls=%fused_computation.6 | convolution fusion | flops 270794752 | bytes 2883584 | tf_op jit(solution)/shard_map/dot_general | solution.py:362
  113.2 5.8 %fusion = bf16[32,32,8,128]{3,2,1,0:T(8,128)(2,1)S(1)} fusion(bf16[1024,256]{1,0:T(8,128)(2,1)S(1)} %fusion.2, bf16[1024,4096]{1,0:T(8,128)(2,1)} %bitcast.38), kind=kOutput, calls=%fused_computation.3 | convolution fusion | flops 2148532224 | bytes 11010048 | tf_op jit(solution)/shard_map/dot_general | solution.py:372
  119.0 0.6 copy.21
  119.5 0.2 pad_maximum_fusion.p_ref
  119.7 39.8 %shard_map.81 = f32[288,128]{1,0:T(8,128)S(1)} custom-call(bf16[4,8,288,128]{3,2,1,0:T(8,128)(2,1)S(1)} %pad_maximum_fusion.p_ref), custom_call_target="tpu_custom_call" | custom-call | tf_op jit(solution)/shard_map/pallas_call | solution.py:285
  159.6 0.8 copy.18
  160.3 0.6 reshape.80
  (13 shorter events, 0.0 us)
Async XLA Ops:
  0.6 55.3 %copy-start = (bf16[4096,256]{1,0:T(8,128)(2,1)S(1)}, bf16[4096,256]{1,0:T(8,128)(2,1)}, u32[]{:S(2)}) copy-start(bf16[4096,256]{1,0:T(8,128)(2,1)} %param.7) | copy-start | bytes 6291460
  0.6 1.4 copy-start.2
  55.9 3.2 %copy-start.1 = (bf16[2,4,128,4096]{3,2,1,0:T(8,128)(2,1)}, bf16[2,4,128,4096]{3,2,1,0:T(8,128)(2,1)S(1)}, u32[]{:S(2)}) copy-start(bf16[2,4,128,4096]{3,2,1,0:T(8,128)(2,1)S(1)} %shard_map.77) | copy-start | bytes 25165828
  56.0 3.2 %copy-start.6 = (bf16[256,512]{1,0:T(8,128)(2,1)S(1)}, bf16[256,512]{1,0:T(8,128)(2,1)}, u32[]{:S(2)}) copy-start(bf16[256,512]{1,0:T(8,128)(2,1)} %param.8) | copy-start | bytes 786436
  59.2 1.0 copy-start.7
  60.2 16.7 %copy-start.3 = (s32[1,1,32,8]{2,3,1,0:T(8,128)S(1)}, s32[1,1,32,8]{2,3,1,0:T(8,128)}, u32[]{:S(2)}) copy-start(s32[1,1,32,8]{2,3,1,0:T(8,128)} %param.9) | copy-start | bytes 3076
  60.2 34.0 %copy-start.4 = (s32[1,1,32,8]{2,3,1,0:T(8,128)S(1)}, s32[1,1,32,8]{2,3,1,0:T(8,128)}, u32[]{:S(2)}) copy-start(s32[1,1,32,8]{2,3,1,0:T(8,128)} %param.11) | copy-start | bytes 3076
  60.2 34.1 %copy-start.5 = (s32[1,1,32]{2,1,0:T(1,128)S(1)}, s32[1,1,32]{2,1,0:T(1,128)}, u32[]{:S(2)}) copy-start(s32[1,1,32]{2,1,0:T(1,128)} %param.10) | copy-start | bytes 388
  94.3 14.7 %copy-start.8 = (f32[1024,256]{1,0:T(8,128)S(1)}, f32[1024,256]{1,0:T(8,128)}, u32[]{:S(2)}) copy-start(f32[1024,256]{1,0:T(8,128)} %copy-done.7) | copy-start | bytes 3145732

commit v20 on v18

--- a/solution.py
+++ b/solution.py
@@ -185,14 +185,18 @@
     return got.reshape((n * x.shape[0],) + x.shape[1:])
 
 
-def _reduce_kernel(n_o, s_o, n_i, s_i, chunks, axis, p_ref, o_ref, g1, b_ref, g2, s1, r1, s2, r2):
+def _reduce_kernel(n_o, s_o, n_i, s_i, chunks, halves, axis, p_ref, o_ref, g1, b_ref, g2, s1, r1, s2, r2):
     me = lax.axis_index(axis)
     zi = lax.rem(lax.div(me, s_i), n_i)
     xo = lax.rem(lax.div(me, s_o), n_o)
     zc = n_i // chunks
+    rh = p_ref.shape[2] // halves
 
     def device(x, z):
         return {axis: me + (x - xo) * s_o + (z - zi) * s_i}
+
+    def half(h):
+        return pl.ds(h * rh, rh)
 
     barrier = pltpu.get_barrier_semaphore()
     for k in range(1, n_o):
@@ -205,85 +209,83 @@
         )
     pl.semaphore_wait(barrier, n_o + n_i - 2)
 
-    def along_x(k, c, to, dst_x):
+    def along_x(k, c, h, to, dst_x):
         blocks = pl.ds(c * zc, zc)
         return pltpu.make_async_remote_copy(
-            src_ref=p_ref.at[to, blocks],
-            dst_ref=g1.at[dst_x, blocks],
-            send_sem=s1.at[k, c],
-            recv_sem=r1.at[k, c],
+            src_ref=p_ref.at[to, blocks, half(h)],
+            dst_ref=g1.at[dst_x, blocks, half(h)],
+            send_sem=s1.at[k, c * halves + h],
+            recv_sem=r1.at[k, c * halves + h],
             device_id=device(to, zi),
             device_id_type=MESH,
         )
 
-    def along_z(k, z):
+    def along_z(k, z, h):
         return pltpu.make_async_remote_copy(
-            src_ref=b_ref.at[z],
-            dst_ref=g2.at[zi],
-            send_sem=s2.at[k],
-            recv_sem=r2.at[k],
+            src_ref=b_ref.at[z, half(h)],
+            dst_ref=g2.at[zi, half(h)],
+            send_sem=s2.at[k, h],
+            recv_sem=r2.at[k, h],
             device_id=device(xo, z),
             device_id_type=MESH,
         )
 
     first = []
     for c in range(chunks):
-        for k in range(1, n_o):
-            copy = along_x(k, c, lax.rem(xo + k, n_o), xo)
-            copy.start()
-            first.append(copy)
+        for h in range(halves):
+            for k in range(1, n_o):
+                copy = along_x(k, c, h, lax.rem(xo + k, n_o), xo)
+                copy.start()
+                first.append(copy)
     sources = [lax.rem(xo + n_o - k, n_o) for k in range(1, n_o)]
     for c in range(chunks):
-        for k in range(1, n_o):
+        for h in range(halves):
+            for k in range(1, n_o):
+                along_x(k, c, h, sources[k - 1], sources[k - 1]).wait_recv()
+            for z in range(c * zc, (c + 1) * zc):
+                total = p_ref[xo, z, half(h)].astype(jnp.float32)
+                for src in sources:
+                    total = total + g1[src, z, half(h)].astype(jnp.float32)
+                b_ref[z, half(h)] = total.astype(b_ref.dtype)
+                offset = lax.rem(z - zi + n_i, n_i)
+
+                @pl.when(offset == 0)
+                def _():
+                    o_ref[half(h)] = total
+
+                @pl.when(offset != 0)
+                def _():
+                    along_z(offset, z, h).start()
+
+    for k in range(1, n_i):
+        src = lax.rem(zi + n_i - k, n_i)
+        for h in range(halves):
             pltpu.make_async_remote_copy(
-                src_ref=p_ref.at[sources[k - 1], pl.ds(c * zc, zc)],
-                dst_ref=g1.at[sources[k - 1], pl.ds(c * zc, zc)],
-                send_sem=s1.at[k, c],
-                recv_sem=r1.at[k, c],
-                device_id=device(sources[k - 1], zi),
+                src_ref=b_ref.at[src, half(h)],
+                dst_ref=g2.at[src, half(h)],
+                send_sem=s2.at[k, h],
+                recv_sem=r2.at[k, h],
+                device_id=device(xo, src),
                 device_id_type=MESH,
             ).wait_recv()
-        for z in range(c * zc, (c + 1) * zc):
-            total = p_ref[xo, z].astype(jnp.float32)
-            for src in sources:
-                total = total + g1[src, z].astype(jnp.float32)
-            b_ref[z] = total.astype(b_ref.dtype)
-            offset = lax.rem(z - zi + n_i, n_i)
-
-            @pl.when(offset == 0)
-            def _():
-                o_ref[...] = total
-
-            @pl.when(offset != 0)
-            def _():
-                along_z(offset, z).start()
-
-    for k in range(1, n_i):
-        src = lax.rem(zi + n_i - k, n_i)
-        pltpu.make_async_remote_copy(
-            src_ref=b_ref.at[src],
-            dst_ref=g2.at[src],
-            send_sem=s2.at[k],
-            recv_sem=r2.at[k],
-            device_id=device(xo, src),
-            device_id_type=MESH,
-        ).wait_recv()
-        o_ref[...] = o_ref[...] + g2[src].astype(jnp.float32)
+            o_ref[half(h)] = o_ref[half(h)] + g2[src, half(h)].astype(jnp.float32)
     for copy in first:
         copy.wait_send()
     for z in range(n_i):
         offset = lax.rem(z - zi + n_i, n_i)
-
-        @pl.when(offset != 0)
-        def _():
-            along_z(offset, z).wait_send()
+        for h in range(halves):
+
+            @pl.when(offset != 0)
+            def _():
+                along_z(offset, z, h).wait_send()
 
 
 def reduce_scatter_2d(x, axis, first, second, collective_id):
     (n_o, s_o), (n_i, s_i) = first, second
     chunks = next(c for c in (8, 4, 2, 1) if n_i % c == 0)
+    halves = 2 if x.shape[2] % 32 == 0 else 1
     return pl.pallas_call(
-        functools.partial(_reduce_kernel, n_o, s_o, n_i, s_i, chunks, axis),
+        functools.partial(_reduce_kernel, n_o, s_o, n_i, s_i, chunks, halves, axis),
         out_shape=jax.ShapeDtypeStruct(x.shape[2:], jnp.float32),
         in_specs=[pl.BlockSpec(memory_space=pltpu.VMEM)],
         out_specs=pl.BlockSpec(memory_space=pltpu.VMEM),
@@ -291,10 +293,10 @@
             pltpu.VMEM(x.shape, x.dtype),
             pltpu.VMEM(x.shape[1:], x.dtype),
             pltpu.VMEM(x.shape[1:], x.dtype),
-            pltpu.SemaphoreType.DMA((n_o, chunks)),
-            pltpu.SemaphoreType.DMA((n_o, chunks)),
-            pltpu.SemaphoreType.DMA((n_i,)),
-            pltpu.SemaphoreType.DMA((n_i,)),
+            pltpu.SemaphoreType.DMA((n_o, chunks * halves)),
+            pltpu.SemaphoreType.DMA((n_o, chunks * halves)),
+            pltpu.SemaphoreType.DMA((n_i, halves)),
+            pltpu.SemaphoreType.DMA((n_i, halves)),
         ],
         compiler_params=pltpu.CompilerParams(
             collective_id=collective_id,

time: 161 us -> 160 us (level)
  no operation moved by 1% of the time
where the time goes in v20:
time: 160 us
  Pallas kernels  140 us (88%)
  matrix products  12.5 us (8%)
  local copies, waits for them, and re-layouts  6.05 us (4%)
    pallas_call x2, Pallas kernels, all_gather(): pl.pallas_call(functools.partial(_gather_kernel, outer, inner, parts, axi...  67 us
    pallas_call x2, Pallas kernels, reduce_scatter_2d(): pl.pallas_call(functools.partial(_reduce_kernel, n_o, s_o, n_i, s_i, chun...  56 us
    pallas_call x1, Pallas kernels, exchange(): pl.pallas_call(functools.partial(_exchange_kernel, n, stride, axis, gathe...  17 us
    dot_general x1, matrix products, per_device(): lax.dot_general(grad_pre, shard_rows, (((0,), (0,)), ((), ())), preferred...  5.77 us
    unnamed x21, local copies, waits for them, and re-layouts  3.73 us

profile of v20, /device:TPU:1, one launch (start us, length us, event | category | flops | bytes accessed | tf_op | source)
XLA Modules:
  0.0 160.0 jit_solution(5100135765881646456)
XLA Ops:
  0.6 0.0 copy-start
  0.6 0.0 copy-start.2
  0.7 1.4 copy-done.2
  2.0 53.5 %shard_map.77 = bf16[2,4,128,4096]{3,2,1,0:T(8,128)(2,1)S(1)} custom-call(bf16[128,4096]{1,0:T(8,128)(2,1)S(1)} %copy-done.2), custom_call_target="tpu_custom_call" | custom-call | tf_op jit(solution)/shard_map/pallas_call | solution.py:169
  55.6 0.0 copy-start.1
  55.6 0.0 copy-done
  55.6 0.0 copy-start.6
  55.6 2.3 %fusion.15 = f32[1024,256]{1,0:T(8,128)S(1)} fusion(bf16[1024,4096]{1,0:T(8,128)(2,1)S(1)} %bitcast.37, bf16[4096,256]{1,0:T(8,128)(2,1)S(1)} %copy-done), kind=kOutput, calls=%fused_computation.33 | convolution fusion | flops 2147483648 | bytes 11534336 | tf_op jit(solution)/shard_map/dot_general | solution.py:328
  57.9 0.8 copy-done.1
  58.8 0.5 fusion.14
  59.2 0.6 copy-done.7
  59.8 16.6 %shard_map.78 = f32[128,512]{1,0:T(8,128)S(1)} custom-call(f32[2,4,128,512]{3,2,1,0:T(8,128)S(1)} %bitcast.39), custom_call_target="tpu_custom_call" | custom-call | tf_op jit(solution)/shard_map/pallas_call | solution.py:287
  76.4 0.1 multiply_reduce_fusion.1
  76.6 0.1 copy.15
  76.6 0.1 eq.15
  76.7 0.3 fusion.3.x_ref
  77.0 17.0 %shard_map.79 = bf16[32,8,512]{2,1,0:T(8,128)(2,1)S(1)} custom-call(bf16[32,8,512]{2,1,0:T(8,128)(2,1)S(1)} %fusion.3.x_ref), custom_call_target="tpu_custom_call" | custom-call | tf_op jit(solution)/shard_map/pallas_call | solution.py:58
  94.1 0.1 fusion.4
  94.2 0.1 copy.16
  94.3 0.1 fusion.13
  94.4 0.5 multiply_reduce_fusion
  94.9 0.1 divide_convert_fusion.x_ref
  95.0 13.5 %shard_map.80 = bf16[2,4,128,512]{3,2,1,0:T(8,128)(2,1)S(1)} custom-call(bf16[128,512]{1,0:T(8,128)(2,1)S(1)} %divide_convert_fusion.x_ref), custom_call_target="tpu_custom_call" | custom-call | tf_op jit(solution)/shard_map/pallas_call | solution.py:169
  108.5 1.3 convolution_convert_fusion.1
  109.8 1.0 concatenate.9
  110.8 1.9 %fusion.2 = bf16[1024,256]{1,0:T(8,128)(2,1)S(1)} fusion(bf16[1024,512]{1,0:T(8,128)(2,1)S(1)} %bitcast.41, bf16[256,512]{1,0:T(8,128)(2,1)} %param.8, f32[1024,256]{1,0:T(8,128)} %copy-done.7), kind=kOutput, calls=%fused_computation.6 | convolution fusion | flops 270794752 | bytes 2883584 | tf_op jit(solution)/shard_map/dot_general | solution.py:364
  112.7 5.8 %fusion = bf16[32,32,8,128]{3,2,1,0:T(8,128)(2,1)S(1)} fusion(bf16[1024,256]{1,0:T(8,128)(2,1)S(1)} %fusion.2, bf16[1024,4096]{1,0:T(8,128)(2,1)} %bitcast.38), kind=kOutput, calls=%fused_computation.3 | convolution fusion | flops 2148532224 | bytes 11010048 | tf_op jit(solution)/shard_map/dot_general | solution.py:374
  118.5 0.6 copy.21
  119.1 0.2 pad_maximum_fusion.p_ref
  119.2 39.4 %shard_map.81 = f32[288,128]{1,0:T(8,128)S(1)} custom-call(bf16[4,8,288,128]{3,2,1,0:T(8,128)(2,1)S(1)} %pad_maximum_fusion.p_ref), custom_call_target="tpu_custom_call" | custom-call | tf_op jit(solution)/shard_map/pallas_call | solution.py:287
  158.7 0.8 copy.18
  159.4 0.6 reshape.80
  (13 shorter events, 0.0 us)
Async XLA Ops:
  0.6 54.9 %copy-start = (bf16[4096,256]{1,0:T(8,128)(2,1)S(1)}, bf16[4096,256]{1,0:T(8,128)(2,1)}, u32[]{:S(2)}) copy-start(bf16[4096,256]{1,0:T(8,128)(2,1)} %param.7) | copy-start | bytes 6291460
  0.6 1.4 copy-start.2
  55.6 3.2 %copy-start.1 = (bf16[2,4,128,4096]{3,2,1,0:T(8,128)(2,1)}, bf16[2,4,128,4096]{3,2,1,0:T(8,128)(2,1)S(1)}, u32[]{:S(2)}) copy-start(bf16[2,4,128,4096]{3,2,1,0:T(8,128)(2,1)S(1)} %shard_map.77) | copy-start | bytes 25165828
  55.6 3.2 %copy-start.6 = (bf16[256,512]{1,0:T(8,128)(2,1)S(1)}, bf16[256,512]{1,0:T(8,128)(2,1)}, u32[]{:S(2)}) copy-start(bf16[256,512]{1,0:T(8,128)(2,1)} %param.8) | copy-start | bytes 786436
  58.8 1.0 copy-start.7
  59.8 16.7 %copy-start.3 = (s32[1,1,32,8]{2,3,1,0:T(8,128)S(1)}, s32[1,1,32,8]{2,3,1,0:T(8,128)}, u32[]{:S(2)}) copy-start(s32[1,1,32,8]{2,3,1,0:T(8,128)} %param.9) | copy-start | bytes 3076
  59.8 34.4 %copy-start.4 = (s32[1,1,32,8]{2,3,1,0:T(8,128)S(1)}, s32[1,1,32,8]{2,3,1,0:T(8,128)}, u32[]{:S(2)}) copy-start(s32[1,1,32,8]{2,3,1,0:T(8,128)} %param.11) | copy-start | bytes 3076
  59.8 34.5 %copy-start.5 = (s32[1,1,32]{2,1,0:T(1,128)S(1)}, s32[1,1,32]{2,1,0:T(1,128)}, u32[]{:S(2)}) copy-start(s32[1,1,32]{2,1,0:T(1,128)} %param.10) | copy-start | bytes 388
  94.3 14.2 %copy-start.8 = (f32[1024,256]{1,0:T(8,128)S(1)}, f32[1024,256]{1,0:T(8,128)}, u32[]{:S(2)}) copy-start(f32[1024,256]{1,0:T(8,128)} %copy-done.7) | copy-start | bytes 3145732

commit v21 on v20

--- a/solution.py
+++ b/solution.py
@@ -283,7 +283,7 @@
 def reduce_scatter_2d(x, axis, first, second, collective_id):
     (n_o, s_o), (n_i, s_i) = first, second
     chunks = next(c for c in (8, 4, 2, 1) if n_i % c == 0)
-    halves = 2 if x.shape[2] % 32 == 0 else 1
+    halves = next(p for p in (3, 2, 1) if x.shape[2] % (16 * p) == 0)
     return pl.pallas_call(
         functools.partial(_reduce_kernel, n_o, s_o, n_i, s_i, chunks, halves, axis),
         out_shape=jax.ShapeDtypeStruct(x.shape[2:], jnp.float32),

time: 160 us -> 160 us (level)
  no operation moved by 1% of the time
where the time goes in v21:
time: 160 us
  Pallas kernels  140 us (88%)
  matrix products  12.5 us (8%)
  local copies, waits for them, and re-layouts  6.05 us (4%)
    pallas_call x2, Pallas kernels, all_gather(): pl.pallas_call(functools.partial(_gather_kernel, outer, inner, parts, axi...  67 us
    pallas_call x2, Pallas kernels, reduce_scatter_2d(): pl.pallas_call(functools.partial(_reduce_kernel, n_o, s_o, n_i, s_i, chun...  56.1 us
    pallas_call x1, Pallas kernels, exchange(): pl.pallas_call(functools.partial(_exchange_kernel, n, stride, axis, gathe...  17 us
    dot_general x1, matrix products, per_device(): lax.dot_general(grad_pre, shard_rows, (((0,), (0,)), ((), ())), preferred...  5.77 us
    unnamed x21, local copies, waits for them, and re-layouts  3.73 us

profile of v21, /device:TPU:1, one launch (start us, length us, event | category | flops | bytes accessed | tf_op | source)
XLA Modules:
  0.0 160.2 jit_solution(441273064176452771)
XLA Ops:
  0.6 0.0 copy-start
  0.6 0.0 copy-start.2
  0.7 1.4 copy-done.2
  2.0 53.5 %shard_map.77 = bf16[2,4,128,4096]{3,2,1,0:T(8,128)(2,1)S(1)} custom-call(bf16[128,4096]{1,0:T(8,128)(2,1)S(1)} %copy-done.2), custom_call_target="tpu_custom_call" | custom-call | tf_op jit(solution)/shard_map/pallas_call | solution.py:169
  55.6 0.0 copy-start.1
  55.6 0.0 copy-done
  55.6 0.0 copy-start.6
  55.6 2.3 %fusion.15 = f32[1024,256]{1,0:T(8,128)S(1)} fusion(bf16[1024,4096]{1,0:T(8,128)(2,1)S(1)} %bitcast.37, bf16[4096,256]{1,0:T(8,128)(2,1)S(1)} %copy-done), kind=kOutput, calls=%fused_computation.33 | convolution fusion | flops 2147483648 | bytes 11534336 | tf_op jit(solution)/shard_map/dot_general | solution.py:328
  57.9 0.8 copy-done.1
  58.8 0.5 fusion.14
  59.2 0.6 copy-done.7
  59.8 16.6 %shard_map.78 = f32[128,512]{1,0:T(8,128)S(1)} custom-call(f32[2,4,128,512]{3,2,1,0:T(8,128)S(1)} %bitcast.39), custom_call_target="tpu_custom_call" | custom-call | tf_op jit(solution)/shard_map/pallas_call | solution.py:287
  76.4 0.1 multiply_reduce_fusion.1
  76.6 0.1 copy.15
  76.6 0.1 eq.15
  76.7 0.3 fusion.3.x_ref
  77.0 17.0 %shard_map.79 = bf16[32,8,512]{2,1,0:T(8,128)(2,1)S(1)} custom-call(bf16[32,8,512]{2,1,0:T(8,128)(2,1)S(1)} %fusion.3.x_ref), custom_call_target="tpu_custom_call" | custom-call | tf_op jit(solution)/shard_map/pallas_call | solution.py:58
  94.1 0.1 fusion.4
  94.2 0.1 copy.16
  94.3 0.1 fusion.13
  94.4 0.5 multiply_reduce_fusion
  94.9 0.1 divide_convert_fusion.x_ref
  95.0 13.5 %shard_map.80 = bf16[2,4,128,512]{3,2,1,0:T(8,128)(2,1)S(1)} custom-call(bf16[128,512]{1,0:T(8,128)(2,1)S(1)} %divide_convert_fusion.x_ref), custom_call_target="tpu_custom_call" | custom-call | tf_op jit(solution)/shard_map/pallas_call | solution.py:169
  108.5 1.3 convolution_convert_fusion.1
  109.8 1.0 concatenate.9
  110.8 1.9 %fusion.2 = bf16[1024,256]{1,0:T(8,128)(2,1)S(1)} fusion(bf16[1024,512]{1,0:T(8,128)(2,1)S(1)} %bitcast.41, bf16[256,512]{1,0:T(8,128)(2,1)} %param.8, f32[1024,256]{1,0:T(8,128)} %copy-done.7), kind=kOutput, calls=%fused_computation.6 | convolution fusion | flops 270794752 | bytes 2883584 | tf_op jit(solution)/shard_map/dot_general | solution.py:364
  112.7 5.8 %fusion = bf16[32,32,8,128]{3,2,1,0:T(8,128)(2,1)S(1)} fusion(bf16[1024,256]{1,0:T(8,128)(2,1)S(1)} %fusion.2, bf16[1024,4096]{1,0:T(8,128)(2,1)} %bitcast.38), kind=kOutput, calls=%fused_computation.3 | convolution fusion | flops 2148532224 | bytes 11010048 | tf_op jit(solution)/shard_map/dot_general | solution.py:374
  118.5 0.6 copy.21
  119.1 0.2 pad_maximum_fusion.p_ref
  119.2 39.5 %shard_map.81 = f32[288,128]{1,0:T(8,128)S(1)} custom-call(bf16[4,8,288,128]{3,2,1,0:T(8,128)(2,1)S(1)} %pad_maximum_fusion.p_ref), custom_call_target="tpu_custom_call" | custom-call | tf_op jit(solution)/shard_map/pallas_call | solution.py:287
  158.8 0.8 copy.18
  159.6 0.6 reshape.80
  (13 shorter events, 0.0 us)
Async XLA Ops:
  0.6 54.9 %copy-start = (bf16[4096,256]{1,0:T(8,128)(2,1)S(1)}, bf16[4096,256]{1,0:T(8,128)(2,1)}, u32[]{:S(2)}) copy-start(bf16[4096,256]{1,0:T(8,128)(2,1)} %param.7) | copy-start | bytes 6291460
  0.6 1.4 copy-start.2
  55.6 3.2 %copy-start.1 = (bf16[2,4,128,4096]{3,2,1,0:T(8,128)(2,1)}, bf16[2,4,128,4096]{3,2,1,0:T(8,128)(2,1)S(1)}, u32[]{:S(2)}) copy-start(bf16[2,4,128,4096]{3,2,1,0:T(8,128)(2,1)S(1)} %shard_map.77) | copy-start | bytes 25165828
  55.6 3.2 %copy-start.6 = (bf16[256,512]{1,0:T(8,128)(2,1)S(1)}, bf16[256,512]{1,0:T(8,128)(2,1)}, u32[]{:S(2)}) copy-start(bf16[256,512]{1,0:T(8,128)(2,1)} %param.8) | copy-start | bytes 786436
  58.8 1.0 copy-start.7
  59.8 16.7 %copy-start.3 = (s32[1,1,32,8]{2,3,1,0:T(8,128)S(1)}, s32[1,1,32,8]{2,3,1,0:T(8,128)}, u32[]{:S(2)}) copy-start(s32[1,1,32,8]{2,3,1,0:T(8,128)} %param.9) | copy-start | bytes 3076
  59.8 34.4 %copy-start.4 = (s32[1,1,32,8]{2,3,1,0:T(8,128)S(1)}, s32[1,1,32,8]{2,3,1,0:T(8,128)}, u32[]{:S(2)}) copy-start(s32[1,1,32,8]{2,3,1,0:T(8,128)} %param.11) | copy-start | bytes 3076
  59.8 34.5 %copy-start.5 = (s32[1,1,32]{2,1,0:T(1,128)S(1)}, s32[1,1,32]{2,1,0:T(1,128)}, u32[]{:S(2)}) copy-start(s32[1,1,32]{2,1,0:T(1,128)} %param.10) | copy-start | bytes 388
  94.3 14.2 %copy-start.8 = (f32[1024,256]{1,0:T(8,128)S(1)}, f32[1024,256]{1,0:T(8,128)}, u32[]{:S(2)}) copy-start(f32[1024,256]{1,0:T(8,128)} %copy-done.7) | copy-start | bytes 3145732

commit v22 on v21

--- a/solution.py
+++ b/solution.py
@@ -283,7 +283,7 @@
 def reduce_scatter_2d(x, axis, first, second, collective_id):
     (n_o, s_o), (n_i, s_i) = first, second
     chunks = next(c for c in (8, 4, 2, 1) if n_i % c == 0)
-    halves = next(p for p in (3, 2, 1) if x.shape[2] % (16 * p) == 0)
+    halves = next(p for p in (4, 2, 1) if x.shape[2] % (16 * p) == 0)
     return pl.pallas_call(
         functools.partial(_reduce_kernel, n_o, s_o, n_i, s_i, chunks, halves, axis),
         out_shape=jax.ShapeDtypeStruct(x.shape[2:], jnp.float32),

time: 160 us -> 161 us (level)
  no operation moved by 1% of the time
where the time goes in v22:
time: 161 us; the launch traced here: 160 us
  Pallas kernels  140 us (87%)
  matrix products  12.5 us (8%)
  local copies, waits for them, and re-layouts  6.05 us (4%)
    pallas_call x2, Pallas kernels, all_gather(): pl.pallas_call(functools.partial(_gather_kernel, outer, inner, parts, axi...  67 us
    pallas_call x2, Pallas kernels, reduce_scatter_2d(): pl.pallas_call(functools.partial(_reduce_kernel, n_o, s_o, n_i, s_i, chun...  56.3 us
    pallas_call x1, Pallas kernels, exchange(): pl.pallas_call(functools.partial(_exchange_kernel, n, stride, axis, gathe...  17 us
    dot_general x1, matrix products, per_device(): lax.dot_general(grad_pre, shard_rows, (((0,), (0,)), ((), ())), preferred...  5.77 us
    unnamed x21, local copies, waits for them, and re-layouts  3.73 us

profile of v22, /device:TPU:1, one launch (start us, length us, event | category | flops | bytes accessed | tf_op | source)
XLA Modules:
  0.0 160.4 jit_solution(12265100477056584542)
XLA Ops:
  0.6 0.0 copy-start
  0.6 0.0 copy-start.2
  0.7 1.4 copy-done.2
  2.0 53.5 %shard_map.77 = bf16[2,4,128,4096]{3,2,1,0:T(8,128)(2,1)S(1)} custom-call(bf16[128,4096]{1,0:T(8,128)(2,1)S(1)} %copy-done.2), custom_call_target="tpu_custom_call" | custom-call | tf_op jit(solution)/shard_map/pallas_call | solution.py:169
  55.6 0.0 copy-start.1
  55.6 0.0 copy-done
  55.6 0.0 copy-start.6
  55.6 2.3 %fusion.15 = f32[1024,256]{1,0:T(8,128)S(1)} fusion(bf16[1024,4096]{1,0:T(8,128)(2,1)S(1)} %bitcast.37, bf16[4096,256]{1,0:T(8,128)(2,1)S(1)} %copy-done), kind=kOutput, calls=%fused_computation.33 | convolution fusion | flops 2147483648 | bytes 11534336 | tf_op jit(solution)/shard_map/dot_general | solution.py:328
  57.9 0.8 copy-done.1
  58.8 0.5 fusion.14
  59.2 0.6 copy-done.7
  59.8 16.9 %shard_map.78 = f32[128,512]{1,0:T(8,128)S(1)} custom-call(f32[2,4,128,512]{3,2,1,0:T(8,128)S(1)} %bitcast.39), custom_call_target="tpu_custom_call" | custom-call | tf_op jit(solution)/shard_map/pallas_call | solution.py:287
  76.8 0.1 multiply_reduce_fusion.1
  76.9 0.1 copy.15
  77.0 0.1 eq.15
  77.1 0.3 fusion.3.x_ref
  77.4 17.0 %shard_map.79 = bf16[32,8,512]{2,1,0:T(8,128)(2,1)S(1)} custom-call(bf16[32,8,512]{2,1,0:T(8,128)(2,1)S(1)} %fusion.3.x_ref), custom_call_target="tpu_custom_call" | custom-call | tf_op jit(solution)/shard_map/pallas_call | solution.py:58
  94.4 0.1 fusion.4
  94.6 0.1 copy.16
  94.6 0.1 fusion.13
  94.7 0.5 multiply_reduce_fusion
  95.2 0.1 divide_convert_fusion.x_ref
  95.4 13.5 %shard_map.80 = bf16[2,4,128,512]{3,2,1,0:T(8,128)(2,1)S(1)} custom-call(bf16[128,512]{1,0:T(8,128)(2,1)S(1)} %divide_convert_fusion.x_ref), custom_call_target="tpu_custom_call" | custom-call | tf_op jit(solution)/shard_map/pallas_call | solution.py:169
  108.9 1.3 convolution_convert_fusion.1
  110.1 1.0 concatenate.9
  111.2 1.9 %fusion.2 = bf16[1024,256]{1,0:T(8,128)(2,1)S(1)} fusion(bf16[1024,512]{1,0:T(8,128)(2,1)S(1)} %bitcast.41, bf16[256,512]{1,0:T(8,128)(2,1)} %param.8, f32[1024,256]{1,0:T(8,128)} %copy-done.7), kind=kOutput, calls=%fused_computation.6 | convolution fusion | flops 270794752 | bytes 2883584 | tf_op jit(solution)/shard_map/dot_general | solution.py:364
  113.1 5.8 %fusion = bf16[32,32,8,128]{3,2,1,0:T(8,128)(2,1)S(1)} fusion(bf16[1024,256]{1,0:T(8,128)(2,1)S(1)} %fusion.2, bf16[1024,4096]{1,0:T(8,128)(2,1)} %bitcast.38), kind=kOutput, calls=%fused_computation.3 | convolution fusion | flops 2148532224 | bytes 11010048 | tf_op jit(solution)/shard_map/dot_general | solution.py:374
  118.8 0.6 copy.21
  119.4 0.2 pad_maximum_fusion.p_ref
  119.6 39.4 %shard_map.81 = f32[288,128]{1,0:T(8,128)S(1)} custom-call(bf16[4,8,288,128]{3,2,1,0:T(8,128)(2,1)S(1)} %pad_maximum_fusion.p_ref), custom_call_target="tpu_custom_call" | custom-call | tf_op jit(solution)/shard_map/pallas_call | solution.py:287
  159.0 0.8 copy.18
  159.8 0.6 reshape.80
  (13 shorter events, 0.0 us)
Async XLA Ops:
  0.6 54.9 %copy-start = (bf16[4096,256]{1,0:T(8,128)(2,1)S(1)}, bf16[4096,256]{1,0:T(8,128)(2,1)}, u32[]{:S(2)}) copy-start(bf16[4096,256]{1,0:T(8,128)(2,1)} %param.7) | copy-start | bytes 6291460
  0.6 1.4 copy-start.2
  55.6 3.2 %copy-start.1 = (bf16[2,4,128,4096]{3,2,1,0:T(8,128)(2,1)}, bf16[2,4,128,4096]{3,2,1,0:T(8,128)(2,1)S(1)}, u32[]{:S(2)}) copy-start(bf16[2,4,128,4096]{3,2,1,0:T(8,128)(2,1)S(1)} %shard_map.77) | copy-start | bytes 25165828
  55.6 3.2 %copy-start.6 = (bf16[256,512]{1,0:T(8,128)(2,1)S(1)}, bf16[256,512]{1,0:T(8,128)(2,1)}, u32[]{:S(2)}) copy-start(bf16[256,512]{1,0:T(8,128)(2,1)} %param.8) | copy-start | bytes 786436
  58.8 1.0 copy-start.7
  59.8 17.1 %copy-start.3 = (s32[1,1,32,8]{2,3,1,0:T(8,128)S(1)}, s32[1,1,32,8]{2,3,1,0:T(8,128)}, u32[]{:S(2)}) copy-start(s32[1,1,32,8]{2,3,1,0:T(8,128)} %param.9) | copy-start | bytes 3076
  59.8 34.7 %copy-start.4 = (s32[1,1,32,8]{2,3,1,0:T(8,128)S(1)}, s32[1,1,32,8]{2,3,1,0:T(8,128)}, u32[]{:S(2)}) copy-start(s32[1,1,32,8]{2,3,1,0:T(8,128)} %param.11) | copy-start | bytes 3076
  59.8 34.8 %copy-start.5 = (s32[1,1,32]{2,1,0:T(1,128)S(1)}, s32[1,1,32]{2,1,0:T(1,128)}, u32[]{:S(2)}) copy-start(s32[1,1,32]{2,1,0:T(1,128)} %param.10) | copy-start | bytes 388
  94.6 14.2 %copy-start.8 = (f32[1024,256]{1,0:T(8,128)S(1)}, f32[1024,256]{1,0:T(8,128)}, u32[]{:S(2)}) copy-start(f32[1024,256]{1,0:T(8,128)} %copy-done.7) | copy-start | bytes 3145732

commit v23 on v22

--- a/solution.py
+++ b/solution.py
@@ -283,7 +283,7 @@
 def reduce_scatter_2d(x, axis, first, second, collective_id):
     (n_o, s_o), (n_i, s_i) = first, second
     chunks = next(c for c in (8, 4, 2, 1) if n_i % c == 0)
-    halves = next(p for p in (4, 2, 1) if x.shape[2] % (16 * p) == 0)
+    halves = 2 if x.shape[2] % 32 == 0 and x.shape[2] >= 256 else 1
     return pl.pallas_call(
         functools.partial(_reduce_kernel, n_o, s_o, n_i, s_i, chunks, halves, axis),
         out_shape=jax.ShapeDtypeStruct(x.shape[2:], jnp.float32),

time: 161 us -> 160 us (level)
  no operation moved by 1% of the time
where the time goes in v23:
time: 160 us
  Pallas kernels  140 us (88%)
  matrix products  12.5 us (8%)
  local copies, waits for them, and re-layouts  6.05 us (4%)
    pallas_call x2, Pallas kernels, all_gather(): pl.pallas_call(functools.partial(_gather_kernel, outer, inner, parts, axi...  67 us
    pallas_call x2, Pallas kernels, reduce_scatter_2d(): pl.pallas_call(functools.partial(_reduce_kernel, n_o, s_o, n_i, s_i, chun...  56 us
    pallas_call x1, Pallas kernels, exchange(): pl.pallas_call(functools.partial(_exchange_kernel, n, stride, axis, gathe...  17 us
    dot_general x1, matrix products, per_device(): lax.dot_general(grad_pre, shard_rows, (((0,), (0,)), ((), ())), preferred...  5.77 us
    unnamed x21, local copies, waits for them, and re-layouts  3.73 us

profile of v23, /device:TPU:1, one launch (start us, length us, event | category | flops | bytes accessed | tf_op | source)
XLA Modules:
  0.0 160.1 jit_solution(5429871160721119571)
XLA Ops:
  0.6 0.0 copy-start
  0.6 0.0 copy-start.2
  0.7 1.4 copy-done.2
  2.0 53.5 %shard_map.77 = bf16[2,4,128,4096]{3,2,1,0:T(8,128)(2,1)S(1)} custom-call(bf16[128,4096]{1,0:T(8,128)(2,1)S(1)} %copy-done.2), custom_call_target="tpu_custom_call" | custom-call | tf_op jit(solution)/shard_map/pallas_call | solution.py:169
  55.6 0.0 copy-start.1
  55.6 0.0 copy-done
  55.6 0.0 copy-start.6
  55.6 2.3 %fusion.15 = f32[1024,256]{1,0:T(8,128)S(1)} fusion(bf16[1024,4096]{1,0:T(8,128)(2,1)S(1)} %bitcast.37, bf16[4096,256]{1,0:T(8,128)(2,1)S(1)} %copy-done), kind=kOutput, calls=%fused_computation.33 | convolution fusion | flops 2147483648 | bytes 11534336 | tf_op jit(solution)/shard_map/dot_general | solution.py:328
  57.9 0.8 copy-done.1
  58.8 0.5 fusion.14
  59.2 0.6 copy-done.7
  59.8 16.6 %shard_map.78 = f32[128,512]{1,0:T(8,128)S(1)} custom-call(f32[2,4,128,512]{3,2,1,0:T(8,128)S(1)} %bitcast.39), custom_call_target="tpu_custom_call" | custom-call | tf_op jit(solution)/shard_map/pallas_call | solution.py:287
  76.4 0.1 multiply_reduce_fusion.1
  76.5 0.1 copy.15
  76.6 0.1 eq.15
  76.7 0.3 fusion.3.x_ref
  77.0 17.0 %shard_map.79 = bf16[32,8,512]{2,1,0:T(8,128)(2,1)S(1)} custom-call(bf16[32,8,512]{2,1,0:T(8,128)(2,1)S(1)} %fusion.3.x_ref), custom_call_target="tpu_custom_call" | custom-call | tf_op jit(solution)/shard_map/pallas_call | solution.py:58
  94.0 0.1 fusion.4
  94.2 0.1 copy.16
  94.3 0.1 fusion.13
  94.3 0.5 multiply_reduce_fusion
  94.9 0.1 divide_convert_fusion.x_ref
  95.0 13.5 %shard_map.80 = bf16[2,4,128,512]{3,2,1,0:T(8,128)(2,1)S(1)} custom-call(bf16[128,512]{1,0:T(8,128)(2,1)S(1)} %divide_convert_fusion.x_ref), custom_call_target="tpu_custom_call" | custom-call | tf_op jit(solution)/shard_map/pallas_call | solution.py:169
  108.5 1.3 convolution_convert_fusion.1
  109.8 1.0 concatenate.9
  110.8 1.9 %fusion.2 = bf16[1024,256]{1,0:T(8,128)(2,1)S(1)} fusion(bf16[1024,512]{1,0:T(8,128)(2,1)S(1)} %bitcast.41, bf16[256,512]{1,0:T(8,128)(2,1)} %param.8, f32[1024,256]{1,0:T(8,128)} %copy-done.7), kind=kOutput, calls=%fused_computation.6 | convolution fusion | flops 270794752 | bytes 2883584 | tf_op jit(solution)/shard_map/dot_general | solution.py:364
  112.7 5.8 %fusion = bf16[32,32,8,128]{3,2,1,0:T(8,128)(2,1)S(1)} fusion(bf16[1024,256]{1,0:T(8,128)(2,1)S(1)} %fusion.2, bf16[1024,4096]{1,0:T(8,128)(2,1)} %bitcast.38), kind=kOutput, calls=%fused_computation.3 | convolution fusion | flops 2148532224 | bytes 11010048 | tf_op jit(solution)/shard_map/dot_general | solution.py:374
  118.5 0.6 copy.21
  119.0 0.2 pad_maximum_fusion.p_ref
  119.2 39.4 %shard_map.81 = f32[288,128]{1,0:T(8,128)S(1)} custom-call(bf16[4,8,288,128]{3,2,1,0:T(8,128)(2,1)S(1)} %pad_maximum_fusion.p_ref), custom_call_target="tpu_custom_call" | custom-call | tf_op jit(solution)/shard_map/pallas_call | solution.py:287
  158.7 0.8 copy.18
  159.5 0.6 reshape.80
  (13 shorter events, 0.0 us)
Async XLA Ops:
  0.6 54.9 %copy-start = (bf16[4096,256]{1,0:T(8,128)(2,1)S(1)}, bf16[4096,256]{1,0:T(8,128)(2,1)}, u32[]{:S(2)}) copy-start(bf16[4096,256]{1,0:T(8,128)(2,1)} %param.7) | copy-start | bytes 6291460
  0.6 1.4 copy-start.2
  55.6 3.2 %copy-start.1 = (bf16[2,4,128,4096]{3,2,1,0:T(8,128)(2,1)}, bf16[2,4,128,4096]{3,2,1,0:T(8,128)(2,1)S(1)}, u32[]{:S(2)}) copy-start(bf16[2,4,128,4096]{3,2,1,0:T(8,128)(2,1)S(1)} %shard_map.77) | copy-start | bytes 25165828
  55.6 3.2 %copy-start.6 = (bf16[256,512]{1,0:T(8,128)(2,1)S(1)}, bf16[256,512]{1,0:T(8,128)(2,1)}, u32[]{:S(2)}) copy-start(bf16[256,512]{1,0:T(8,128)(2,1)} %param.8) | copy-start | bytes 786436
  58.8 1.0 copy-start.7
  59.8 16.7 %copy-start.3 = (s32[1,1,32,8]{2,3,1,0:T(8,128)S(1)}, s32[1,1,32,8]{2,3,1,0:T(8,128)}, u32[]{:S(2)}) copy-start(s32[1,1,32,8]{2,3,1,0:T(8,128)} %param.9) | copy-start | bytes 3076
  59.8 34.4 %copy-start.4 = (s32[1,1,32,8]{2,3,1,0:T(8,128)S(1)}, s32[1,1,32,8]{2,3,1,0:T(8,128)}, u32[]{:S(2)}) copy-start(s32[1,1,32,8]{2,3,1,0:T(8,128)} %param.11) | copy-start | bytes 3076
  59.8 34.5 %copy-start.5 = (s32[1,1,32]{2,1,0:T(1,128)S(1)}, s32[1,1,32]{2,1,0:T(1,128)}, u32[]{:S(2)}) copy-start(s32[1,1,32]{2,1,0:T(1,128)} %param.10) | copy-start | bytes 388
  94.3 14.2 %copy-start.8 = (f32[1024,256]{1,0:T(8,128)S(1)}, f32[1024,256]{1,0:T(8,128)}, u32[]{:S(2)}) copy-start(f32[1024,256]{1,0:T(8,128)} %copy-done.7) | copy-start | bytes 3145732

commit v24 on v20

--- a/solution.py
+++ b/solution.py
@@ -165,7 +165,7 @@
 def all_gather(x, axis, n, inner, collective_id):
     outer = n // inner
     shape = (inner, outer) + x.shape
-    parts = next(p for p in (4, 2, 1) if x.shape[0] % (16 * p) == 0)
+    parts = next(p for p in (2, 1) if x.shape[0] % (16 * p) == 0)
     got = pl.pallas_call(
         functools.partial(_gather_kernel, outer, inner, parts, axis),
         out_shape=jax.ShapeDtypeStruct(shape, x.dtype),

time: 160 us -> 161 us (level)
  no operation moved by 1% of the time
where the time goes in v24:
time: 161 us; the launch traced here: 160 us
  Pallas kernels  140 us (87%)
  matrix products  12.5 us (8%)
  local copies, waits for them, and re-layouts  6.05 us (4%)
    pallas_call x2, Pallas kernels, all_gather(): pl.pallas_call(functools.partial(_gather_kernel, outer, inner, parts, axi...  67.3 us
    pallas_call x2, Pallas kernels, reduce_scatter_2d(): pl.pallas_call(functools.partial(_reduce_kernel, n_o, s_o, n_i, s_i, chun...  56 us
    pallas_call x1, Pallas kernels, exchange(): pl.pallas_call(functools.partial(_exchange_kernel, n, stride, axis, gathe...  17 us
    dot_general x1, matrix products, per_device(): lax.dot_general(grad_pre, shard_rows, (((0,), (0,)), ((), ())), preferred...  5.77 us
    unnamed x21, local copies, waits for them, and re-layouts  3.73 us

profile of v24, /device:TPU:1, one launch (start us, length us, event | category | flops | bytes accessed | tf_op | source)
XLA Modules:
  0.0 160.3 jit_solution(15847990650752741685)
XLA Ops:
  0.6 0.0 copy-start
  0.7 1.4 copy-done.2
  2.0 53.9 %shard_map.77 = bf16[2,4,128,4096]{3,2,1,0:T(8,128)(2,1)S(1)} custom-call(bf16[128,4096]{1,0:T(8,128)(2,1)S(1)} %copy-done.2), custom_call_target="tpu_custom_call" | custom-call | tf_op jit(solution)/shard_map/pallas_call | solution.py:169
  56.0 0.0 copy-start.6
  56.0 2.3 %fusion.15 = f32[1024,256]{1,0:T(8,128)S(1)} fusion(bf16[1024,4096]{1,0:T(8,128)(2,1)S(1)} %bitcast.37, bf16[4096,256]{1,0:T(8,128)(2,1)S(1)} %copy-done), kind=kOutput, calls=%fused_computation.33 | convolution fusion | flops 2147483648 | bytes 11534336 | tf_op jit(solution)/shard_map/dot_general | solution.py:328
  58.3 0.8 copy-done.1
  59.2 0.5 fusion.14
  59.6 0.6 copy-done.7
  60.2 16.5 %shard_map.78 = f32[128,512]{1,0:T(8,128)S(1)} custom-call(f32[2,4,128,512]{3,2,1,0:T(8,128)S(1)} %bitcast.39), custom_call_target="tpu_custom_call" | custom-call | tf_op jit(solution)/shard_map/pallas_call | solution.py:287
  76.8 0.1 multiply_reduce_fusion.1
  76.9 0.0 copy-done.3
  76.9 0.1 copy.15
  77.0 0.1 eq.15
  77.1 0.3 fusion.3.x_ref
  77.4 17.0 %shard_map.79 = bf16[32,8,512]{2,1,0:T(8,128)(2,1)S(1)} custom-call(bf16[32,8,512]{2,1,0:T(8,128)(2,1)S(1)} %fusion.3.x_ref), custom_call_target="tpu_custom_call" | custom-call | tf_op jit(solution)/shard_map/pallas_call | solution.py:58
  94.4 0.1 fusion.4
  94.5 0.0 copy-done.4
  94.6 0.1 copy.16
  94.6 0.0 copy-done.5
  94.6 0.1 fusion.13
  94.7 0.5 multiply_reduce_fusion
  95.2 0.1 divide_convert_fusion.x_ref
  95.4 13.4 %shard_map.80 = bf16[2,4,128,512]{3,2,1,0:T(8,128)(2,1)S(1)} custom-call(bf16[128,512]{1,0:T(8,128)(2,1)S(1)} %divide_convert_fusion.x_ref), custom_call_target="tpu_custom_call" | custom-call | tf_op jit(solution)/shard_map/pallas_call | solution.py:169
  108.8 1.3 convolution_convert_fusion.1
  110.0 1.0 concatenate.9
  111.1 1.9 %fusion.2 = bf16[1024,256]{1,0:T(8,128)(2,1)S(1)} fusion(bf16[1024,512]{1,0:T(8,128)(2,1)S(1)} %bitcast.41, bf16[256,512]{1,0:T(8,128)(2,1)} %param.8, f32[1024,256]{1,0:T(8,128)} %copy-done.7), kind=kOutput, calls=%fused_computation.6 | convolution fusion | flops 270794752 | bytes 2883584 | tf_op jit(solution)/shard_map/dot_general | solution.py:364
  113.0 5.8 %fusion = bf16[32,32,8,128]{3,2,1,0:T(8,128)(2,1)S(1)} fusion(bf16[1024,256]{1,0:T(8,128)(2,1)S(1)} %fusion.2, bf16[1024,4096]{1,0:T(8,128)(2,1)} %bitcast.38), kind=kOutput, calls=%fused_computation.3 | convolution fusion | flops 2148532224 | bytes 11010048 | tf_op jit(solution)/shard_map/dot_general | solution.py:374
  118.7 0.6 copy.21
  119.3 0.2 pad_maximum_fusion.p_ref
  119.5 39.5 %shard_map.81 = f32[288,128]{1,0:T(8,128)S(1)} custom-call(bf16[4,8,288,128]{3,2,1,0:T(8,128)(2,1)S(1)} %pad_maximum_fusion.p_ref), custom_call_target="tpu_custom_call" | custom-call | tf_op jit(solution)/shard_map/pallas_call | solution.py:287
  159.0 0.8 copy.18
  159.7 0.6 reshape.80
  (13 shorter events, 0.0 us)
Async XLA Ops:
  0.6 55.3 %copy-start = (bf16[4096,256]{1,0:T(8,128)(2,1)S(1)}, bf16[4096,256]{1,0:T(8,128)(2,1)}, u32[]{:S(2)}) copy-start(bf16[4096,256]{1,0:T(8,128)(2,1)} %param.7) | copy-start | bytes 6291460
  0.6 1.4 copy-start.2
  56.0 3.2 %copy-start.1 = (bf16[2,4,128,4096]{3,2,1,0:T(8,128)(2,1)}, bf16[2,4,128,4096]{3,2,1,0:T(8,128)(2,1)S(1)}, u32[]{:S(2)}) copy-start(bf16[2,4,128,4096]{3,2,1,0:T(8,128)(2,1)S(1)} %shard_map.77) | copy-start | bytes 25165828
  56.0 3.2 %copy-start.6 = (bf16[256,512]{1,0:T(8,128)(2,1)S(1)}, bf16[256,512]{1,0:T(8,128)(2,1)}, u32[]{:S(2)}) copy-start(bf16[256,512]{1,0:T(8,128)(2,1)} %param.8) | copy-start | bytes 786436
  59.2 1.0 copy-start.7
  60.2 16.7 %copy-start.3 = (s32[1,1,32,8]{2,3,1,0:T(8,128)S(1)}, s32[1,1,32,8]{2,3,1,0:T(8,128)}, u32[]{:S(2)}) copy-start(s32[1,1,32,8]{2,3,1,0:T(8,128)} %param.9) | copy-start | bytes 3076
  60.2 34.3 %copy-start.4 = (s32[1,1,32,8]{2,3,1,0:T(8,128)S(1)}, s32[1,1,32,8]{2,3,1,0:T(8,128)}, u32[]{:S(2)}) copy-start(s32[1,1,32,8]{2,3,1,0:T(8,128)} %param.11) | copy-start | bytes 3076
  60.2 34.4 %copy-start.5 = (s32[1,1,32]{2,1,0:T(1,128)S(1)}, s32[1,1,32]{2,1,0:T(1,128)}, u32[]{:S(2)}) copy-start(s32[1,1,32]{2,1,0:T(1,128)} %param.10) | copy-start | bytes 388
  94.6 14.1 %copy-start.8 = (f32[1024,256]{1,0:T(8,128)S(1)}, f32[1024,256]{1,0:T(8,128)}, u32[]{:S(2)}) copy-start(f32[1024,256]{1,0:T(8,128)} %copy-done.7) | copy-start | bytes 3145732
